TPU v7x, 256 devices: a whole 4x4x8 slice. The times are simulated.
256 devices in a mesh: tile: 16 (over z_hi, y), group: 16 (over x, z_lo, core).
Axes of the slice: x: 4, y: 4, z: 8 (z_hi: 4, z_lo: 2; z = z_hi * 2 + z_lo), core: 2. Of those that a mesh axis runs over, the one named last changes fastest.
Arguments:
- tracers: float32 [128, 16, 128, 256], P('group', None, 'tile'), may hold values from -6 to 6
- emissions: float32 [128, 128, 256], P('group', 'tile'), may hold values from -6 to 6
- winds: float32 [16, 2, 16, 128, 256], P('group', None, None, 'tile'), may hold values from -1.44 to 1.44, as said below
- diffusivity: float32 [16, 15, 128, 256], P('group', None, 'tile'), may hold values from 0.05 to 2
- substeps: int32 [16], replicated, may hold values from 1 to 6, as said below
- loader: int32 [16], replicated, may hold values from 0 to 15
Outputs:
- mixed: float32 [128, 16, 128, 256], P('group', None, 'tile')
Inputs may be any that keep to these rules, and one draw needn't show every extreme that they name: The first and the last tile take 6 substeps. `winds`: divided by the substep count of the tile that holds the face (for a meridional value on a tile's first row, by the smaller count of that tile and the tile south of it), every entry lies within -0.24 to 0.24.
All inputs are finite; a program needn't handle non-finite values.
Results may differ from a plain program's by a relative error of at most 0.00002.
Values sent between devices are 32-bit elements; how exact they have to be, the bound alone decides.
A program may use at most 64 MiB of HBM per device.

v0:
```python
import jax
import jax.numpy as jnp
from jax import lax
from jax.sharding import PartitionSpec as P

ROUNDS = 6


def spread(value, axis, root):
    mine = lax.axis_index(axis) == root
    return lax.psum(jnp.where(mine, value, jnp.zeros_like(value)), axis)


def from_behind(value, axis, by):
    count = lax.axis_size(axis)
    pairs = [(i, i + by) for i in range(count) if 0 <= i + by < count]
    return lax.ppermute(value, axis, pairs)


def thomas_solve(mixing, coefficient):
    levels = mixing.shape[1]
    zero_plane = jnp.zeros_like(coefficient[0])
    previous_ratio = zero_plane
    previous_value = jnp.zeros_like(mixing[:, 0])
    ratios = []
    values = []
    for level in range(levels):
        lower_coef = coefficient[level - 1] if level > 0 else zero_plane
        upper_coef = coefficient[level] if level < levels - 1 else zero_plane
        pivot = 1.0 / (1.0 + lower_coef + upper_coef - lower_coef * previous_ratio)
        previous_ratio = upper_coef * pivot
        previous_value = (mixing[:, level] + lower_coef * previous_value) * pivot
        ratios.append(previous_ratio)
        values.append(previous_value)
    solved = [None] * levels
    current = values[levels - 1]
    solved[levels - 1] = current
    for level in range(levels - 2, -1, -1):
        current = values[level] + ratios[level] * current
        solved[level] = current
    return jnp.stack(solved, axis=1)


def zonal_tendency(mixing, zonal):
    from_west = jnp.roll(mixing, 1, axis=3)
    west_flux = jnp.maximum(zonal, 0.0) * from_west + jnp.minimum(zonal, 0.0) * mixing
    east_flux = jnp.roll(west_flux, -1, axis=3)
    return east_flux - west_flux


def shards(tracers, emissions, winds, diffusivity, substeps, loader):
    tile_position = lax.axis_index("tile")
    tile_numbers = jnp.arange(substeps.shape[0])
    loader_slot = jnp.sum(jnp.where(tile_numbers == tile_position, loader, 0))
    local_winds, coefficient = (
        spread(winds[0], "group", loader_slot),
        spread(diffusivity[0], "group", loader_slot),
    )
    height = tracers.shape[2]
    row_global = tile_position * height + jnp.arange(height)
    zonal = local_winds[0]
    meridional = local_winds[1] * (row_global > 0).astype(jnp.float32)[:, None]
    count = jnp.sum(jnp.where(tile_numbers == tile_position, substeps, 0))
    count_float = count.astype(jnp.float32)
    mixing = tracers
    for substep in range(ROUNDS):
        fraction = jnp.where(substep < count, 1.0 / count_float, jnp.float32(0.0))
        below_row = from_behind(mixing[:, :, -1:], "tile", 1)
        from_south = jnp.concatenate([below_row, mixing[:, :, :-1]], axis=2)
        south_flux = (
            jnp.maximum(meridional, 0.0) * from_south + jnp.minimum(meridional, 0.0) * mixing
        )
        above_flux = from_behind(south_flux[:, :, :1], "tile", -1)
        north_flux = jnp.concatenate([south_flux[:, :, 1:], above_flux], axis=2)
        mixing = mixing - fraction * (zonal_tendency(mixing, zonal) + (north_flux - south_flux))
    mixing = mixing.at[:, 0].add(emissions)
    return thomas_solve(mixing, coefficient)


def solution(mesh):
    return jax.shard_map(
        shards,
        mesh=mesh,
        in_specs=(
            P("group", None, "tile", None),
            P("group", "tile", None),
            P("group", None, None, "tile", None),
            P("group", None, "tile", None),
            P(),
            P(),
        ),
        out_specs=P("group", None, "tile", None),
        check_vma=False,
    )
```

profile of v0, /device:TPU:88, one launch (start us, length us, event | category | flops | bytes accessed | tf_op | source)
XLA Modules:
  0.0 260.8 jit_solution(10605741622031917092)
XLA Ops:
  12.0 4.2 %collective-permute-start = (f32[8,16,1,256]{3,1,2,0:T(8,128)S(1)}, f32[8,16,1,256]{3,1,2,0:T(8,128)S(1)}, u32[]{:S(2)}, u32[]{:S(2)}) collective-permute-start(f32[8,16,1,256]{3,1,2,0:T(8,128)S(1)} %copy.50), channel_id=1, source_target_pairs={{0,16},{16,32},{32,48},{48,64},{64,80},{80,96},{96,112},{112,128},... | collective-permute-start | bytes 393224 | tf_op jit(solution)/shard_map/ppermute | solution.py:17
  16.3 5.4 %collective-permute-done = f32[8,16,1,256]{3,1,2,0:T(8,128)S(1)} collective-permute-done((f32[8,16,1,256]{3,1,2,0:T(8,128)S(1)}, f32[8,16,1,256]{3,1,2,0:T(8,128)S(1)}, u32[]{:S(2)}, u32[]{:S(2)}) %collective-permute-start) | collective-permute-done | bytes 131104 | tf_op jit(solution)/shard_map/ppermute | solution.py:17
  22.5 111.5 %all-reduce.3.cloned.1.call-done = (f32[15,8,256]{2,1,0:T(8,128)}, f32[2,16,8,256]{3,2,1,0:T(8,128)}) async-done(((f32[15,8,256]{2,1,0:T(8,128)}, f32[2,16,8,256]{3,2,1,0:T(8,128)}), (f32[15,8,256]{2,1,0:T(8,128)}, f32[2,16,8,256]{3,2,1,0:T(8,128)})) %all-reduce.3.cloned.1.call-update) | async-done | bytes 385040 | tf_op jit(solution)/shard_map/psum | solution.py:11
  136.6 2.7 %collective-permute-start.1 = (f32[8,16,1,256]{3,1,2,0:T(8,128)}, f32[8,16,1,256]{3,1,2,0:T(8,128)}, u32[]{:S(2)}, u32[]{:S(2)}) collective-permute-start(f32[8,16,1,256]{3,1,2,0:T(8,128)} %copy.26), channel_id=1, source_target_pairs={{16,0},{32,16},{48,32},{64,48},{80,64},{96,80},{112,96},{128,112},... | collective-permute-start | bytes 393224 | tf_op jit(solution)/shard_map/ppermute | solution.py:17
  141.2 8.0 %collective-permute-done.1 = f32[8,16,1,256]{3,1,2,0:T(8,128)} collective-permute-done((f32[8,16,1,256]{3,1,2,0:T(8,128)}, f32[8,16,1,256]{3,1,2,0:T(8,128)}, u32[]{:S(2)}, u32[]{:S(2)}) %collective-permute-start.1) | collective-permute-done | bytes 131104 | tf_op jit(solution)/shard_map/ppermute | solution.py:17
  151.0 1.9 collective-permute-start.2
  159.2 2.8 %collective-permute-start.3 = (f32[8,16,1,256]{3,1,2,0:T(8,128)S(1)}, f32[8,16,1,256]{3,1,2,0:T(8,128)S(1)}, u32[]{:S(2)}, u32[]{:S(2)}) collective-permute-start(f32[8,16,1,256]{3,1,2,0:T(8,128)S(1)} %copy.31), channel_id=1, source_target_pairs={{16,0},{32,16},{48,32},{64,48},{80,64},{96,80},{112,96},{128,112},... | collective-permute-start | bytes 393224 | tf_op jit(solution)/shard_map/ppermute | solution.py:17
  162.5 7.7 %collective-permute-done.3 = f32[8,16,1,256]{3,1,2,0:T(8,128)S(1)} collective-permute-done((f32[8,16,1,256]{3,1,2,0:T(8,128)S(1)}, f32[8,16,1,256]{3,1,2,0:T(8,128)S(1)}, u32[]{:S(2)}, u32[]{:S(2)}) %collective-permute-start.3) | collective-permute-done | bytes 131104 | tf_op jit(solution)/shard_map/ppermute | solution.py:17
  171.2 2.2 collective-permute-start.4
  173.7 4.4 %collective-permute-done.4 = f32[8,16,1,256]{3,1,2,0:T(8,128)S(1)} collective-permute-done((f32[8,16,1,256]{3,1,2,0:T(8,128)S(1)}, f32[8,16,1,256]{3,1,2,0:T(8,128)S(1)}, u32[]{:S(2)}, u32[]{:S(2)}) %collective-permute-start.4) | collective-permute-done | bytes 131104 | tf_op jit(solution)/shard_map/ppermute | solution.py:17
  179.1 1.9 collective-permute-start.5
  181.5 9.3 %collective-permute-done.5 = f32[8,16,1,256]{3,1,2,0:T(8,128)S(1)} collective-permute-done((f32[8,16,1,256]{3,1,2,0:T(8,128)S(1)}, f32[8,16,1,256]{3,1,2,0:T(8,128)S(1)}, u32[]{:S(2)}, u32[]{:S(2)}) %collective-permute-start.5) | collective-permute-done | bytes 131104 | tf_op jit(solution)/shard_map/ppermute | solution.py:17
  191.8 1.9 collective-permute-start.6
  194.0 4.7 %collective-permute-done.6 = f32[8,16,1,256]{3,1,2,0:T(8,128)S(1)} collective-permute-done((f32[8,16,1,256]{3,1,2,0:T(8,128)S(1)}, f32[8,16,1,256]{3,1,2,0:T(8,128)S(1)}, u32[]{:S(2)}, u32[]{:S(2)}) %collective-permute-start.6) | collective-permute-done | bytes 131104 | tf_op jit(solution)/shard_map/ppermute | solution.py:17
  199.7 1.9 collective-permute-start.7
  202.1 8.9 %collective-permute-done.7 = f32[8,16,1,256]{3,1,2,0:T(8,128)S(1)} collective-permute-done((f32[8,16,1,256]{3,1,2,0:T(8,128)S(1)}, f32[8,16,1,256]{3,1,2,0:T(8,128)S(1)}, u32[]{:S(2)}, u32[]{:S(2)}) %collective-permute-start.7) | collective-permute-done | bytes 131104 | tf_op jit(solution)/shard_map/ppermute | solution.py:17
  212.0 2.1 collective-permute-start.8
  214.4 4.5 %collective-permute-done.8 = f32[8,16,1,256]{3,1,2,0:T(8,128)S(1)} collective-permute-done((f32[8,16,1,256]{3,1,2,0:T(8,128)S(1)}, f32[8,16,1,256]{3,1,2,0:T(8,128)S(1)}, u32[]{:S(2)}, u32[]{:S(2)}) %collective-permute-start.8) | collective-permute-done | bytes 131104 | tf_op jit(solution)/shard_map/ppermute | solution.py:17
  219.9 1.9 collective-permute-start.9
  222.3 8.6 %collective-permute-done.9 = f32[8,16,1,256]{3,1,2,0:T(8,128)S(1)} collective-permute-done((f32[8,16,1,256]{3,1,2,0:T(8,128)S(1)}, f32[8,16,1,256]{3,1,2,0:T(8,128)S(1)}, u32[]{:S(2)}, u32[]{:S(2)}) %collective-permute-start.9) | collective-permute-done | bytes 131104 | tf_op jit(solution)/shard_map/ppermute | solution.py:17
  231.9 2.0 collective-permute-start.10
  234.1 4.6 %collective-permute-done.10 = f32[8,16,1,256]{3,1,2,0:T(8,128)S(1)} collective-permute-done((f32[8,16,1,256]{3,1,2,0:T(8,128)S(1)}, f32[8,16,1,256]{3,1,2,0:T(8,128)S(1)}, u32[]{:S(2)}, u32[]{:S(2)}) %collective-permute-start.10) | collective-permute-done | bytes 131104 | tf_op jit(solution)/shard_map/ppermute | solution.py:17
  239.8 1.9 collective-permute-start.11
  242.2 8.6 %collective-permute-done.11 = f32[8,16,1,256]{3,1,2,0:T(8,128)S(1)} collective-permute-done((f32[8,16,1,256]{3,1,2,0:T(8,128)S(1)}, f32[8,16,1,256]{3,1,2,0:T(8,128)S(1)}, u32[]{:S(2)}, u32[]{:S(2)}) %collective-permute-start.11) | collective-permute-done | bytes 131104 | tf_op jit(solution)/shard_map/ppermute | solution.py:17
  (121 shorter events, 27.5 us)
Async XLA Ops:
  6.5 5.3 %copy-start = (f32[8,16,8,256]{3,2,1,0:T(8,128)S(1)}, f32[8,16,8,256]{3,2,1,0:T(8,128)}, u32[]{:S(2)}) copy-start(f32[8,16,8,256]{3,2,1,0:T(8,128)} %param.8) | copy-start | bytes 3145732
  6.5 127.4 %all-reduce.3.cloned.1.call-start = ((), (), s32[]{:S(2)}) async-start(), calls=%async_computation | async-start | bytes 770048 | tf_op jit(solution)/shard_map/psum | solution.py:11
  12.0 9.7 %collective-permute-start = (f32[8,16,1,256]{3,1,2,0:T(8,128)S(1)}, f32[8,16,1,256]{3,1,2,0:T(8,128)S(1)}, u32[]{:S(2)}, u32[]{:S(2)}) collective-permute-start(f32[8,16,1,256]{3,1,2,0:T(8,128)S(1)} %copy.50), channel_id=1, source_target_pairs={{0,16},{16,32},{32,48},{48,64},{64,80},{80,96},{96,112},{112,128},... | collective-permute-start | bytes 393224 | tf_op jit(solution)/shard_map/ppermute | solution.py:17
  134.0 1.1 copy-start.6
  135.1 0.7 copy-start.3
  135.7 5.1 %copy-start.1 = (f32[8,16,8,256]{3,2,0,1:T(8,128)}, f32[8,16,8,256]{3,2,0,1:T(8,128)S(1)}, u32[]{:S(2)}) copy-start(f32[8,16,8,256]{3,2,0,1:T(8,128)S(1)} %get-tuple-element.66) | copy-start | bytes 3145732
  136.6 12.6 %collective-permute-start.1 = (f32[8,16,1,256]{3,1,2,0:T(8,128)}, f32[8,16,1,256]{3,1,2,0:T(8,128)}, u32[]{:S(2)}, u32[]{:S(2)}) collective-permute-start(f32[8,16,1,256]{3,1,2,0:T(8,128)} %copy.26), channel_id=1, source_target_pairs={{16,0},{32,16},{48,32},{64,48},{80,64},{96,80},{112,96},{128,112},... | collective-permute-start | bytes 393224 | tf_op jit(solution)/shard_map/ppermute | solution.py:17
  141.1 9.1 %copy-start.2 = (f32[8,16,8,256]{3,2,0,1:T(8,128)S(1)}, f32[8,16,8,256]{3,2,0,1:T(8,128)}, u32[]{:S(2)}) copy-start(f32[8,16,8,256]{3,2,0,1:T(8,128)} %copy-done.1) | copy-start | bytes 3145732
  151.0 7.2 %collective-permute-start.2 = (f32[8,16,1,256]{3,1,2,0:T(8,128)S(1)}, f32[8,16,1,256]{3,1,2,0:T(8,128)S(1)}, u32[]{:S(2)}, u32[]{:S(2)}) collective-permute-start(f32[8,16,1,256]{3,1,2,0:T(8,128)S(1)} %copy.29), channel_id=1, source_target_pairs={{0,16},{16,32},{32,48},{48,64},{64,80},{80,96},{96,112},{112,128},... | collective-permute-start | bytes 393224 | tf_op jit(solution)/shard_map/ppermute | solution.py:17
  156.3 2.0 copy-start.4
  159.1 2.9 %copy-start.5 = (f32[15,8,256]{2,1,0:T(8,128)S(1)}, f32[15,8,256]{2,1,0:T(8,128)}, u32[]{:S(2)}) copy-start(f32[15,8,256]{2,1,0:T(8,128)} %get-tuple-element.17) | copy-start | bytes 368644
  159.2 11.1 %collective-permute-start.3 = (f32[8,16,1,256]{3,1,2,0:T(8,128)S(1)}, f32[8,16,1,256]{3,1,2,0:T(8,128)S(1)}, u32[]{:S(2)}, u32[]{:S(2)}) collective-permute-start(f32[8,16,1,256]{3,1,2,0:T(8,128)S(1)} %copy.31), channel_id=1, source_target_pairs={{16,0},{32,16},{48,32},{64,48},{80,64},{96,80},{112,96},{128,112},... | collective-permute-start | bytes 393224 | tf_op jit(solution)/shard_map/ppermute | solution.py:17
  171.2 6.9 %collective-permute-start.4 = (f32[8,16,1,256]{3,1,2,0:T(8,128)S(1)}, f32[8,16,1,256]{3,1,2,0:T(8,128)S(1)}, u32[]{:S(2)}, u32[]{:S(2)}) collective-permute-start(f32[8,16,1,256]{3,1,2,0:T(8,128)S(1)} %copy.33), channel_id=1, source_target_pairs={{0,16},{16,32},{32,48},{48,64},{64,80},{80,96},{96,112},{112,128},... | collective-permute-start | bytes 393224 | tf_op jit(solution)/shard_map/ppermute | solution.py:17
  179.1 11.8 %collective-permute-start.5 = (f32[8,16,1,256]{3,1,2,0:T(8,128)S(1)}, f32[8,16,1,256]{3,1,2,0:T(8,128)S(1)}, u32[]{:S(2)}, u32[]{:S(2)}) collective-permute-start(f32[8,16,1,256]{3,1,2,0:T(8,128)S(1)} %copy.35), channel_id=1, source_target_pairs={{16,0},{32,16},{48,32},{64,48},{80,64},{96,80},{112,96},{128,112},... | collective-permute-start | bytes 393224 | tf_op jit(solution)/shard_map/ppermute | solution.py:17
  191.8 6.9 %collective-permute-start.6 = (f32[8,16,1,256]{3,1,2,0:T(8,128)S(1)}, f32[8,16,1,256]{3,1,2,0:T(8,128)S(1)}, u32[]{:S(2)}, u32[]{:S(2)}) collective-permute-start(f32[8,16,1,256]{3,1,2,0:T(8,128)S(1)} %copy.37), channel_id=1, source_target_pairs={{0,16},{16,32},{32,48},{48,64},{64,80},{80,96},{96,112},{112,128},... | collective-permute-start | bytes 393224 | tf_op jit(solution)/shard_map/ppermute | solution.py:17
  199.7 11.4 %collective-permute-start.7 = (f32[8,16,1,256]{3,1,2,0:T(8,128)S(1)}, f32[8,16,1,256]{3,1,2,0:T(8,128)S(1)}, u32[]{:S(2)}, u32[]{:S(2)}) collective-permute-start(f32[8,16,1,256]{3,1,2,0:T(8,128)S(1)} %copy.39), channel_id=1, source_target_pairs={{16,0},{32,16},{48,32},{64,48},{80,64},{96,80},{112,96},{128,112},... | collective-permute-start | bytes 393224 | tf_op jit(solution)/shard_map/ppermute | solution.py:17
  212.0 6.9 %collective-permute-start.8 = (f32[8,16,1,256]{3,1,2,0:T(8,128)S(1)}, f32[8,16,1,256]{3,1,2,0:T(8,128)S(1)}, u32[]{:S(2)}, u32[]{:S(2)}) collective-permute-start(f32[8,16,1,256]{3,1,2,0:T(8,128)S(1)} %copy.41), channel_id=1, source_target_pairs={{0,16},{16,32},{32,48},{48,64},{64,80},{80,96},{96,112},{112,128},... | collective-permute-start | bytes 393224 | tf_op jit(solution)/shard_map/ppermute | solution.py:17
  219.9 11.1 %collective-permute-start.9 = (f32[8,16,1,256]{3,1,2,0:T(8,128)S(1)}, f32[8,16,1,256]{3,1,2,0:T(8,128)S(1)}, u32[]{:S(2)}, u32[]{:S(2)}) collective-permute-start(f32[8,16,1,256]{3,1,2,0:T(8,128)S(1)} %copy.43), channel_id=1, source_target_pairs={{16,0},{32,16},{48,32},{64,48},{80,64},{96,80},{112,96},{128,112},... | collective-permute-start | bytes 393224 | tf_op jit(solution)/shard_map/ppermute | solution.py:17
  231.9 6.9 %collective-permute-start.10 = (f32[8,16,1,256]{3,1,2,0:T(8,128)S(1)}, f32[8,16,1,256]{3,1,2,0:T(8,128)S(1)}, u32[]{:S(2)}, u32[]{:S(2)}) collective-permute-start(f32[8,16,1,256]{3,1,2,0:T(8,128)S(1)} %copy.45), channel_id=1, source_target_pairs={{0,16},{16,32},{32,48},{48,64},{64,80},{80,96},{96,112},{112,128},... | collective-permute-start | bytes 393224 | tf_op jit(solution)/shard_map/ppermute | solution.py:17
  239.8 11.1 %collective-permute-start.11 = (f32[8,16,1,256]{3,1,2,0:T(8,128)S(1)}, f32[8,16,1,256]{3,1,2,0:T(8,128)S(1)}, u32[]{:S(2)}, u32[]{:S(2)}) collective-permute-start(f32[8,16,1,256]{3,1,2,0:T(8,128)S(1)} %copy.47), channel_id=1, source_target_pairs={{16,0},{32,16},{48,32},{64,48},{80,64},{96,80},{112,96},{128,112},... | collective-permute-start | bytes 393224 | tf_op jit(solution)/shard_map/ppermute | solution.py:17
  251.6 0.8 copy-start.7
Sparse Core Ops, SparseCore 0:
  12.0 121.9 all-reduce.2
where the time goes:
time: 261 us
  waiting for transfers between devices  188 us (72%)
  starting transfers between devices  27.6 us (11%)
  between operations  19.3 us (7%)
  other arithmetic  14.1 us (5%)
  local copies, waits for them, and re-layouts  11.5 us (4%)
    psum x1, waiting for transfers between devices, spread(): return lax.psum(jnp.where(mine, value, jnp.zeros_like(value)), axis)  111 us
    ppermute x12, waiting for transfers between devices, from_behind(): return lax.ppermute(value, axis, pairs)  76.8 us
    ppermute x12, starting transfers between devices, from_behind(): return lax.ppermute(value, axis, pairs)  27.6 us
  transfers between devices with their start and end apart: 13, of which 13 were waited for; matrix products, arithmetic and copies ran while one was open for 2% of the time, Pallas kernels for 0%

commit v1 on v0

v1 whole, which is shorter than its diff:
```python
import jax
import jax.numpy as jnp
from jax import lax
from jax.sharding import PartitionSpec as P

ROUNDS = 6


def from_behind(value, axis, by):
    count = lax.axis_size(axis)
    pairs = [(i, i + by) for i in range(count) if 0 <= i + by < count]
    return lax.ppermute(value, axis, pairs)


def broadcast_from(value, axis, root):
    count = lax.axis_size(axis)
    assert count & (count - 1) == 0
    distance = lax.axis_index(axis) ^ root
    current = value
    bit = 0
    while (1 << bit) < count:
        pairs = [(i, i ^ (1 << bit)) for i in range(count)]
        received = lax.ppermute(current, axis, pairs)
        current = jnp.where((distance >> bit) == 1, received, current)
        bit += 1
    return current


def thomas_solve(mixing, coefficient):
    levels = mixing.shape[1]
    zero_plane = jnp.zeros_like(coefficient[0])
    previous_ratio = zero_plane
    previous_value = jnp.zeros_like(mixing[:, 0])
    ratios = []
    values = []
    for level in range(levels):
        lower_coef = coefficient[level - 1] if level > 0 else zero_plane
        upper_coef = coefficient[level] if level < levels - 1 else zero_plane
        pivot = 1.0 / (1.0 + lower_coef + upper_coef - lower_coef * previous_ratio)
        previous_ratio = upper_coef * pivot
        previous_value = (mixing[:, level] + lower_coef * previous_value) * pivot
        ratios.append(previous_ratio)
        values.append(previous_value)
    solved = [None] * levels
    current = values[levels - 1]
    solved[levels - 1] = current
    for level in range(levels - 2, -1, -1):
        current = values[level] + ratios[level] * current
        solved[level] = current
    return jnp.stack(solved, axis=1)


def advance(mixing, zonal, meridional, fraction):
    from_west = jnp.roll(mixing, 1, axis=3)
    west_flux = jnp.maximum(zonal, 0.0) * from_west + jnp.minimum(zonal, 0.0) * mixing
    east_flux = jnp.roll(west_flux, -1, axis=3)
    zeros_row = jnp.zeros_like(mixing[:, :, :1])
    from_south = jnp.concatenate([zeros_row, mixing[:, :, :-1]], axis=2)
    south_flux = jnp.maximum(meridional, 0.0) * from_south + jnp.minimum(meridional, 0.0) * mixing
    north_flux = jnp.concatenate([south_flux[:, :, 1:], zeros_row], axis=2)
    return mixing - fraction * ((east_flux - west_flux) + (north_flux - south_flux))


def shards(tracers, emissions, winds, diffusivity, substeps, loader):
    tiles = lax.axis_size("tile")
    tile_position = lax.axis_index("tile")
    tile_numbers = jnp.arange(substeps.shape[0])
    loader_slot = jnp.sum(jnp.where(tile_numbers == tile_position, loader, 0))
    levels = tracers.shape[1]
    height = tracers.shape[2]
    width = tracers.shape[3]
    halo = ROUNDS

    local = jnp.concatenate(
        [winds[0].reshape(2 * levels, height, width), diffusivity[0]], axis=0
    )
    chosen = broadcast_from(local, "group", loader_slot)
    courant = chosen[: 2 * levels]
    coefficient = chosen[2 * levels :]

    south_tracers = from_behind(tracers[:, :, height - halo :], "tile", 1)
    north_tracers = from_behind(tracers[:, :, :halo], "tile", -1)
    south_courant = from_behind(courant[:, height - halo :], "tile", 1)
    north_courant = from_behind(courant[:, :halo], "tile", -1)

    row_global = tile_position * height + jnp.arange(height)
    own_mask = (row_global > 0).astype(jnp.float32)[:, None]
    zonal = jnp.concatenate(
        [south_courant[:levels], courant[:levels], north_courant[:levels]], axis=1
    )
    meridional = jnp.concatenate(
        [
            south_courant[levels:],
            courant[levels:] * own_mask,
            north_courant[levels:],
        ],
        axis=1,
    )
    mixing = jnp.concatenate([south_tracers, tracers, north_tracers], axis=2)

    def count_of(position):
        clamped = jnp.clip(position, 0, tiles - 1)
        return jnp.sum(jnp.where(tile_numbers == clamped, substeps, 0))

    row_counts = jnp.concatenate(
        [
            jnp.full((halo,), count_of(tile_position - 1)),
            jnp.full((height,), count_of(tile_position)),
            jnp.full((halo,), count_of(tile_position + 1)),
        ]
    )
    counts_float = row_counts.astype(jnp.float32)
    for substep in range(ROUNDS):
        fraction = jnp.where(substep < row_counts, 1.0 / counts_float, jnp.float32(0.0))
        mixing = advance(mixing, zonal, meridional, fraction[:, None])
    mixing = mixing[:, :, halo : halo + height]
    mixing = mixing.at[:, 0].add(emissions)
    return thomas_solve(mixing, coefficient)


def solution(mesh):
    return jax.shard_map(
        shards,
        mesh=mesh,
        in_specs=(
            P("group", None, "tile", None),
            P("group", "tile", None),
            P("group", None, None, "tile", None),
            P("group", None, "tile", None),
            P(),
            P(),
        ),
        out_specs=P("group", None, "tile", None),
        check_vma=False,
    )
```

time: 261 us -> 166 us (0.64)
  waiting for transfers between devices: 188 us -> 52.7 us
  other arithmetic: 14.1 us -> 49.8 us
  local copies, waits for them, and re-layouts: 11.5 us -> 34.8 us
  between operations: 19.3 us -> 1.21 us
    psum x1 -> x0, waiting for transfers between devices: 111 us -> none  [spread(): return lax.psum(jnp.where(mine, value, jnp.zeros_like(value)), axis)]
    ppermute x12 -> x4, waiting for transfers between devices: 76.8 us -> 43.1 us  [from_behind(): return lax.ppermute(value, axis, pairs)]
    sub x6, other arithmetic: 3.85 us -> 24.5 us  [advance(): mixing - fraction * (east_flux - west_flux + (north_flux - south_flux))]
    slice x46 -> x28, local copies, waits for them, and re-layouts: 6.36 us -> 25.9 us  [the longest x6 11 us: advance(): north_flux = jnp.concatenate([south_flux[:, :, 1:], zeros_row], axis=2)]
    add x6, other arithmetic: 4.09 us -> 16.3 us  [advance(): jnp.maximum(meridional, 0.0) * from_south]
    ppermute x0 -> x4, waiting for transfers between devices: none -> 9.6 us  [broadcast_from(): received = lax.ppermute(current, axis, pairs)]
    ppermute x12 -> x4, starting transfers between devices: 27.6 us -> 20.6 us  [from_behind(): return lax.ppermute(value, axis, pairs)]
    ppermute x0 -> x4, starting transfers between devices: none -> 6.49 us  [broadcast_from(): received = lax.ppermute(current, axis, pairs)]
  transfers between devices with their start and end apart: 13 -> 8, of which waited for: 13 -> 5; matrix products, arithmetic and copies ran while one was open for 2% -> 5% of each run, Pallas kernels for 0% -> 0%
where the time goes in v1:
time: 166 us
  waiting for transfers between devices  52.7 us (32%)
  other arithmetic  49.8 us (30%)
  local copies, waits for them, and re-layouts  34.8 us (21%)
  starting transfers between devices  27.1 us (16%)
    ppermute x4, waiting for transfers between devices, from_behind(): return lax.ppermute(value, axis, pairs)  43.1 us
    sub x6, other arithmetic, advance(): mixing - fraction * (east_flux - west_flux + (north_flux - south_flux))  24.5 us
    ppermute x4, starting transfers between devices, from_behind(): return lax.ppermute(value, axis, pairs)  20.6 us
    add x6, other arithmetic, advance(): jnp.maximum(meridional, 0.0) * from_south  16.3 us
    slice x6, local copies, waits for them, and re-layouts, advance(): north_flux = jnp.concatenate([south_flux[:, :, 1:], zeros_row], axis=2)  11 us
    ppermute x4, waiting for transfers between devices, broadcast_from(): received = lax.ppermute(current, axis, pairs)  9.6 us
    slice x6, local copies, waits for them, and re-layouts, advance(): from_west = jnp.roll(mixing, 1, axis=3)  8.77 us
    ppermute x4, starting transfers between devices, broadcast_from(): received = lax.ppermute(current, axis, pairs)  6.49 us
  transfers between devices with their start and end apart: 8, of which 5 were waited for; matrix products, arithmetic and copies ran while one was open for 5% of the time, Pallas kernels for 0%

profile of v1, /device:TPU:88, one launch (start us, length us, event | category | flops | bytes accessed | tf_op | source)
XLA Modules:
  0.0 165.6 jit_solution(5576833407254321444)
XLA Ops:
  6.3 9.6 %collective-permute-done.3 = f32[47,8,256]{2,1,0:T(8,128)S(1)} collective-permute-done((f32[47,8,256]{2,1,0:T(8,128)S(1)}, f32[47,8,256]{2,1,0:T(8,128)S(1)}, u32[]{:S(2)}, u32[]{:S(2)}) %collective-permute-start.3) | collective-permute-done | bytes 385056 | tf_op jit(solution)/shard_map/ppermute | solution.py:23
  17.9 2.7 %collective-permute-start.1 = (f32[8,16,6,256]{3,1,2,0:T(8,128)S(1)}, f32[8,16,6,256]{3,1,2,0:T(8,128)S(1)}, u32[]{:S(2)}, u32[]{:S(2)}) collective-permute-start(f32[8,16,6,256]{3,1,2,0:T(8,128)S(1)} %copy.12), channel_id=1, source_target_pairs={{16,0},{32,16},{48,32},{64,48},{80,64},{96,80},{112,96},{128,112},... | collective-permute-start | bytes 2359304 | tf_op jit(solution)/shard_map/ppermute | solution.py:12
  21.7 7.4 %collective-permute-start = (f32[8,16,6,256]{3,1,2,0:T(8,128)}, f32[8,16,6,256]{3,1,2,0:T(8,128)}, u32[]{:S(2)}, u32[]{:S(2)}) collective-permute-start(f32[8,16,6,256]{3,1,2,0:T(8,128)} %copy.11), channel_id=1, source_target_pairs={{0,16},{16,32},{32,48},{48,64},{64,80},{80,96},{96,112},{112,128},... | collective-permute-start | bytes 2359304 | tf_op jit(solution)/shard_map/ppermute | solution.py:12
  32.0 2.8 %collective-permute-start.5 = (f32[47,8,256]{2,1,0:T(8,128)S(1)}, f32[47,8,256]{2,1,0:T(8,128)S(1)}, u32[]{:S(2)}, u32[]{:S(2)}) collective-permute-start(f32[47,8,256]{2,1,0:T(8,128)S(1)} %broadcast_select_fusion.2), channel_id=1, source_target_pairs={{0,8},{1,9},{2,10},{3,11},{4,12},{5,13},{6,14},{7,15},{8,0},{9,1},... | collective-permute-start | bytes 1155080 | tf_op jit(solution)/shard_map/ppermute | solution.py:23
  34.8 25.1 %collective-permute-done.1 = f32[8,16,6,256]{3,1,2,0:T(8,128)S(1)} collective-permute-done((f32[8,16,6,256]{3,1,2,0:T(8,128)S(1)}, f32[8,16,6,256]{3,1,2,0:T(8,128)S(1)}, u32[]{:S(2)}, u32[]{:S(2)}) %collective-permute-start.1) | collective-permute-done | bytes 786464 | tf_op jit(solution)/shard_map/ppermute | solution.py:12
  60.3 2.1 %collective-permute-done = f32[8,16,6,256]{3,1,2,0:T(8,128)} collective-permute-done((f32[8,16,6,256]{3,1,2,0:T(8,128)}, f32[8,16,6,256]{3,1,2,0:T(8,128)}, u32[]{:S(2)}, u32[]{:S(2)}) %collective-permute-start) | collective-permute-done | bytes 786464 | tf_op jit(solution)/shard_map/ppermute | solution.py:12
  65.4 8.7 %collective-permute-start.6 = (f32[32,6,256]{2,1,0:T(8,128)S(1)}, f32[32,6,256]{2,1,0:T(8,128)S(1)}, u32[]{:S(2)}, u32[]{:S(2)}) collective-permute-start(f32[32,6,256]{2,1,0:T(8,128)S(1)} %get-tuple-element.104), channel_id=1, source_target_pairs={{0,16},{16,32},{32,48},{48,64},{64,80},{80,96},{96,112},{112,128},... | collective-permute-start | bytes 589832 | tf_op jit(solution)/shard_map/ppermute | solution.py:12
  76.1 6.1 %collective-permute-done.6 = f32[32,6,256]{2,1,0:T(8,128)S(1)} collective-permute-done((f32[32,6,256]{2,1,0:T(8,128)S(1)}, f32[32,6,256]{2,1,0:T(8,128)S(1)}, u32[]{:S(2)}, u32[]{:S(2)}) %collective-permute-start.6) | collective-permute-done | bytes 196640 | tf_op jit(solution)/shard_map/ppermute | solution.py:12
  82.2 9.8 %collective-permute-done.7 = f32[32,6,256]{2,1,0:T(8,128)S(1)} collective-permute-done((f32[32,6,256]{2,1,0:T(8,128)S(1)}, f32[32,6,256]{2,1,0:T(8,128)S(1)}, u32[]{:S(2)}, u32[]{:S(2)}) %collective-permute-start.7) | collective-permute-done | bytes 196640 | tf_op jit(solution)/shard_map/ppermute | solution.py:12
  99.1 2.9 %multiply_add_fusion.4 = (f32[8,16,20,256]{3,2,1,0:T(8,128)S(1)}, f32[8,16,20,256]{3,2,1,0:T(8,128)S(1)}) fusion(f32[8,16,20,256]{3,2,1,0:T(8,128)S(1)} %fusion.3, f32[8,16,19,256]{3,2,1,0:T(8,128)S(1)} %bitcast.101, f32[16,20,256]{2,1,0:T(8,128)S(1)} %get-tuple-element.75, f32[16,20,256]{2,1,0:T(8,128)S(1)} %get-tuple-element.74, ...), kind=kLoop, calls=%fused_computation.41 | loop fusion | flops 4587520 | bytes 14286848 | tf_op jit(solution)/shard_map/add | solution.py:59
  103.6 2.1 %slice.409 = f32[8,16,19,256]{3,2,1,0:T(8,128)} slice(f32[8,16,20,256]{3,2,1,0:T(8,128)S(1)} %get-tuple-element.68), slice={[0:8], [0:16], [1:20], [0:256]} | slice | bytes 4980736 | tf_op jit(solution)/shard_map/slice | solution.py:60
  105.7 4.3 %fusion.7 = f32[8,16,20,256]{3,2,1,0:T(8,128)S(1)} fusion(f32[8,16,20,256]{3,2,1,0:T(8,128)S(1)} %fusion.3, f32[8,16,20,256]{3,2,1,0:T(8,128)S(1)} %get-tuple-element.69, f32[8,16,20,1]{3,2,1,0:T(8,128)S(1)} %slice.407, f32[8,16,20,255]{3,2,1,0:T(8,128)S(1)} %slice.406, f32[8,16,20,256]{3,2,1,0:T(8,128)} %copy-done.1, f32[8,16,19,256]{3,2,1,0:T(8,128)} %slice.409, ...), kind=kLoop, calls=%fused_computation.12 | loop fusion | flops 3932160 | bytes 15597648 | tf_op jit(solution)/shard_map/sub | solution.py:61
  111.7 2.9 %multiply_add_fusion.3 = (f32[8,16,20,256]{3,2,1,0:T(8,128)S(1)}, f32[8,16,20,256]{3,2,1,0:T(8,128)S(1)}) fusion(f32[8,16,20,256]{3,2,1,0:T(8,128)S(1)} %fusion.7, f32[8,16,19,256]{3,2,1,0:T(8,128)S(1)} %bitcast.105, f32[16,20,256]{2,1,0:T(8,128)S(1)} %get-tuple-element.75, f32[16,20,256]{2,1,0:T(8,128)S(1)} %get-tuple-element.74, ...), kind=kLoop, calls=%fused_computation.40 | loop fusion | flops 4587520 | bytes 14286848 | tf_op jit(solution)/shard_map/add | solution.py:59
  116.2 2.1 %slice.415 = f32[8,16,19,256]{3,2,1,0:T(8,128)} slice(f32[8,16,20,256]{3,2,1,0:T(8,128)S(1)} %get-tuple-element.66), slice={[0:8], [0:16], [1:20], [0:256]} | slice | bytes 4980736 | tf_op jit(solution)/shard_map/slice | solution.py:60
  118.3 4.3 %fusion.11 = f32[8,16,20,256]{3,2,1,0:T(8,128)S(1)} fusion(f32[8,16,20,256]{3,2,1,0:T(8,128)S(1)} %fusion.7, f32[8,16,20,256]{3,2,1,0:T(8,128)S(1)} %get-tuple-element.67, f32[8,16,20,1]{3,2,1,0:T(8,128)S(1)} %slice.413, f32[8,16,20,255]{3,2,1,0:T(8,128)S(1)} %slice.412, f32[8,16,20,256]{3,2,1,0:T(8,128)} %copy-done.2, f32[8,16,19,256]{3,2,1,0:T(8,128)} %slice.415, ...), kind=kLoop, calls=%fused_computation.18 | loop fusion | flops 3932160 | bytes 15597648 | tf_op jit(solution)/shard_map/sub | solution.py:61
  124.3 2.9 %multiply_add_fusion.2 = (f32[8,16,20,256]{3,2,1,0:T(8,128)S(1)}, f32[8,16,20,256]{3,2,1,0:T(8,128)S(1)}) fusion(f32[8,16,20,256]{3,2,1,0:T(8,128)S(1)} %fusion.11, f32[8,16,19,256]{3,2,1,0:T(8,128)S(1)} %bitcast.107, f32[16,20,256]{2,1,0:T(8,128)S(1)} %get-tuple-element.75, f32[16,20,256]{2,1,0:T(8,128)S(1)} %get-tuple-element.74, ...), kind=kLoop, calls=%fused_computation.39 | loop fusion | flops 4587520 | bytes 14286848 | tf_op jit(solution)/shard_map/add | solution.py:59
  128.8 2.3 %slice.421 = f32[8,16,19,256]{3,2,1,0:T(8,128)} slice(f32[8,16,20,256]{3,2,1,0:T(8,128)S(1)} %get-tuple-element.64), slice={[0:8], [0:16], [1:20], [0:256]} | slice | bytes 4980736 | tf_op jit(solution)/shard_map/slice | solution.py:60
  131.1 4.3 %fusion.15 = f32[8,16,20,256]{3,2,1,0:T(8,128)S(1)} fusion(f32[8,16,20,256]{3,2,1,0:T(8,128)S(1)} %fusion.11, f32[8,16,20,256]{3,2,1,0:T(8,128)S(1)} %get-tuple-element.65, f32[8,16,20,1]{3,2,1,0:T(8,128)S(1)} %slice.419, f32[8,16,20,255]{3,2,1,0:T(8,128)S(1)} %slice.418, f32[8,16,20,256]{3,2,1,0:T(8,128)} %copy-done.3, f32[8,16,19,256]{3,2,1,0:T(8,128)} %slice.421, ...), kind=kLoop, calls=%fused_computation.24 | loop fusion | flops 3932160 | bytes 15597648 | tf_op jit(solution)/shard_map/sub | solution.py:61
  137.1 2.9 %multiply_add_fusion.1 = (f32[8,16,20,256]{3,2,1,0:T(8,128)S(1)}, f32[8,16,20,256]{3,2,1,0:T(8,128)S(1)}) fusion(f32[8,16,20,256]{3,2,1,0:T(8,128)S(1)} %fusion.15, f32[8,16,19,256]{3,2,1,0:T(8,128)S(1)} %bitcast.103, f32[16,20,256]{2,1,0:T(8,128)S(1)} %get-tuple-element.75, f32[16,20,256]{2,1,0:T(8,128)S(1)} %get-tuple-element.74, ...), kind=kLoop, calls=%fused_computation.38 | loop fusion | flops 4587520 | bytes 14286848 | tf_op jit(solution)/shard_map/add | solution.py:59
  141.6 2.1 %slice.427 = f32[8,16,19,256]{3,2,1,0:T(8,128)} slice(f32[8,16,20,256]{3,2,1,0:T(8,128)S(1)} %get-tuple-element.62), slice={[0:8], [0:16], [1:20], [0:256]} | slice | bytes 4980736 | tf_op jit(solution)/shard_map/slice | solution.py:60
  143.7 4.3 %fusion.19 = f32[8,16,20,256]{3,2,1,0:T(8,128)S(1)} fusion(f32[8,16,20,256]{3,2,1,0:T(8,128)S(1)} %fusion.15, f32[8,16,20,256]{3,2,1,0:T(8,128)S(1)} %get-tuple-element.63, f32[8,16,20,1]{3,2,1,0:T(8,128)S(1)} %slice.425, f32[8,16,20,255]{3,2,1,0:T(8,128)S(1)} %slice.424, f32[8,16,20,256]{3,2,1,0:T(8,128)} %copy-done, f32[8,16,19,256]{3,2,1,0:T(8,128)} %slice.427, ...), kind=kLoop, calls=%fused_computation.30 | loop fusion | flops 3932160 | bytes 15597648 | tf_op jit(solution)/shard_map/sub | solution.py:61
  149.7 2.9 %multiply_add_fusion = (f32[8,16,20,256]{3,2,1,0:T(8,128)S(1)}, f32[8,16,20,256]{3,2,1,0:T(8,128)S(1)}) fusion(f32[8,16,20,256]{3,2,1,0:T(8,128)S(1)} %fusion.19, f32[8,16,19,256]{3,2,1,0:T(8,128)S(1)} %bitcast.99, f32[16,20,256]{2,1,0:T(8,128)S(1)} %get-tuple-element.75, f32[16,20,256]{2,1,0:T(8,128)S(1)} %get-tuple-element.74, ...), kind=kLoop, calls=%fused_computation.37 | loop fusion | flops 4587520 | bytes 14286848 | tf_op jit(solution)/shard_map/add | solution.py:59
  153.6 2.0 %slice.433 = f32[8,16,19,256]{3,2,1,0:T(8,128)} slice(f32[8,16,20,256]{3,2,1,0:T(8,128)S(1)} %get-tuple-element.60), slice={[0:8], [0:16], [1:20], [0:256]} | slice | bytes 4980736 | tf_op jit(solution)/shard_map/slice | solution.py:60
  155.6 5.2 %fusion.23 = f32[8,16,20,256]{3,2,1,0:T(8,128)} fusion(f32[8,16,20,256]{3,2,1,0:T(8,128)S(1)} %fusion.19, f32[8,16,20,256]{3,2,1,0:T(8,128)S(1)} %get-tuple-element.61, f32[8,16,20,1]{3,2,1,0:T(8,128)S(1)} %slice.431, f32[8,16,20,255]{3,2,1,0:T(8,128)S(1)} %slice.430, f32[8,16,20,256]{3,2,1,0:T(8,128)S(1)} %get-tuple-element.60, ...), kind=kLoop, calls=%fused_computation.36 | loop fusion | flops 3932160 | bytes 15597648 | tf_op jit(solution)/shard_map/sub | solution.py:61
  (93 shorter events, 42.7 us)
Async XLA Ops:
  0.0 17.5 %copy-start.4 = (f32[8,16,8,256]{3,2,1,0:T(8,128)S(1)}, f32[8,16,8,256]{3,2,1,0:T(8,128)}, u32[]{:S(2)}) copy-start(f32[8,16,8,256]{3,2,1,0:T(8,128)} %param.8) | copy-start | bytes 3145732
  1.1 2.1 %collective-permute-start.2 = (f32[47,8,256]{2,1,0:T(8,128)S(1)}, f32[47,8,256]{2,1,0:T(8,128)S(1)}, u32[]{:S(2)}, u32[]{:S(2)}) collective-permute-start(f32[47,8,256]{2,1,0:T(8,128)S(1)} %pad_maximum_fusion.3), channel_id=1, source_target_pairs={{0,1},{1,0},{2,3},{3,2},{4,5},{5,4},{6,7},{7,6},{8,9},{9,8},{10,11... | collective-permute-start | bytes 1155080 | tf_op jit(solution)/shard_map/ppermute | solution.py:23
  4.3 11.6 %collective-permute-start.3 = (f32[47,8,256]{2,1,0:T(8,128)S(1)}, f32[47,8,256]{2,1,0:T(8,128)S(1)}, u32[]{:S(2)}, u32[]{:S(2)}) collective-permute-start(f32[47,8,256]{2,1,0:T(8,128)S(1)} %broadcast_select_fusion), channel_id=1, source_target_pairs={{0,2},{1,3},{2,0},{3,1},{4,6},{5,7},{6,4},{7,5},{8,10},{9,11},{10,... | collective-permute-start | bytes 1155080 | tf_op jit(solution)/shard_map/ppermute | solution.py:23
  15.9 13.3 %copy-start.7 = (s32[16]{0:T(128)S(1)}, s32[16]{0:T(128)}, u32[]{:S(2)}) copy-start(s32[16]{0:T(128)} %param.12) | copy-start | bytes 196
  15.9 16.0 %collective-permute-start.4 = (f32[47,8,256]{2,1,0:T(8,128)S(1)}, f32[47,8,256]{2,1,0:T(8,128)S(1)}, u32[]{:S(2)}, u32[]{:S(2)}) collective-permute-start(f32[47,8,256]{2,1,0:T(8,128)S(1)} %broadcast_select_fusion.1), channel_id=1, source_target_pairs={{0,4},{1,5},{2,6},{3,7},{4,0},{5,1},{6,2},{7,3},{8,12},{9,13},{10,... | collective-permute-start | bytes 1155080 | tf_op jit(solution)/shard_map/ppermute | solution.py:23
  17.9 41.9 %collective-permute-start.1 = (f32[8,16,6,256]{3,1,2,0:T(8,128)S(1)}, f32[8,16,6,256]{3,1,2,0:T(8,128)S(1)}, u32[]{:S(2)}, u32[]{:S(2)}) collective-permute-start(f32[8,16,6,256]{3,1,2,0:T(8,128)S(1)} %copy.12), channel_id=1, source_target_pairs={{16,0},{32,16},{48,32},{64,48},{80,64},{96,80},{112,96},{128,112},... | collective-permute-start | bytes 2359304 | tf_op jit(solution)/shard_map/ppermute | solution.py:12
  21.7 40.8 %collective-permute-start = (f32[8,16,6,256]{3,1,2,0:T(8,128)}, f32[8,16,6,256]{3,1,2,0:T(8,128)}, u32[]{:S(2)}, u32[]{:S(2)}) collective-permute-start(f32[8,16,6,256]{3,1,2,0:T(8,128)} %copy.11), channel_id=1, source_target_pairs={{0,16},{16,32},{32,48},{48,64},{64,80},{80,96},{96,112},{112,128},... | collective-permute-start | bytes 2359304 | tf_op jit(solution)/shard_map/ppermute | solution.py:12
  32.0 33.1 %collective-permute-start.5 = (f32[47,8,256]{2,1,0:T(8,128)S(1)}, f32[47,8,256]{2,1,0:T(8,128)S(1)}, u32[]{:S(2)}, u32[]{:S(2)}) collective-permute-start(f32[47,8,256]{2,1,0:T(8,128)S(1)} %broadcast_select_fusion.2), channel_id=1, source_target_pairs={{0,8},{1,9},{2,10},{3,11},{4,12},{5,13},{6,14},{7,15},{8,0},{9,1},... | collective-permute-start | bytes 1155080 | tf_op jit(solution)/shard_map/ppermute | solution.py:23
  65.4 16.7 %collective-permute-start.6 = (f32[32,6,256]{2,1,0:T(8,128)S(1)}, f32[32,6,256]{2,1,0:T(8,128)S(1)}, u32[]{:S(2)}, u32[]{:S(2)}) collective-permute-start(f32[32,6,256]{2,1,0:T(8,128)S(1)} %get-tuple-element.104), channel_id=1, source_target_pairs={{0,16},{16,32},{32,48},{48,64},{64,80},{80,96},{96,112},{112,128},... | collective-permute-start | bytes 589832 | tf_op jit(solution)/shard_map/ppermute | solution.py:12
  74.1 17.9 %collective-permute-start.7 = (f32[32,6,256]{2,1,0:T(8,128)S(1)}, f32[32,6,256]{2,1,0:T(8,128)S(1)}, u32[]{:S(2)}, u32[]{:S(2)}) collective-permute-start(f32[32,6,256]{2,1,0:T(8,128)S(1)} %get-tuple-element.105), channel_id=1, source_target_pairs={{16,0},{32,16},{48,32},{64,48},{80,64},{96,80},{112,96},{128,112},... | collective-permute-start | bytes 589832 | tf_op jit(solution)/shard_map/ppermute | solution.py:12
  102.0 1.6 copy-start.1
  114.6 1.6 copy-start.2
  127.2 1.6 copy-start.3
  140.0 1.6 copy-start
  155.6 5.2 %copy-start.5 = (f32[8,8,256]{2,1,0:T(8,128)S(1)}, f32[8,8,256]{2,1,0:T(8,128)}, u32[]{:S(2)}) copy-start(f32[8,8,256]{2,1,0:T(8,128)} %param.9) | copy-start | bytes 196612
  163.0 1.0 copy-start.6

commit v2 on v1

v2 whole, which is shorter than its diff:
```python
import jax
import jax.numpy as jnp
from jax import lax
from jax.experimental import pallas as pl
from jax.experimental.pallas import tpu as pltpu
from jax.sharding import PartitionSpec as P

ROUNDS = 6


def from_behind(value, axis, by):
    count = lax.axis_size(axis)
    pairs = [(i, i + by) for i in range(count) if 0 <= i + by < count]
    return lax.ppermute(value, axis, pairs)


def broadcast_from(value, axis, root):
    count = lax.axis_size(axis)
    assert count & (count - 1) == 0
    distance = lax.axis_index(axis) ^ root
    current = value
    bit = 0
    while (1 << bit) < count:
        pairs = [(i, i ^ (1 << bit)) for i in range(count)]
        received = lax.ppermute(current, axis, pairs)
        current = jnp.where((distance >> bit) == 1, received, current)
        bit += 1
    return current


def transport_kernel(
    scalars, own, north, south, courant, north_courant, south_courant, coefficient,
    emissions, out, zonal_up, zonal_down, merid_up, merid_down, fractions, pivots,
    ratios, held,
):
    levels = own.shape[1]
    height = own.shape[2]
    width = own.shape[3]
    extent = 3 * height

    @pl.when(pl.program_id(0) == 0)
    def _prepare():
        row = lax.broadcasted_iota(jnp.int32, (extent, width), 0)
        for substep in range(ROUNDS):
            fractions[substep] = jnp.where(
                row < height,
                scalars[3 * substep],
                jnp.where(row < 2 * height, scalars[3 * substep + 1], scalars[3 * substep + 2]),
            )
        own_row = lax.broadcasted_iota(jnp.int32, (height, width), 0)
        mask = jnp.where(own_row == 0, scalars[3 * ROUNDS], jnp.float32(1.0))
        for level in range(levels):
            zonal = jnp.concatenate(
                [courant[level], north_courant[level], south_courant[level]], axis=0
            )
            meridional = jnp.concatenate(
                [
                    courant[levels + level] * mask,
                    north_courant[levels + level],
                    south_courant[levels + level],
                ],
                axis=0,
            )
            zonal_up[level] = jnp.maximum(zonal, 0.0)
            zonal_down[level] = jnp.minimum(zonal, 0.0)
            merid_up[level] = jnp.maximum(meridional, 0.0)
            merid_down[level] = jnp.minimum(meridional, 0.0)
        zero_plane = jnp.zeros((height, width), jnp.float32)
        previous_ratio = zero_plane
        for level in range(levels):
            lower_coef = coefficient[level - 1] if level > 0 else zero_plane
            upper_coef = coefficient[level] if level < levels - 1 else zero_plane
            pivot = 1.0 / (1.0 + lower_coef + upper_coef - lower_coef * previous_ratio)
            previous_ratio = upper_coef * pivot
            pivots[level] = pivot
            ratios[level] = previous_ratio

    def advect(level, carry):
        mixing = jnp.concatenate([own[0, level], north[0, level], south[0, level]], axis=0)
        z_up = zonal_up[level]
        z_down = zonal_down[level]
        m_up = merid_up[level]
        m_down = merid_down[level]
        for substep in range(ROUNDS):
            from_west = pltpu.roll(mixing, 1, 1)
            west_flux = z_up * from_west + z_down * mixing
            east_flux = pltpu.roll(west_flux, width - 1, 1)
            from_south = pltpu.roll(mixing, 1, 0)
            south_flux = m_up * from_south + m_down * mixing
            north_flux = pltpu.roll(south_flux, extent - 1, 0)
            mixing = mixing - fractions[substep] * (
                (east_flux - west_flux) + (north_flux - south_flux)
            )
        held[level] = mixing[:height]
        return carry

    lax.fori_loop(0, levels, advect, 0)
    held[0] = held[0] + emissions[0]
    zero_plane = jnp.zeros((height, width), jnp.float32)
    previous_value = zero_plane
    for level in range(levels):
        lower_coef = coefficient[level - 1] if level > 0 else zero_plane
        previous_value = (held[level] + lower_coef * previous_value) * pivots[level]
        held[level] = previous_value
    current = held[levels - 1]
    out[0, levels - 1] = current
    for level in range(levels - 2, -1, -1):
        current = held[level] + ratios[level] * current
        out[0, level] = current


def transport(scalars, tracers, north, south, courant, north_courant, south_courant,
              coefficient, emissions):
    tracer_count, levels, height, width = tracers.shape
    extent = 3 * height
    block = pl.BlockSpec((1, levels, height, width), lambda i: (i, 0, 0, 0))

    def whole(shape):
        return pl.BlockSpec(shape, lambda i: (0,) * len(shape))

    plane = pltpu.VMEM((levels, extent, width), jnp.float32)
    return pl.pallas_call(
        transport_kernel,
        grid=(tracer_count,),
        out_shape=jax.ShapeDtypeStruct(tracers.shape, jnp.float32),
        in_specs=[
            pl.BlockSpec(memory_space=pltpu.SMEM),
            block,
            block,
            block,
            whole(courant.shape),
            whole(courant.shape),
            whole(courant.shape),
            whole(coefficient.shape),
            pl.BlockSpec((1, height, width), lambda i: (i, 0, 0)),
        ],
        out_specs=block,
        scratch_shapes=[
            plane,
            plane,
            plane,
            plane,
            pltpu.VMEM((ROUNDS, extent, width), jnp.float32),
            pltpu.VMEM((levels, height, width), jnp.float32),
            pltpu.VMEM((levels, height, width), jnp.float32),
            pltpu.VMEM((levels, height, width), jnp.float32),
        ],
        cost_estimate=pl.CostEstimate(
            flops=tracer_count * levels * extent * width * ROUNDS * 14,
            bytes_accessed=4 * (5 * tracers.size + 3 * courant.size),
            transcendentals=0,
        ),
    )(scalars, tracers, north, south, courant, north_courant, south_courant,
      coefficient, emissions)


def shards(tracers, emissions, winds, diffusivity, substeps, loader):
    tiles = lax.axis_size("tile")
    tile_position = lax.axis_index("tile")
    tile_numbers = jnp.arange(substeps.shape[0])
    loader_slot = jnp.sum(jnp.where(tile_numbers == tile_position, loader, 0))
    levels = tracers.shape[1]
    height = tracers.shape[2]
    width = tracers.shape[3]

    local = jnp.concatenate(
        [winds[0].reshape(2 * levels, height, width), diffusivity[0]], axis=0
    )
    chosen = broadcast_from(local, "group", loader_slot)
    courant = chosen[: 2 * levels]
    coefficient = chosen[2 * levels :]

    south_tracers = from_behind(tracers, "tile", 1)
    north_tracers = from_behind(tracers, "tile", -1)
    south_courant = from_behind(courant, "tile", 1)
    north_courant = from_behind(courant, "tile", -1)

    def count_of(position):
        clamped = jnp.clip(position, 0, tiles - 1)
        return jnp.sum(jnp.where(tile_numbers == clamped, substeps, 0))

    counts = jnp.stack(
        [count_of(tile_position), count_of(tile_position + 1), count_of(tile_position - 1)]
    )
    counts_float = counts.astype(jnp.float32)
    steps = jnp.arange(ROUNDS)[:, None]
    fractions = jnp.where(steps < counts[None, :], 1.0 / counts_float[None, :], jnp.float32(0.0))
    first_row = jnp.where(tile_position > 0, jnp.float32(1.0), jnp.float32(0.0))
    scalars = jnp.concatenate([fractions.reshape(-1), first_row[None]])
    return transport(
        scalars, tracers, north_tracers, south_tracers, courant, north_courant,
        south_courant, coefficient, emissions,
    )


def solution(mesh):
    return jax.shard_map(
        shards,
        mesh=mesh,
        in_specs=(
            P("group", None, "tile", None),
            P("group", "tile", None),
            P("group", None, None, "tile", None),
            P("group", None, "tile", None),
            P(),
            P(),
        ),
        out_specs=P("group", None, "tile", None),
        check_vma=False,
    )
```

time: 166 us -> 200 us (1.20)
  the two profiles are of different devices: /device:TPU:88 before, /device:TPU:161 now
where the time goes in v2:
time: 200 us; the launch traced here: 198 us
  Pallas kernels  113 us (56%)
  waiting for transfers between devices  53.6 us (27%)
  starting transfers between devices  21.7 us (11%)
  other arithmetic  5.13 us (3%)
  local copies, waits for them, and re-layouts  3.48 us (2%)
    pallas_call x1, Pallas kernels, transport(): pl.pallas_call(transport_kernel, grid=(tracer_count,), out_shape=jax.Shap...  113 us
    ppermute x4, waiting for transfers between devices, from_behind(): return lax.ppermute(value, axis, pairs)  37.7 us
    ppermute x4, starting transfers between devices, from_behind(): return lax.ppermute(value, axis, pairs)  16 us
    ppermute x4, waiting for transfers between devices, broadcast_from(): received = lax.ppermute(current, axis, pairs)  15.9 us
    ppermute x4, starting transfers between devices, broadcast_from(): received = lax.ppermute(current, axis, pairs)  5.71 us
  transfers between devices with their start and end apart: 8, of which 5 were waited for; matrix products, arithmetic and copies ran while one was open for 2% of the time, Pallas kernels for 0%

profile of v2, /device:TPU:161, one launch (start us, length us, event | category | flops | bytes accessed | tf_op | source)
XLA Modules:
  0.0 197.9 jit_solution(12665736726802455745)
XLA Ops:
  0.0 1.1 pad_maximum_fusion
  1.1 0.8 collective-permute-start.2
  1.9 0.7 copy-done.8
  2.5 0.6 fusion.4
  3.9 0.8 collective-permute-start.3
  4.7 9.8 %collective-permute-done.3 = f32[47,8,256]{2,1,0:T(8,128)S(1)} collective-permute-done((f32[47,8,256]{2,1,0:T(8,128)S(1)}, f32[47,8,256]{2,1,0:T(8,128)S(1)}, u32[]{:S(2)}, u32[]{:S(2)}) %collective-permute-start.3) | collective-permute-done | bytes 385056 | tf_op jit(solution)/shard_map/ppermute | solution.py:25
  14.6 1.3 collective-permute-start.4
  15.9 4.6 %collective-permute-start = (f32[8,16,8,256]{3,2,1,0:T(8,128)S(1)}, f32[8,16,8,256]{3,2,1,0:T(8,128)S(1)}, u32[]{:S(2)}, u32[]{:S(2)}) collective-permute-start(f32[8,16,8,256]{3,2,1,0:T(8,128)S(1)} %copy-done.1), channel_id=1, source_target_pairs={{16,0},{32,16},{48,32},{64,48},{80,64},{96,80},{112,96},{128,112},... | collective-permute-start | bytes 3145736 | tf_op jit(solution)/shard_map/ppermute | solution.py:14
  20.5 1.9 collective-permute-start.1
  22.5 1.9 collective-permute-done.4
  24.4 2.8 %collective-permute-start.5 = (f32[47,8,256]{2,1,0:T(8,128)S(1)}, f32[47,8,256]{2,1,0:T(8,128)S(1)}, u32[]{:S(2)}, u32[]{:S(2)}) collective-permute-start(f32[47,8,256]{2,1,0:T(8,128)S(1)} %broadcast_select_fusion.2), channel_id=1, source_target_pairs={{0,8},{1,9},{2,10},{3,11},{4,12},{5,13},{6,14},{7,15},{8,0},{9,1},... | collective-permute-start | bytes 1155080 | tf_op jit(solution)/shard_map/ppermute | solution.py:25
  27.2 0.7 copy-done.7
  27.9 0.7 fusion.1
  28.6 2.0 convert_divide_fusion
  30.5 4.2 %collective-permute-done.5 = f32[47,8,256]{2,1,0:T(8,128)S(1)} collective-permute-done((f32[47,8,256]{2,1,0:T(8,128)S(1)}, f32[47,8,256]{2,1,0:T(8,128)S(1)}, u32[]{:S(2)}, u32[]{:S(2)}) %collective-permute-start.5) | collective-permute-done | bytes 385056 | tf_op jit(solution)/shard_map/ppermute | solution.py:25
  34.8 3.2 %collective-permute-start.7 = (f32[32,8,256]{2,1,0:T(8,128)S(1)}, f32[32,8,256]{2,1,0:T(8,128)S(1)}, u32[]{:S(2)}, u32[]{:S(2)}) collective-permute-start(f32[32,8,256]{2,1,0:T(8,128)S(1)} %slice.8.courant), channel_id=1, source_target_pairs={{0,16},{16,32},{32,48},{48,64},{64,80},{80,96},{96,112},{112,128},... | collective-permute-start | bytes 786440 | tf_op jit(solution)/shard_map/ppermute | solution.py:14
  38.0 6.3 %collective-permute-start.6 = (f32[32,8,256]{2,1,0:T(8,128)S(1)}, f32[32,8,256]{2,1,0:T(8,128)S(1)}, u32[]{:S(2)}, u32[]{:S(2)}) collective-permute-start(f32[32,8,256]{2,1,0:T(8,128)S(1)} %slice.8.courant), channel_id=1, source_target_pairs={{16,0},{32,16},{48,32},{64,48},{80,64},{96,80},{112,96},{128,112},... | collective-permute-start | bytes 786440 | tf_op jit(solution)/shard_map/ppermute | solution.py:14
  44.4 0.6 pad_maximum_fusion.1.scalars
  45.0 0.7 slice.9.coefficient
  45.7 32.2 %collective-permute-done.1.south = f32[8,16,8,256]{3,2,1,0:T(8,128)} collective-permute-done((f32[8,16,8,256]{3,2,1,0:T(8,128)S(1)}, f32[8,16,8,256]{3,2,1,0:T(8,128)}, u32[]{:S(2)}, u32[]{:S(2)}) %collective-permute-start.1) | collective-permute-done | bytes 1048608 | tf_op jit(solution)/shard_map/ppermute | solution.py:14
  77.8 5.5 %collective-permute-done.7.south_courant = f32[32,8,256]{2,1,0:T(8,128)S(1)} collective-permute-done((f32[32,8,256]{2,1,0:T(8,128)S(1)}, f32[32,8,256]{2,1,0:T(8,128)S(1)}, u32[]{:S(2)}, u32[]{:S(2)}) %collective-permute-start.7) | collective-permute-done | bytes 262176 | tf_op jit(solution)/shard_map/ppermute | solution.py:14
  83.3 0.7 copy-done.5
  84.0 0.7 copy-done.6
  84.7 113.2 %shard_map.64 = f32[8,16,8,256]{3,2,1,0:T(8,128)} custom-call(f32[19]{0:T(128)} %pad_maximum_fusion.1.scalars, f32[8,16,8,256]{3,2,1,0:T(8,128)} %own.1, f32[8,16,8,256]{3,2,1,0:T(8,128)} %copy-done.2, f32[8,16,8,256]{3,2,1,0:T(8,128)} %collective-permute-done.1.south, f32[32,8,256]{2,1,0:T(8,128)} %copy-done.3, f32[32,8,256]{2,1,0:T(8,128)} %copy-done.6, ...), custom_call_target="tpu_custom_call" | custom-call | flops 66060288 | bytes 6029312 | tf_op jit(solution)/shard_map/pallas_call | solution.py:122
  (24 shorter events, 0.3 us)
Async XLA Ops:
  0.0 3.8 %copy-start = (f32[1,2,16,8,256]{4,3,2,1,0:T(8,128)S(1)}, f32[1,2,16,8,256]{4,3,2,1,0:T(8,128)}, u32[]{:S(2)}) copy-start(f32[1,2,16,8,256]{4,3,2,1,0:T(8,128)} %param.8) | copy-start | bytes 786436
  0.0 3.8 %copy-start.4 = (f32[1,15,8,256]{3,2,1,0:T(8,128)S(1)}, f32[1,15,8,256]{3,2,1,0:T(8,128)}, u32[]{:S(2)}) copy-start(f32[1,15,8,256]{3,2,1,0:T(8,128)} %param.9) | copy-start | bytes 368644
  1.1 2.7 %collective-permute-start.2 = (f32[47,8,256]{2,1,0:T(8,128)S(1)}, f32[47,8,256]{2,1,0:T(8,128)S(1)}, u32[]{:S(2)}, u32[]{:S(2)}) collective-permute-start(f32[47,8,256]{2,1,0:T(8,128)S(1)} %pad_maximum_fusion), channel_id=1, source_target_pairs={{0,1},{1,0},{2,3},{3,2},{4,5},{5,4},{6,7},{7,6},{8,9},{9,8},{10,11... | collective-permute-start | bytes 1155080 | tf_op jit(solution)/shard_map/ppermute | solution.py:25
  1.9 0.7 copy-start.8
  3.8 12.1 %copy-start.1 = (f32[8,16,8,256]{3,2,1,0:T(8,128)S(1)}, f32[8,16,8,256]{3,2,1,0:T(8,128)}, u32[]{:S(2)}) copy-start(f32[8,16,8,256]{3,2,1,0:T(8,128)} %own.1) | copy-start | bytes 3145732
  3.9 10.6 %collective-permute-start.3 = (f32[47,8,256]{2,1,0:T(8,128)S(1)}, f32[47,8,256]{2,1,0:T(8,128)S(1)}, u32[]{:S(2)}, u32[]{:S(2)}) collective-permute-start(f32[47,8,256]{2,1,0:T(8,128)S(1)} %broadcast_select_fusion), channel_id=1, source_target_pairs={{0,2},{1,3},{2,0},{3,1},{4,6},{5,7},{6,4},{7,5},{8,10},{9,11},{10,... | collective-permute-start | bytes 1155080 | tf_op jit(solution)/shard_map/ppermute | solution.py:25
  14.6 9.8 %collective-permute-start.4 = (f32[47,8,256]{2,1,0:T(8,128)S(1)}, f32[47,8,256]{2,1,0:T(8,128)S(1)}, u32[]{:S(2)}, u32[]{:S(2)}) collective-permute-start(f32[47,8,256]{2,1,0:T(8,128)S(1)} %broadcast_select_fusion.1), channel_id=1, source_target_pairs={{0,4},{1,5},{2,6},{3,7},{4,0},{5,1},{6,2},{7,3},{8,12},{9,13},{10,... | collective-permute-start | bytes 1155080 | tf_op jit(solution)/shard_map/ppermute | solution.py:25
  15.9 29.8 %collective-permute-start = (f32[8,16,8,256]{3,2,1,0:T(8,128)S(1)}, f32[8,16,8,256]{3,2,1,0:T(8,128)S(1)}, u32[]{:S(2)}, u32[]{:S(2)}) collective-permute-start(f32[8,16,8,256]{3,2,1,0:T(8,128)S(1)} %copy-done.1), channel_id=1, source_target_pairs={{16,0},{32,16},{48,32},{64,48},{80,64},{96,80},{112,96},{128,112},... | collective-permute-start | bytes 3145736 | tf_op jit(solution)/shard_map/ppermute | solution.py:14
  20.5 57.3 %collective-permute-start.1 = (f32[8,16,8,256]{3,2,1,0:T(8,128)S(1)}, f32[8,16,8,256]{3,2,1,0:T(8,128)}, u32[]{:S(2)}, u32[]{:S(2)}) collective-permute-start(f32[8,16,8,256]{3,2,1,0:T(8,128)S(1)} %copy-done.1), channel_id=1, source_target_pairs={{0,16},{16,32},{32,48},{48,64},{64,80},{80,96},{96,112},{112,128},... | collective-permute-start | bytes 3145736 | tf_op jit(solution)/shard_map/ppermute | solution.py:14
  24.4 10.3 %collective-permute-start.5 = (f32[47,8,256]{2,1,0:T(8,128)S(1)}, f32[47,8,256]{2,1,0:T(8,128)S(1)}, u32[]{:S(2)}, u32[]{:S(2)}) collective-permute-start(f32[47,8,256]{2,1,0:T(8,128)S(1)} %broadcast_select_fusion.2), channel_id=1, source_target_pairs={{0,8},{1,9},{2,10},{3,11},{4,12},{5,13},{6,14},{7,15},{8,0},{9,1},... | collective-permute-start | bytes 1155080 | tf_op jit(solution)/shard_map/ppermute | solution.py:25
  27.2 0.7 copy-start.7
  34.8 48.5 %copy-start.3 = (f32[32,8,256]{2,1,0:T(8,128)}, f32[32,8,256]{2,1,0:T(8,128)S(1)}, u32[]{:S(2)}) copy-start(f32[32,8,256]{2,1,0:T(8,128)S(1)} %slice.8.courant) | copy-start | bytes 786436
  34.8 48.5 %collective-permute-start.7 = (f32[32,8,256]{2,1,0:T(8,128)S(1)}, f32[32,8,256]{2,1,0:T(8,128)S(1)}, u32[]{:S(2)}, u32[]{:S(2)}) collective-permute-start(f32[32,8,256]{2,1,0:T(8,128)S(1)} %slice.8.courant), channel_id=1, source_target_pairs={{0,16},{16,32},{32,48},{48,64},{64,80},{80,96},{96,112},{112,128},... | collective-permute-start | bytes 786440 | tf_op jit(solution)/shard_map/ppermute | solution.py:14
  38.0 45.3 %collective-permute-start.6 = (f32[32,8,256]{2,1,0:T(8,128)S(1)}, f32[32,8,256]{2,1,0:T(8,128)S(1)}, u32[]{:S(2)}, u32[]{:S(2)}) collective-permute-start(f32[32,8,256]{2,1,0:T(8,128)S(1)} %slice.8.courant), channel_id=1, source_target_pairs={{16,0},{32,16},{48,32},{64,48},{80,64},{96,80},{112,96},{128,112},... | collective-permute-start | bytes 786440 | tf_op jit(solution)/shard_map/ppermute | solution.py:14
  45.6 37.7 %copy-start.2 = (f32[8,16,8,256]{3,2,1,0:T(8,128)}, f32[8,16,8,256]{3,2,1,0:T(8,128)S(1)}, u32[]{:S(2)}) copy-start(f32[8,16,8,256]{3,2,1,0:T(8,128)S(1)} %collective-permute-done.north) | copy-start | bytes 3145732
  83.3 0.7 copy-start.5
  84.0 0.7 copy-start.6

commit v3 on v1

v3 whole, which is shorter than its diff:
```python
import jax
import jax.numpy as jnp
from jax import lax
from jax.experimental import pallas as pl
from jax.experimental.pallas import tpu as pltpu
from jax.sharding import PartitionSpec as P

ROUNDS = 6


def from_behind(value, axis, by):
    count = lax.axis_size(axis)
    pairs = [(i, i + by) for i in range(count) if 0 <= i + by < count]
    return lax.ppermute(value, axis, pairs)


def broadcast_from(value, axis, root):
    count = lax.axis_size(axis)
    assert count & (count - 1) == 0
    distance = lax.axis_index(axis) ^ root
    current = value
    bit = 0
    while (1 << bit) < count:
        pairs = [(i, i ^ (1 << bit)) for i in range(count)]
        received = lax.ppermute(current, axis, pairs)
        current = jnp.where((distance >> bit) == 1, received, current)
        bit += 1
    return current


def transport_kernel(
    scalars, own, south, north, courant, south_courant, north_courant, coefficient,
    emissions, out, held, pivots, ratios, lowers, planes,
):
    height, _, tracer_count, width = own.shape
    levels = held.shape[0]
    halo = south.shape[0]
    rows = height + 2 * halo
    level = pl.program_id(0)
    lane_shape = (tracer_count, width)

    def spread(row_ref, row):
        return jnp.broadcast_to(row_ref[pl.ds(row, 1), :], lane_shape)

    @pl.when(level == 0)
    def _prepare():
        zero_plane = jnp.zeros((height, width), jnp.float32)
        previous_ratio = zero_plane
        for lev in range(levels):
            lower_coef = coefficient[lev - 1] if lev > 0 else zero_plane
            upper_coef = coefficient[lev] if lev < levels - 1 else zero_plane
            pivot = 1.0 / (1.0 + lower_coef + upper_coef - lower_coef * previous_ratio)
            previous_ratio = upper_coef * pivot
            planes[0] = pivot
            planes[1] = previous_ratio
            planes[2] = lower_coef
            for row in range(height):
                pivots[lev, row] = spread(planes.at[0], row)
                ratios[lev, row] = spread(planes.at[1], row)
                lowers[lev, row] = spread(planes.at[2], row)

    def wind_row(component, row):
        index = component * levels + level
        if row < halo:
            return spread(south_courant.at[index], row)
        if row < halo + height:
            return spread(courant.at[index], row - halo)
        return spread(north_courant.at[index], row - halo - height)

    first_row = scalars[3 * ROUNDS]
    zonal_up, zonal_down, merid_up, merid_down = [], [], [], []
    for row in range(rows):
        zonal = wind_row(0, row)
        meridional = wind_row(1, row)
        if row == halo:
            meridional = meridional * first_row
        zonal_up.append(jnp.maximum(zonal, 0.0))
        zonal_down.append(jnp.minimum(zonal, 0.0))
        merid_up.append(jnp.maximum(meridional, 0.0))
        merid_down.append(jnp.minimum(meridional, 0.0))

    mixing = [south[row, 0] for row in range(halo)]
    mixing += [own[row, 0] for row in range(height)]
    mixing += [north[row, 0] for row in range(halo)]
    for substep in range(ROUNDS):
        low, high = substep + 1, rows - 2 - substep
        south_flux = {}
        for row in range(low, high + 2):
            south_flux[row] = merid_up[row] * mixing[row - 1] + merid_down[row] * mixing[row]
        advanced = list(mixing)
        for row in range(low, high + 1):
            band = 0 if row < halo else (1 if row < halo + height else 2)
            fraction = scalars[3 * substep + band]
            from_west = pltpu.roll(mixing[row], 1, 1)
            west_flux = zonal_up[row] * from_west + zonal_down[row] * mixing[row]
            east_flux = pltpu.roll(west_flux, width - 1, 1)
            advanced[row] = mixing[row] - fraction * (
                (east_flux - west_flux) + (south_flux[row + 1] - south_flux[row])
            )
        mixing = advanced
    for row in range(height):
        held[level, row] = mixing[halo + row]

    @pl.when(level == levels - 1)
    def _finish():
        for row in range(height):
            held[0, row] = held[0, row] + emissions[row]
            previous_value = jnp.zeros(lane_shape, jnp.float32)
            for lev in range(levels):
                previous_value = (
                    held[lev, row] + lowers[lev, row] * previous_value
                ) * pivots[lev, row]
                held[lev, row] = previous_value
            current = held[levels - 1, row]
            out[row, levels - 1] = current
            for lev in range(levels - 2, -1, -1):
                current = held[lev, row] + ratios[lev, row] * current
                out[row, lev] = current


def transport(scalars, own, south, north, courant, south_courant, north_courant,
              coefficient, emissions):
    height, levels, tracer_count, width = own.shape
    halo = south.shape[0]

    def whole(shape):
        return pl.BlockSpec(shape, lambda i: (0,) * len(shape))

    def by_level(shape):
        return pl.BlockSpec((shape[0], 1) + shape[2:], lambda i: (0, i, 0, 0))

    table = pltpu.VMEM((levels, height, tracer_count, width), jnp.float32)
    return pl.pallas_call(
        transport_kernel,
        grid=(levels,),
        out_shape=jax.ShapeDtypeStruct(own.shape, jnp.float32),
        in_specs=[
            pl.BlockSpec(memory_space=pltpu.SMEM),
            by_level(own.shape),
            by_level(south.shape),
            by_level(north.shape),
            whole(courant.shape),
            whole(south_courant.shape),
            whole(north_courant.shape),
            whole(coefficient.shape),
            whole(emissions.shape),
        ],
        out_specs=whole(own.shape),
        scratch_shapes=[
            table,
            table,
            table,
            table,
            pltpu.VMEM((3, height, width), jnp.float32),
        ],
        cost_estimate=pl.CostEstimate(
            flops=levels * tracer_count * width * 78 * 14,
            bytes_accessed=4 * (3 * own.size + 2 * south.size + 3 * courant.size),
            transcendentals=0,
        ),
    )(scalars, own, south, north, courant, south_courant, north_courant,
      coefficient, emissions)


def shards(tracers, emissions, winds, diffusivity, substeps, loader):
    tiles = lax.axis_size("tile")
    tile_position = lax.axis_index("tile")
    tile_numbers = jnp.arange(substeps.shape[0])
    loader_slot = jnp.sum(jnp.where(tile_numbers == tile_position, loader, 0))
    levels = tracers.shape[1]
    height = tracers.shape[2]
    width = tracers.shape[3]
    halo = ROUNDS

    local = jnp.concatenate(
        [winds[0].reshape(2 * levels, height, width), diffusivity[0]], axis=0
    )
    chosen = broadcast_from(local, "group", loader_slot)
    courant = chosen[: 2 * levels]
    coefficient = chosen[2 * levels :]

    by_row = jnp.transpose(tracers, (2, 1, 0, 3))
    south_rows = from_behind(by_row[height - halo :], "tile", 1)
    north_rows = from_behind(by_row[:halo], "tile", -1)
    south_courant = from_behind(courant[:, height - halo :], "tile", 1)
    north_courant = from_behind(courant[:, :halo], "tile", -1)

    def count_of(position):
        clamped = jnp.clip(position, 0, tiles - 1)
        return jnp.sum(jnp.where(tile_numbers == clamped, substeps, 0))

    counts = jnp.stack(
        [count_of(tile_position - 1), count_of(tile_position), count_of(tile_position + 1)]
    )
    counts_float = counts.astype(jnp.float32)
    steps = jnp.arange(ROUNDS)[:, None]
    fractions = jnp.where(steps < counts[None, :], 1.0 / counts_float[None, :], jnp.float32(0.0))
    first_row = jnp.where(tile_position > 0, jnp.float32(1.0), jnp.float32(0.0))
    scalars = jnp.concatenate([fractions.reshape(-1), first_row[None]])
    mixed = transport(
        scalars, by_row, south_rows, north_rows, courant, south_courant,
        north_courant, coefficient, jnp.transpose(emissions, (1, 0, 2)),
    )
    return jnp.transpose(mixed, (2, 1, 0, 3))


def solution(mesh):
    return jax.shard_map(
        shards,
        mesh=mesh,
        in_specs=(
            P("group", None, "tile", None),
            P("group", "tile", None),
            P("group", None, None, "tile", None),
            P("group", None, "tile", None),
            P(),
            P(),
        ),
        out_specs=P("group", None, "tile", None),
        check_vma=False,
    )
```

time: 166 us -> 108 us (0.65)
  the two profiles are of different devices: /device:TPU:88 before, /device:TPU:161 now
where the time goes in v3:
time: 108 us; the launch traced here: 106 us
  waiting for transfers between devices  51.8 us (48%)
  starting transfers between devices  21.7 us (20%)
  Pallas kernels  17.6 us (16%)
  local copies, waits for them, and re-layouts  8.88 us (8%)
  other arithmetic  5.32 us (5%)
    ppermute x4, waiting for transfers between devices, from_behind(): return lax.ppermute(value, axis, pairs)  34.1 us
    ppermute x4, waiting for transfers between devices, broadcast_from(): received = lax.ppermute(current, axis, pairs)  17.7 us
    pallas_call x1, Pallas kernels, transport(): pl.pallas_call(transport_kernel, grid=(levels,), out_shape=jax.ShapeDtype...  17.6 us
    ppermute x4, starting transfers between devices, from_behind(): return lax.ppermute(value, axis, pairs)  16 us
    ppermute x4, starting transfers between devices, broadcast_from(): received = lax.ppermute(current, axis, pairs)  5.71 us
    unnamed x24, local copies, waits for them, and re-layouts  3.29 us
    transpose x1, local copies, waits for them, and re-layouts, shards(): return jnp.transpose(mixed, (2, 1, 0, 3))  2.8 us
  transfers between devices with their start and end apart: 8, of which 4 were waited for; matrix products, arithmetic and copies ran while one was open for 8% of the time, Pallas kernels for 0%

profile of v3, /device:TPU:161, one launch (start us, length us, event | category | flops | bytes accessed | tf_op | source)
XLA Modules:
  0.0 106.1 jit_solution(2946986049214538706)
XLA Ops:
  0.0 1.1 %pad_maximum_fusion = f32[47,8,256]{2,1,0:T(8,128)S(1)} fusion(f32[15,8,256]{2,1,0:T(8,128)} %bitcast.18, f32[32,8,256]{2,1,0:T(8,128)} %bitcast.16), kind=kLoop, calls=%fused_computation.1 | loop fusion | flops 96256 | bytes 770048 | tf_op jit(solution)/shard_map/concatenate | solution.py:175
  1.1 0.8 collective-permute-start.2
  1.9 0.7 copy-done.10
  3.9 0.8 collective-permute-start.3
  4.7 9.8 %collective-permute-done.3 = f32[47,8,256]{2,1,0:T(8,128)S(1)} collective-permute-done((f32[47,8,256]{2,1,0:T(8,128)S(1)}, f32[47,8,256]{2,1,0:T(8,128)S(1)}, u32[]{:S(2)}, u32[]{:S(2)}) %collective-permute-start.3) | collective-permute-done | bytes 385056 | tf_op jit(solution)/shard_map/ppermute | solution.py:25
  14.6 1.3 %collective-permute-start.4 = (f32[47,8,256]{2,1,0:T(8,128)S(1)}, f32[47,8,256]{2,1,0:T(8,128)S(1)}, u32[]{:S(2)}, u32[]{:S(2)}) collective-permute-start(f32[47,8,256]{2,1,0:T(8,128)S(1)} %broadcast_select_fusion.1), channel_id=1, source_target_pairs={{0,4},{1,5},{2,6},{3,7},{4,0},{5,1},{6,2},{7,3},{8,12},{9,13},{10,... | collective-permute-start | bytes 1155080 | tf_op jit(solution)/shard_map/ppermute | solution.py:25
  16.5 7.8 %collective-permute-done.4 = f32[47,8,256]{2,1,0:T(8,128)S(1)} collective-permute-done((f32[47,8,256]{2,1,0:T(8,128)S(1)}, f32[47,8,256]{2,1,0:T(8,128)S(1)}, u32[]{:S(2)}, u32[]{:S(2)}) %collective-permute-start.4) | collective-permute-done | bytes 385056 | tf_op jit(solution)/shard_map/ppermute | solution.py:25
  24.4 2.8 %collective-permute-start.5 = (f32[47,8,256]{2,1,0:T(8,128)S(1)}, f32[47,8,256]{2,1,0:T(8,128)S(1)}, u32[]{:S(2)}, u32[]{:S(2)}) collective-permute-start(f32[47,8,256]{2,1,0:T(8,128)S(1)} %broadcast_select_fusion.2), channel_id=1, source_target_pairs={{0,8},{1,9},{2,10},{3,11},{4,12},{5,13},{6,14},{7,15},{8,0},{9,1},... | collective-permute-start | bytes 1155080 | tf_op jit(solution)/shard_map/ppermute | solution.py:25
  27.2 1.3 %fusion.5 = (f32[6,16,8,256]{3,2,1,0:T(8,128)}, f32[6,16,8,256]{3,2,1,0:T(8,128)}) fusion(f32[8,16,8,256]{3,2,1,0:T(8,128)S(1)} %bitcast.13), kind=kLoop, calls=%fused_computation.20 | loop fusion | bytes 3145728 | tf_op jit(solution)/shard_map/slice | solution.py:184
  28.5 4.6 %collective-permute-start.1 = (f32[6,16,8,256]{3,2,1,0:T(8,128)}, f32[6,16,8,256]{3,2,1,0:T(8,128)S(1)}, u32[]{:S(2)}, u32[]{:S(2)}) collective-permute-start(f32[6,16,8,256]{3,2,1,0:T(8,128)} %get-tuple-element.10), channel_id=1, source_target_pairs={{16,0},{32,16},{48,32},{64,48},{80,64},{96,80},{112,96},{128,112},... | collective-permute-start | bytes 2359304 | tf_op jit(solution)/shard_map/ppermute | solution.py:14
  33.1 1.9 %collective-permute-start = (f32[6,16,8,256]{3,2,1,0:T(8,128)}, f32[6,16,8,256]{3,2,1,0:T(8,128)S(1)}, u32[]{:S(2)}, u32[]{:S(2)}) collective-permute-start(f32[6,16,8,256]{3,2,1,0:T(8,128)} %get-tuple-element.11), channel_id=1, source_target_pairs={{0,16},{16,32},{32,48},{48,64},{64,80},{80,96},{96,112},{112,128},... | collective-permute-start | bytes 2359304 | tf_op jit(solution)/shard_map/ppermute | solution.py:14
  35.1 0.6 copy-done.9
  35.7 0.7 fusion.1
  36.5 2.0 %convert_divide_fusion = (f32[3]{0:T(128)S(1)}, s32[3]{0:T(128)S(1)}) fusion(s32[1]{0:T(128)} %bitcast.2, s32[1]{0:T(128)} %bitcast.1, s32[1]{0:T(128)} %bitcast), kind=kLoop, calls=%fused_computation.19 | loop fusion | flops 12 | bytes 36 | tf_op jit(solution)/shard_map/div | solution.py:197
  38.6 7.6 %collective-permute-start.7 = (f32[32,6,256]{2,1,0:T(8,128)S(1)}, f32[32,6,256]{2,1,0:T(8,128)S(1)}, u32[]{:S(2)}, u32[]{:S(2)}) collective-permute-start(f32[32,6,256]{2,1,0:T(8,128)S(1)} %get-tuple-element.12), channel_id=1, source_target_pairs={{16,0},{32,16},{48,32},{64,48},{80,64},{96,80},{112,96},{128,112},... | collective-permute-start | bytes 589832 | tf_op jit(solution)/shard_map/ppermute | solution.py:14
  46.2 1.9 %collective-permute-start.6 = (f32[32,6,256]{2,1,0:T(8,128)S(1)}, f32[32,6,256]{2,1,0:T(8,128)S(1)}, u32[]{:S(2)}, u32[]{:S(2)}) collective-permute-start(f32[32,6,256]{2,1,0:T(8,128)S(1)} %get-tuple-element.13), channel_id=1, source_target_pairs={{0,16},{16,32},{32,48},{48,64},{64,80},{80,96},{96,112},{112,128},... | collective-permute-start | bytes 589832 | tf_op jit(solution)/shard_map/ppermute | solution.py:14
  48.9 0.6 pad_maximum_fusion.1.scalars
  49.5 0.7 slice.31.coefficient
  50.2 0.7 slice.28.courant
  50.9 28.5 %collective-permute-done.south = f32[6,16,8,256]{3,2,1,0:T(8,128)S(1)} collective-permute-done((f32[6,16,8,256]{3,2,1,0:T(8,128)}, f32[6,16,8,256]{3,2,1,0:T(8,128)S(1)}, u32[]{:S(2)}, u32[]{:S(2)}) %collective-permute-start) | collective-permute-done | bytes 786464 | tf_op jit(solution)/shard_map/ppermute | solution.py:14
  79.4 5.6 %collective-permute-done.6.south_courant = f32[32,6,256]{2,1,0:T(8,128)S(1)} collective-permute-done((f32[32,6,256]{2,1,0:T(8,128)S(1)}, f32[32,6,256]{2,1,0:T(8,128)S(1)}, u32[]{:S(2)}, u32[]{:S(2)}) %collective-permute-start.6) | collective-permute-done | bytes 196640 | tf_op jit(solution)/shard_map/ppermute | solution.py:14
  85.0 0.7 copy-done.7
  85.8 17.6 %shard_map.64 = f32[8,16,8,256]{3,2,1,0:T(8,128)} custom-call(f32[19]{0:T(128)} %pad_maximum_fusion.1.scalars, f32[8,16,8,256]{3,2,1,0:T(8,128)} %bitcast.14, f32[6,16,8,256]{3,2,1,0:T(8,128)} %copy-done.4, f32[6,16,8,256]{3,2,1,0:T(8,128)} %copy-done.3, f32[32,8,256]{2,1,0:T(8,128)} %slice.28.courant, f32[32,6,256]{2,1,0:T(8,128)} %copy-done.7, ...), custom_call_target="tpu_custom_call" | custom-call | flops 35782656 | bytes 5505024 | tf_op jit(solution)/shard_map/pallas_call | solution.py:133
  103.3 2.8 %copy.12 = f32[8,16,8,256]{3,2,1,0:T(8,128)} copy(f32[8,16,8,256]{3,0,1,2:T(8,128)} %bitcast.15) | data formatting | bytes 2097152 | tf_op jit(solution)/shard_map/transpose | solution.py:204
  (33 shorter events, 2.3 us)
Async XLA Ops:
  0.0 3.8 %copy-start.2 = (f32[1,2,16,8,256]{4,3,2,1,0:T(8,128)S(1)}, f32[1,2,16,8,256]{4,3,2,1,0:T(8,128)}, u32[]{:S(2)}) copy-start(f32[1,2,16,8,256]{4,3,2,1,0:T(8,128)} %param.8) | copy-start | bytes 786436
  0.0 3.8 %copy-start.5 = (f32[1,15,8,256]{3,2,1,0:T(8,128)S(1)}, f32[1,15,8,256]{3,2,1,0:T(8,128)}, u32[]{:S(2)}) copy-start(f32[1,15,8,256]{3,2,1,0:T(8,128)} %param.9) | copy-start | bytes 368644
  1.1 2.7 %collective-permute-start.2 = (f32[47,8,256]{2,1,0:T(8,128)S(1)}, f32[47,8,256]{2,1,0:T(8,128)S(1)}, u32[]{:S(2)}, u32[]{:S(2)}) collective-permute-start(f32[47,8,256]{2,1,0:T(8,128)S(1)} %pad_maximum_fusion), channel_id=1, source_target_pairs={{0,1},{1,0},{2,3},{3,2},{4,5},{5,4},{6,7},{7,6},{8,9},{9,8},{10,11... | collective-permute-start | bytes 1155080 | tf_op jit(solution)/shard_map/ppermute | solution.py:25
  1.9 0.7 copy-start.10
  3.8 12.1 %copy-start.1 = (f32[8,16,8,256]{3,2,1,0:T(8,128)S(1)}, f32[8,16,8,256]{3,2,1,0:T(8,128)}, u32[]{:S(2)}) copy-start(f32[8,16,8,256]{3,2,1,0:T(8,128)} %param.6) | copy-start | bytes 3145732
  3.9 10.6 %collective-permute-start.3 = (f32[47,8,256]{2,1,0:T(8,128)S(1)}, f32[47,8,256]{2,1,0:T(8,128)S(1)}, u32[]{:S(2)}, u32[]{:S(2)}) collective-permute-start(f32[47,8,256]{2,1,0:T(8,128)S(1)} %broadcast_select_fusion), channel_id=1, source_target_pairs={{0,2},{1,3},{2,0},{3,1},{4,6},{5,7},{6,4},{7,5},{8,10},{9,11},{10,... | collective-permute-start | bytes 1155080 | tf_op jit(solution)/shard_map/ppermute | solution.py:25
  14.6 9.8 %collective-permute-start.4 = (f32[47,8,256]{2,1,0:T(8,128)S(1)}, f32[47,8,256]{2,1,0:T(8,128)S(1)}, u32[]{:S(2)}, u32[]{:S(2)}) collective-permute-start(f32[47,8,256]{2,1,0:T(8,128)S(1)} %broadcast_select_fusion.1), channel_id=1, source_target_pairs={{0,4},{1,5},{2,6},{3,7},{4,0},{5,1},{6,2},{7,3},{8,12},{9,13},{10,... | collective-permute-start | bytes 1155080 | tf_op jit(solution)/shard_map/ppermute | solution.py:25
  16.5 12.0 %copy-start = (f32[8,16,8,256]{3,0,1,2:T(8,128)}, f32[8,16,8,256]{3,0,1,2:T(8,128)S(1)}, u32[]{:S(2)}) copy-start(f32[8,16,8,256]{3,0,1,2:T(8,128)S(1)} %copy.15) | copy-start | bytes 3145732
  24.4 14.1 %collective-permute-start.5 = (f32[47,8,256]{2,1,0:T(8,128)S(1)}, f32[47,8,256]{2,1,0:T(8,128)S(1)}, u32[]{:S(2)}, u32[]{:S(2)}) collective-permute-start(f32[47,8,256]{2,1,0:T(8,128)S(1)} %broadcast_select_fusion.2), channel_id=1, source_target_pairs={{0,8},{1,9},{2,10},{3,11},{4,12},{5,13},{6,14},{7,15},{8,0},{9,1},... | collective-permute-start | bytes 1155080 | tf_op jit(solution)/shard_map/ppermute | solution.py:25
  28.5 22.4 %collective-permute-start.1 = (f32[6,16,8,256]{3,2,1,0:T(8,128)}, f32[6,16,8,256]{3,2,1,0:T(8,128)S(1)}, u32[]{:S(2)}, u32[]{:S(2)}) collective-permute-start(f32[6,16,8,256]{3,2,1,0:T(8,128)} %get-tuple-element.10), channel_id=1, source_target_pairs={{16,0},{32,16},{48,32},{64,48},{80,64},{96,80},{112,96},{128,112},... | collective-permute-start | bytes 2359304 | tf_op jit(solution)/shard_map/ppermute | solution.py:14
  33.1 46.3 %collective-permute-start = (f32[6,16,8,256]{3,2,1,0:T(8,128)}, f32[6,16,8,256]{3,2,1,0:T(8,128)S(1)}, u32[]{:S(2)}, u32[]{:S(2)}) collective-permute-start(f32[6,16,8,256]{3,2,1,0:T(8,128)} %get-tuple-element.11), channel_id=1, source_target_pairs={{0,16},{16,32},{32,48},{48,64},{64,80},{80,96},{96,112},{112,128},... | collective-permute-start | bytes 2359304 | tf_op jit(solution)/shard_map/ppermute | solution.py:14
  35.1 0.7 copy-start.9
  38.6 9.7 %copy-start.8 = (f32[8,8,256]{2,1,0:T(8,128)S(1)}, f32[8,8,256]{2,1,0:T(8,128)}, u32[]{:S(2)}) copy-start(f32[8,8,256]{2,1,0:T(8,128)} %param.7) | copy-start | bytes 196612
  38.6 40.8 %collective-permute-start.7 = (f32[32,6,256]{2,1,0:T(8,128)S(1)}, f32[32,6,256]{2,1,0:T(8,128)S(1)}, u32[]{:S(2)}, u32[]{:S(2)}) collective-permute-start(f32[32,6,256]{2,1,0:T(8,128)S(1)} %get-tuple-element.12), channel_id=1, source_target_pairs={{16,0},{32,16},{48,32},{64,48},{80,64},{96,80},{112,96},{128,112},... | collective-permute-start | bytes 589832 | tf_op jit(solution)/shard_map/ppermute | solution.py:14
  46.2 38.8 %collective-permute-start.6 = (f32[32,6,256]{2,1,0:T(8,128)S(1)}, f32[32,6,256]{2,1,0:T(8,128)S(1)}, u32[]{:S(2)}, u32[]{:S(2)}) collective-permute-start(f32[32,6,256]{2,1,0:T(8,128)S(1)} %get-tuple-element.13), channel_id=1, source_target_pairs={{0,16},{16,32},{32,48},{48,64},{64,80},{80,96},{96,112},{112,128},... | collective-permute-start | bytes 589832 | tf_op jit(solution)/shard_map/ppermute | solution.py:14
  50.9 34.1 %copy-start.3 = (f32[6,16,8,256]{3,2,1,0:T(8,128)}, f32[6,16,8,256]{3,2,1,0:T(8,128)S(1)}, u32[]{:S(2)}) copy-start(f32[6,16,8,256]{3,2,1,0:T(8,128)S(1)} %collective-permute-done.1.north) | copy-start | bytes 2359300
  79.4 5.6 %copy-start.4 = (f32[6,16,8,256]{3,2,1,0:T(8,128)}, f32[6,16,8,256]{3,2,1,0:T(8,128)S(1)}, u32[]{:S(2)}) copy-start(f32[6,16,8,256]{3,2,1,0:T(8,128)S(1)} %collective-permute-done.south) | copy-start | bytes 2359300
  79.4 5.6 %copy-start.6 = (f32[32,6,256]{2,1,0:T(8,128)}, f32[32,6,256]{2,1,0:T(8,128)S(1)}, u32[]{:S(2)}) copy-start(f32[32,6,256]{2,1,0:T(8,128)S(1)} %collective-permute-done.7.north_courant) | copy-start | bytes 589828
  85.0 0.7 copy-start.7

commit v4 on v3

--- a/solution.py
+++ b/solution.py
@@ -14,18 +14,91 @@
     return lax.ppermute(value, axis, pairs)
 
 
+def spread_kernel(data, out, *scratch):
+    bits = len(scratch) - 3
+    received = scratch[:bits]
+    send_sems, recv_sems, credits = scratch[bits:]
+    me = lax.axis_index("group")
+    tile = lax.axis_index("tile")
+
+    def partner(bit):
+        return me + (1 << bit) * (1 - 2 * ((me // (1 << bit)) % 2))
+
+    barrier = pltpu.get_barrier_semaphore()
+    for bit in range(bits):
+        pl.semaphore_signal(
+            barrier, 1, device_id=(tile, partner(bit)), device_id_type=pl.DeviceIdType.MESH
+        )
+    pl.semaphore_wait(barrier, bits)
+    out[...] = data[...]
+    start = 0
+    size = out.shape[0]
+    for bit in range(bits):
+        half = size // 2
+        side = (me // (1 << bit)) % 2
+        keep = start + side * half
+        give = start + (1 - side) * half
+        copy = pltpu.make_async_remote_copy(
+            src_ref=out.at[pl.ds(give, half)],
+            dst_ref=received[bit],
+            send_sem=send_sems.at[bit],
+            recv_sem=recv_sems.at[bit],
+            device_id=(tile, partner(bit)),
+            device_id_type=pl.DeviceIdType.MESH,
+        )
+        copy.start()
+        copy.wait()
+        pl.semaphore_signal(
+            credits.at[bit], 1, device_id=(tile, partner(bit)),
+            device_id_type=pl.DeviceIdType.MESH,
+        )
+        out[pl.ds(keep, half)] = out[pl.ds(keep, half)] + received[bit][...]
+        start = keep
+        size = half
+    for step, bit in enumerate(reversed(range(bits))):
+        side = (me // (1 << bit)) % 2
+        pl.semaphore_wait(credits.at[bit], 1)
+        copy = pltpu.make_async_remote_copy(
+            src_ref=out.at[pl.ds(start, size)],
+            dst_ref=out.at[pl.ds(start, size)],
+            send_sem=send_sems.at[bits + step],
+            recv_sem=recv_sems.at[bits + step],
+            device_id=(tile, partner(bit)),
+            device_id_type=pl.DeviceIdType.MESH,
+        )
+        copy.start()
+        copy.wait()
+        start = start - side * size
+        size = 2 * size
+
+
 def broadcast_from(value, axis, root):
     count = lax.axis_size(axis)
     assert count & (count - 1) == 0
-    distance = lax.axis_index(axis) ^ root
-    current = value
-    bit = 0
-    while (1 << bit) < count:
-        pairs = [(i, i ^ (1 << bit)) for i in range(count)]
-        received = lax.ppermute(current, axis, pairs)
-        current = jnp.where((distance >> bit) == 1, received, current)
-        bit += 1
-    return current
+    bits = count.bit_length() - 1
+    planes = -(-value.shape[0] // count) * count
+    padded = jnp.concatenate(
+        [value, jnp.zeros((planes - value.shape[0],) + value.shape[1:], value.dtype)]
+    )
+    masked = jnp.where(lax.axis_index(axis) == root, padded, jnp.zeros_like(padded))
+    vmem = pl.BlockSpec(memory_space=pltpu.VMEM)
+    spread = pl.pallas_call(
+        spread_kernel,
+        out_shape=jax.ShapeDtypeStruct(padded.shape, padded.dtype),
+        in_specs=[vmem],
+        out_specs=vmem,
+        scratch_shapes=[
+            pltpu.VMEM((planes >> (bit + 1),) + value.shape[1:], value.dtype)
+            for bit in range(bits)
+        ]
+        + [
+            pltpu.SemaphoreType.DMA((2 * bits,)),
+            pltpu.SemaphoreType.DMA((2 * bits,)),
+            pltpu.SemaphoreType.REGULAR((bits,)),
+        ],
+        compiler_params=pltpu.CompilerParams(collective_id=0, has_side_effects=True),
+    )(masked)
+    return spread[: value.shape[0]]
 
 
 def transport_kernel(

time: 108 us -> 119 us (1.10)
  Pallas kernels: 17.6 us -> 72.8 us
  waiting for transfers between devices: 51.8 us -> 10.7 us
  starting transfers between devices: 21.7 us -> 15.2 us
  local copies, waits for them, and re-layouts: 8.88 us -> 13 us
    pallas_call x0 -> x1, Pallas kernels: none -> 55.2 us  [broadcast_from(): pl.pallas_call(spread_kernel, out_shape=jax.ShapeDtypeStruct(padded.shape...]
    ppermute x4, waiting for transfers between devices: 34.1 us -> 10.7 us  [from_behind(): return lax.ppermute(value, axis, pairs)]
    ppermute x4 -> x0, waiting for transfers between devices: 17.7 us -> none  [broadcast_from(): received = lax.ppermute(current, axis, pairs)]
    ppermute x4 -> x0, starting transfers between devices: 5.71 us -> none  [broadcast_from(): received = lax.ppermute(current, axis, pairs)]
    unnamed x24 -> x18, local copies, waits for them, and re-layouts: 3.29 us -> 6.58 us
    slice x1, local copies, waits for them, and re-layouts: 0.04 us -> 1.93 us  [shards(): north_courant = from_behind(courant[:, :halo], 'tile', -1)]
  transfers between devices with their start and end apart: 8 -> 4, of which waited for: 4 -> 1; matrix products, arithmetic and copies ran while one was open for 8% -> 8% of each run, Pallas kernels for 0% -> 47%
where the time goes in v4:
time: 119 us; the launch traced here: 117 us
  Pallas kernels  72.8 us (61%)
  starting transfers between devices  15.2 us (13%)
  local copies, waits for them, and re-layouts  13 us (11%)
  waiting for transfers between devices  10.7 us (9%)
  other arithmetic  4.8 us (4%)
    pallas_call x1, Pallas kernels, broadcast_from(): pl.pallas_call(spread_kernel, out_shape=jax.ShapeDtypeStruct(padded.shape...  55.2 us
    pallas_call x1, Pallas kernels, transport(): pl.pallas_call(transport_kernel, grid=(levels,), out_shape=jax.ShapeDtype...  17.6 us
    ppermute x4, starting transfers between devices, from_behind(): return lax.ppermute(value, axis, pairs)  15.2 us
    ppermute x4, waiting for transfers between devices, from_behind(): return lax.ppermute(value, axis, pairs)  10.7 us
    unnamed x18, local copies, waits for them, and re-layouts  6.58 us
    transpose x1, local copies, waits for them, and re-layouts, shards(): return jnp.transpose(mixed, (2, 1, 0, 3))  2.8 us
  transfers between devices with their start and end apart: 4, of which 1 were waited for; matrix products, arithmetic and copies ran while one was open for 8% of the time, Pallas kernels for 47%

profile of v4, /device:TPU:161, one launch (start us, length us, event | category | flops | bytes accessed | tf_op | source)
XLA Modules:
  0.0 117.2 jit_solution(10400008821056383013)
XLA Ops:
  0.0 1.8 %copy.15 = f32[8,16,8,256]{3,0,1,2:T(8,128)S(1)} copy(f32[8,16,8,256]{3,2,1,0:T(8,128)} %param.6) | data formatting | bytes 2097152 | tf_op args[0]
  1.9 0.1 fusion.5
  2.0 0.8 copy-done
  2.8 4.6 %collective-permute-start.1 = (f32[6,16,8,256]{3,2,1,0:T(8,128)S(1)}, f32[6,16,8,256]{3,2,1,0:T(8,128)S(1)}, u32[]{:S(2)}, u32[]{:S(2)}) collective-permute-start(f32[6,16,8,256]{3,2,1,0:T(8,128)S(1)} %get-tuple-element.10), channel_id=1, source_target_pairs={{16,0},{32,16},{48,32},{64,48},{80,64},{96,80},{112,96},{128,112},... | collective-permute-start | bytes 2359304 | tf_op jit(solution)/shard_map/ppermute | solution.py:14
  7.4 1.9 %collective-permute-start = (f32[6,16,8,256]{3,2,1,0:T(8,128)S(1)}, f32[6,16,8,256]{3,2,1,0:T(8,128)S(1)}, u32[]{:S(2)}, u32[]{:S(2)}) collective-permute-start(f32[6,16,8,256]{3,2,1,0:T(8,128)S(1)} %get-tuple-element.11), channel_id=1, source_target_pairs={{0,16},{16,32},{32,48},{48,64},{64,80},{80,96},{96,112},{112,128},... | collective-permute-start | bytes 2359304 | tf_op jit(solution)/shard_map/ppermute | solution.py:14
  9.4 0.6 copy-done.7
  10.0 0.6 fusion.4
  11.4 0.9 maximum_select_fusion.data
  12.3 55.2 %shard_map.64 = f32[48,8,256]{2,1,0:T(8,128)} custom-call(f32[48,8,256]{2,1,0:T(8,128)} %maximum_select_fusion.data), custom_call_target="tpu_custom_call" | custom-call | tf_op jit(solution)/shard_map/pallas_call | solution.py:85
  67.5 1.9 %fusion.6 = (f32[32,6,256]{2,1,0:T(8,128)}, f32[32,6,256]{2,1,0:T(8,128)}) fusion(f32[48,8,256]{2,1,0:T(8,128)} %shard_map.64), kind=kLoop, calls=%fused_computation.17 | loop fusion | bytes 786432 | tf_op jit(solution)/shard_map/slice | solution.py:259
  69.4 6.7 %collective-permute-start.3 = (f32[32,6,256]{2,1,0:T(8,128)}, f32[32,6,256]{2,1,0:T(8,128)}, u32[]{:S(2)}, u32[]{:S(2)}) collective-permute-start(f32[32,6,256]{2,1,0:T(8,128)} %get-tuple-element.12), channel_id=1, source_target_pairs={{16,0},{32,16},{48,32},{64,48},{80,64},{96,80},{112,96},{128,112},... | collective-permute-start | bytes 589832 | tf_op jit(solution)/shard_map/ppermute | solution.py:14
  76.2 1.9 %collective-permute-start.2 = (f32[32,6,256]{2,1,0:T(8,128)}, f32[32,6,256]{2,1,0:T(8,128)}, u32[]{:S(2)}, u32[]{:S(2)}) collective-permute-start(f32[32,6,256]{2,1,0:T(8,128)} %get-tuple-element.13), channel_id=1, source_target_pairs={{0,16},{16,32},{32,48},{48,64},{64,80},{80,96},{96,112},{112,128},... | collective-permute-start | bytes 589832 | tf_op jit(solution)/shard_map/ppermute | solution.py:14
  78.1 0.6 copy-done.6
  78.8 0.7 fusion.1
  79.5 1.9 %convert_divide_fusion = (f32[3]{0:T(128)S(1)}, s32[3]{0:T(128)S(1)}) fusion(s32[1]{0:T(128)} %bitcast.2, s32[1]{0:T(128)} %bitcast.1, s32[1]{0:T(128)} %bitcast), kind=kLoop, calls=%fused_computation.15 | loop fusion | flops 12 | bytes 36 | tf_op jit(solution)/shard_map/div | solution.py:270
  81.4 0.7 slice.28.coefficient
  82.0 0.7 slice.25.courant
  82.8 1.5 %copy.16 = f32[8,8,256]{2,0,1:T(8,128)} copy(f32[8,8,256]{2,1,0:T(8,128)} %param.7) | data formatting | bytes 131072 | tf_op args[1]
  84.3 0.7 pad_maximum_fusion.scalars
  85.0 10.7 %collective-permute-done.2.south_courant = f32[32,6,256]{2,1,0:T(8,128)} collective-permute-done((f32[32,6,256]{2,1,0:T(8,128)}, f32[32,6,256]{2,1,0:T(8,128)}, u32[]{:S(2)}, u32[]{:S(2)}) %collective-permute-start.2) | collective-permute-done | bytes 196640 | tf_op jit(solution)/shard_map/ppermute | solution.py:14
  95.7 0.9 copy-done.2
  96.5 0.3 copy-done.3
  96.8 17.6 %shard_map.65 = f32[8,16,8,256]{3,2,1,0:T(8,128)} custom-call(f32[19]{0:T(128)} %pad_maximum_fusion.scalars, f32[8,16,8,256]{3,2,1,0:T(8,128)} %bitcast.15, f32[6,16,8,256]{3,2,1,0:T(8,128)} %copy-done.3, f32[6,16,8,256]{3,2,1,0:T(8,128)} %copy-done.2, f32[32,8,256]{2,1,0:T(8,128)} %slice.25.courant, f32[32,6,256]{2,1,0:T(8,128)} %collective-permute-done.2.south_courant, ...), custom_call_target="tpu_custom_call" | custom-call | flops 35782656 | bytes 5505024 | tf_op jit(solution)/shard_map/pallas_call | solution.py:206
  114.4 2.8 %copy.12 = f32[8,16,8,256]{3,2,1,0:T(8,128)} copy(f32[8,16,8,256]{3,0,1,2:T(8,128)} %bitcast.16) | data formatting | bytes 2097152 | tf_op jit(solution)/shard_map/transpose | solution.py:277
  (17 shorter events, 0.2 us)
Async XLA Ops:
  1.8 1.0 copy-start
  1.9 9.5 %copy-start.4 = (f32[1,2,16,8,256]{4,3,2,1,0:T(8,128)S(1)}, f32[1,2,16,8,256]{4,3,2,1,0:T(8,128)}, u32[]{:S(2)}) copy-start(f32[1,2,16,8,256]{4,3,2,1,0:T(8,128)} %param.8) | copy-start | bytes 786436
  1.9 9.5 %copy-start.5 = (f32[1,15,8,256]{3,2,1,0:T(8,128)S(1)}, f32[1,15,8,256]{3,2,1,0:T(8,128)}, u32[]{:S(2)}) copy-start(f32[1,15,8,256]{3,2,1,0:T(8,128)} %param.9) | copy-start | bytes 368644
  2.8 92.8 %collective-permute-start.1 = (f32[6,16,8,256]{3,2,1,0:T(8,128)S(1)}, f32[6,16,8,256]{3,2,1,0:T(8,128)S(1)}, u32[]{:S(2)}, u32[]{:S(2)}) collective-permute-start(f32[6,16,8,256]{3,2,1,0:T(8,128)S(1)} %get-tuple-element.10), channel_id=1, source_target_pairs={{16,0},{32,16},{48,32},{64,48},{80,64},{96,80},{112,96},{128,112},... | collective-permute-start | bytes 2359304 | tf_op jit(solution)/shard_map/ppermute | solution.py:14
  7.4 88.2 %collective-permute-start = (f32[6,16,8,256]{3,2,1,0:T(8,128)S(1)}, f32[6,16,8,256]{3,2,1,0:T(8,128)S(1)}, u32[]{:S(2)}, u32[]{:S(2)}) collective-permute-start(f32[6,16,8,256]{3,2,1,0:T(8,128)S(1)} %get-tuple-element.11), channel_id=1, source_target_pairs={{0,16},{16,32},{32,48},{48,64},{64,80},{80,96},{96,112},{112,128},... | collective-permute-start | bytes 2359304 | tf_op jit(solution)/shard_map/ppermute | solution.py:14
  9.4 0.7 copy-start.7
  67.5 13.9 %copy-start.1 = (f32[48,8,256]{2,1,0:T(8,128)S(1)}, f32[48,8,256]{2,1,0:T(8,128)}, u32[]{:S(2)}) copy-start(f32[48,8,256]{2,1,0:T(8,128)} %shard_map.64) | copy-start | bytes 1179652
  69.4 15.6 %collective-permute-start.3 = (f32[32,6,256]{2,1,0:T(8,128)}, f32[32,6,256]{2,1,0:T(8,128)}, u32[]{:S(2)}, u32[]{:S(2)}) collective-permute-start(f32[32,6,256]{2,1,0:T(8,128)} %get-tuple-element.12), channel_id=1, source_target_pairs={{16,0},{32,16},{48,32},{64,48},{80,64},{96,80},{112,96},{128,112},... | collective-permute-start | bytes 589832 | tf_op jit(solution)/shard_map/ppermute | solution.py:14
  76.2 19.5 %collective-permute-start.2 = (f32[32,6,256]{2,1,0:T(8,128)}, f32[32,6,256]{2,1,0:T(8,128)}, u32[]{:S(2)}, u32[]{:S(2)}) collective-permute-start(f32[32,6,256]{2,1,0:T(8,128)} %get-tuple-element.13), channel_id=1, source_target_pairs={{0,16},{16,32},{32,48},{48,64},{64,80},{80,96},{96,112},{112,128},... | collective-permute-start | bytes 589832 | tf_op jit(solution)/shard_map/ppermute | solution.py:14
  78.1 0.7 copy-start.6
  95.7 0.9 copy-start.2
  95.7 1.2 copy-start.3

commit v5 on v3

--- a/solution.py
+++ b/solution.py
@@ -16,16 +16,34 @@
 
 def broadcast_from(value, axis, root):
     count = lax.axis_size(axis)
-    assert count & (count - 1) == 0
-    distance = lax.axis_index(axis) ^ root
-    current = value
-    bit = 0
+    assert count & (count - 1) == 0 and count >= 2
+    position = lax.axis_index(axis)
+    distance = position ^ root
+    core = position % 2
+    half = -(-value.shape[0] // 2)
+    padded = jnp.concatenate(
+        [value, jnp.zeros((2 * half - value.shape[0],) + value.shape[1:], value.dtype)]
+    )
+    low, high = padded[:half], padded[half:]
+    mine = jnp.where(core == 0, low, high)
+    theirs = jnp.where(core == 0, high, low)
+
+    def swap(current, bit):
+        pairs = [(i, i ^ (1 << bit)) for i in range(count)]
+        return lax.ppermute(current, axis, pairs)
+
+    current = jnp.where(distance == 1, swap(theirs, 0), mine)
+    bit = 1
     while (1 << bit) < count:
-        pairs = [(i, i ^ (1 << bit)) for i in range(count)]
-        received = lax.ppermute(current, axis, pairs)
-        current = jnp.where((distance >> bit) == 1, received, current)
+        current = jnp.where((distance >> bit) == 1, swap(current, bit), current)
         bit += 1
-    return current
+    other = swap(current, 0)
+    whole = jnp.where(
+        core == 0,
+        jnp.concatenate([current, other]),
+        jnp.concatenate([other, current]),
+    )
+    return whole[: value.shape[0]]
 
 
 def transport_kernel(

time: 108 us -> 98.2 us (0.909)
  the two profiles are of different devices: /device:TPU:161 before, /device:TPU:192 now
where the time goes in v5:
time: 98.2 us; the launch traced here: 97.5 us
  waiting for transfers between devices  42.2 us (43%)
  starting transfers between devices  22.5 us (23%)
  Pallas kernels  17.6 us (18%)
  local copies, waits for them, and re-layouts  7.51 us (8%)
  other arithmetic  6.91 us (7%)
    ppermute x4, waiting for transfers between devices, from_behind(): return lax.ppermute(value, axis, pairs)  31.7 us
    pallas_call x1, Pallas kernels, transport(): pl.pallas_call(transport_kernel, grid=(levels,), out_shape=jax.ShapeDtype...  17.6 us
    ppermute x4, starting transfers between devices, from_behind(): return lax.ppermute(value, axis, pairs)  16.6 us
    ppermute x5, waiting for transfers between devices, swap(): return lax.ppermute(current, axis, pairs)  10.5 us
    ppermute x5, starting transfers between devices, swap(): return lax.ppermute(current, axis, pairs)  5.91 us
    transpose x1, local copies, waits for them, and re-layouts, shards(): return jnp.transpose(mixed, (2, 1, 0, 3))  2.8 us
    unnamed x18, local copies, waits for them, and re-layouts  2.13 us
  transfers between devices with their start and end apart: 9, of which 6 were waited for; matrix products, arithmetic and copies ran while one was open for 10% of the time, Pallas kernels for 0%

profile of v5, /device:TPU:192, one launch (start us, length us, event | category | flops | bytes accessed | tf_op | source)
XLA Modules:
  0.0 97.5 jit_solution(11634952336186235928)
XLA Ops:
  0.2 1.2 %slice_select_fusion = f32[24,8,256]{2,1,0:T(8,128)S(1)} fusion(f32[32,8,256]{2,1,0:T(8,128)} %bitcast.17, pred[]{:T(512)S(6)} %eq.49, f32[24]{0:T(128)S(1)} %slice.39, f32[15,8,256]{2,1,0:T(8,128)} %bitcast.19), kind=kLoop, calls=%fused_computation.5 | loop fusion | flops 147456 | bytes 778337 | tf_op jit(solution)/shard_map/jit(_where)/select_n | solution.py:29
  1.5 0.6 fusion.5
  3.0 1.1 %collective-permute-start.3 = (f32[24,8,256]{2,1,0:T(8,128)S(1)}, f32[24,8,256]{2,1,0:T(8,128)S(1)}, u32[]{:S(2)}, u32[]{:S(2)}) collective-permute-start(f32[24,8,256]{2,1,0:T(8,128)S(1)} %select_select_fusion), channel_id=1, source_target_pairs={{0,2},{1,3},{2,0},{3,1},{4,6},{5,7},{6,4},{7,5},{8,10},{9,11},{10,... | collective-permute-start | bytes 589832 | tf_op jit(solution)/shard_map/ppermute | solution.py:33
  4.2 6.2 %collective-permute-done.3 = f32[24,8,256]{2,1,0:T(8,128)S(1)} collective-permute-done((f32[24,8,256]{2,1,0:T(8,128)S(1)}, f32[24,8,256]{2,1,0:T(8,128)S(1)}, u32[]{:S(2)}, u32[]{:S(2)}) %collective-permute-start.3) | collective-permute-done | bytes 196640 | tf_op jit(solution)/shard_map/ppermute | solution.py:33
  10.3 1.6 %collective-permute-start.4 = (f32[24,8,256]{2,1,0:T(8,128)S(1)}, f32[24,8,256]{2,1,0:T(8,128)S(1)}, u32[]{:S(2)}, u32[]{:S(2)}) collective-permute-start(f32[24,8,256]{2,1,0:T(8,128)S(1)} %broadcast_select_fusion), channel_id=1, source_target_pairs={{0,4},{1,5},{2,6},{3,7},{4,0},{5,1},{6,2},{7,3},{8,12},{9,13},{10,... | collective-permute-start | bytes 589832 | tf_op jit(solution)/shard_map/ppermute | solution.py:33
  12.5 4.2 %collective-permute-done.4 = f32[24,8,256]{2,1,0:T(8,128)S(1)} collective-permute-done((f32[24,8,256]{2,1,0:T(8,128)S(1)}, f32[24,8,256]{2,1,0:T(8,128)S(1)}, u32[]{:S(2)}, u32[]{:S(2)}) %collective-permute-start.4) | collective-permute-done | bytes 196640 | tf_op jit(solution)/shard_map/ppermute | solution.py:33
  16.8 0.7 broadcast_select_fusion.1
  17.5 3.0 %collective-permute-start.5 = (f32[24,8,256]{2,1,0:T(8,128)}, f32[24,8,256]{2,1,0:T(8,128)}, u32[]{:S(2)}, u32[]{:S(2)}) collective-permute-start(f32[24,8,256]{2,1,0:T(8,128)} %broadcast_select_fusion.1), channel_id=1, source_target_pairs={{0,8},{1,9},{2,10},{3,11},{4,12},{5,13},{6,14},{7,15},{8,0},{9,1},... | collective-permute-start | bytes 589832 | tf_op jit(solution)/shard_map/ppermute | solution.py:33
  20.7 5.8 %collective-permute-start.1 = (f32[6,16,8,256]{3,2,1,0:T(8,128)S(1)}, f32[6,16,8,256]{3,2,1,0:T(8,128)S(1)}, u32[]{:S(2)}, u32[]{:S(2)}) collective-permute-start(f32[6,16,8,256]{3,2,1,0:T(8,128)S(1)} %get-tuple-element.10), channel_id=1, source_target_pairs={{16,0},{32,16},{48,32},{64,48},{80,64},{96,80},{112,96},{128,112},... | collective-permute-start | bytes 2359304 | tf_op jit(solution)/shard_map/ppermute | solution.py:14
  26.5 1.9 %collective-permute-start = (f32[6,16,8,256]{3,2,1,0:T(8,128)S(1)}, f32[6,16,8,256]{3,2,1,0:T(8,128)S(1)}, u32[]{:S(2)}, u32[]{:S(2)}) collective-permute-start(f32[6,16,8,256]{3,2,1,0:T(8,128)S(1)} %get-tuple-element.11), channel_id=1, source_target_pairs={{0,16},{16,32},{32,48},{48,64},{64,80},{80,96},{96,112},{112,128},... | collective-permute-start | bytes 2359304 | tf_op jit(solution)/shard_map/ppermute | solution.py:14
  28.5 1.0 broadcast_select_fusion.2
  29.5 0.7 fusion.2
  30.3 2.0 %convert_divide_fusion = (f32[3]{0:T(128)S(1)}, s32[3]{0:T(128)S(1)}) fusion(s32[1]{0:T(128)} %bitcast.2, s32[1]{0:T(128)} %bitcast.1, s32[1]{0:T(128)} %bitcast), kind=kLoop, calls=%fused_computation.22 | loop fusion | flops 12 | bytes 36 | tf_op jit(solution)/shard_map/div | solution.py:215
  32.3 0.8 fusion.7
  33.1 6.9 %collective-permute-start.8 = (f32[32,6,256]{2,1,0:T(8,128)}, f32[32,6,256]{2,1,0:T(8,128)}, u32[]{:S(2)}, u32[]{:S(2)}) collective-permute-start(f32[32,6,256]{2,1,0:T(8,128)} %get-tuple-element.12), channel_id=1, source_target_pairs={{16,0},{32,16},{48,32},{64,48},{80,64},{96,80},{112,96},{128,112},... | collective-permute-start | bytes 589832 | tf_op jit(solution)/shard_map/ppermute | solution.py:14
  40.0 1.9 %collective-permute-start.7 = (f32[32,6,256]{2,1,0:T(8,128)}, f32[32,6,256]{2,1,0:T(8,128)}, u32[]{:S(2)}, u32[]{:S(2)}) collective-permute-start(f32[32,6,256]{2,1,0:T(8,128)} %get-tuple-element.13), channel_id=1, source_target_pairs={{0,16},{16,32},{32,48},{48,64},{64,80},{80,96},{96,112},{112,128},... | collective-permute-start | bytes 589832 | tf_op jit(solution)/shard_map/ppermute | solution.py:14
  42.1 1.5 %copy.16 = f32[8,8,256]{2,0,1:T(8,128)} copy(f32[8,8,256]{2,1,0:T(8,128)} %param.7) | data formatting | bytes 131072 | tf_op args[1]
  44.1 0.6 slice.44.coefficient
  44.7 0.7 slice.41.courant
  45.5 19.4 %collective-permute-done.1.north = f32[6,16,8,256]{3,2,1,0:T(8,128)S(1)} collective-permute-done((f32[6,16,8,256]{3,2,1,0:T(8,128)S(1)}, f32[6,16,8,256]{3,2,1,0:T(8,128)S(1)}, u32[]{:S(2)}, u32[]{:S(2)}) %collective-permute-start.1) | collective-permute-done | bytes 786464 | tf_op jit(solution)/shard_map/ppermute | solution.py:14
  64.9 5.1 %collective-permute-done.8.north_courant = f32[32,6,256]{2,1,0:T(8,128)} collective-permute-done((f32[32,6,256]{2,1,0:T(8,128)}, f32[32,6,256]{2,1,0:T(8,128)}, u32[]{:S(2)}, u32[]{:S(2)}) %collective-permute-start.8) | collective-permute-done | bytes 196640 | tf_op jit(solution)/shard_map/ppermute | solution.py:14
  70.0 7.1 %collective-permute-done.7.south_courant = f32[32,6,256]{2,1,0:T(8,128)} collective-permute-done((f32[32,6,256]{2,1,0:T(8,128)}, f32[32,6,256]{2,1,0:T(8,128)}, u32[]{:S(2)}, u32[]{:S(2)}) %collective-permute-start.7) | collective-permute-done | bytes 196640 | tf_op jit(solution)/shard_map/ppermute | solution.py:14
  77.1 17.6 %shard_map.64 = f32[8,16,8,256]{3,2,1,0:T(8,128)} custom-call(f32[19]{0:T(128)} %pad_maximum_fusion.1.scalars, f32[8,16,8,256]{3,2,1,0:T(8,128)} %bitcast.15, f32[6,16,8,256]{3,2,1,0:T(8,128)} %copy-done.4, f32[6,16,8,256]{3,2,1,0:T(8,128)} %copy-done.3, f32[32,8,256]{2,1,0:T(8,128)} %slice.41.courant, f32[32,6,256]{2,1,0:T(8,128)} %collective-permute-done.7.south_courant, ...), custom_call_target="tpu_custom_call" | custom-call | flops 35782656 | bytes 5505024 | tf_op jit(solution)/shard_map/pallas_call | solution.py:151
  94.7 2.8 %copy.12 = f32[8,16,8,256]{3,2,1,0:T(8,128)} copy(f32[8,16,8,256]{3,0,1,2:T(8,128)} %bitcast.16) | data formatting | bytes 2097152 | tf_op jit(solution)/shard_map/transpose | solution.py:222
  (32 shorter events, 2.1 us)
Async XLA Ops:
  0.0 1.5 %copy-start.7 = (s32[16]{0:T(128)S(1)}, s32[16]{0:T(128)}, u32[]{:S(2)}) copy-start(s32[16]{0:T(128)} %param.11) | copy-start | bytes 196
  0.0 2.9 %copy-start.5 = (f32[1,15,8,256]{3,2,1,0:T(8,128)S(1)}, f32[1,15,8,256]{3,2,1,0:T(8,128)}, u32[]{:S(2)}) copy-start(f32[1,15,8,256]{3,2,1,0:T(8,128)} %param.9) | copy-start | bytes 368644
  0.2 2.8 %copy-start.1 = (f32[1,2,16,8,256]{4,3,2,1,0:T(8,128)S(1)}, f32[1,2,16,8,256]{4,3,2,1,0:T(8,128)}, u32[]{:S(2)}) copy-start(f32[1,2,16,8,256]{4,3,2,1,0:T(8,128)} %param.8) | copy-start | bytes 786436
  0.2 11.8 %copy-start.2 = (f32[8,16,8,256]{3,2,1,0:T(8,128)S(1)}, f32[8,16,8,256]{3,2,1,0:T(8,128)}, u32[]{:S(2)}) copy-start(f32[8,16,8,256]{3,2,1,0:T(8,128)} %param.6) | copy-start | bytes 3145732
  1.4 1.5 %collective-permute-start.2 = (f32[24,8,256]{2,1,0:T(8,128)S(1)}, f32[24,8,256]{2,1,0:T(8,128)S(1)}, u32[]{:S(2)}, u32[]{:S(2)}) collective-permute-start(f32[24,8,256]{2,1,0:T(8,128)S(1)} %slice_select_fusion), channel_id=1, source_target_pairs={{0,1},{1,0},{2,3},{3,2},{4,5},{5,4},{6,7},{7,6},{8,9},{9,8},{10,11... | collective-permute-start | bytes 589832 | tf_op jit(solution)/shard_map/ppermute | solution.py:33
  3.0 7.3 %collective-permute-start.3 = (f32[24,8,256]{2,1,0:T(8,128)S(1)}, f32[24,8,256]{2,1,0:T(8,128)S(1)}, u32[]{:S(2)}, u32[]{:S(2)}) collective-permute-start(f32[24,8,256]{2,1,0:T(8,128)S(1)} %select_select_fusion), channel_id=1, source_target_pairs={{0,2},{1,3},{2,0},{3,1},{4,6},{5,7},{6,4},{7,5},{8,10},{9,11},{10,... | collective-permute-start | bytes 589832 | tf_op jit(solution)/shard_map/ppermute | solution.py:33
  10.3 6.5 %collective-permute-start.4 = (f32[24,8,256]{2,1,0:T(8,128)S(1)}, f32[24,8,256]{2,1,0:T(8,128)S(1)}, u32[]{:S(2)}, u32[]{:S(2)}) collective-permute-start(f32[24,8,256]{2,1,0:T(8,128)S(1)} %broadcast_select_fusion), channel_id=1, source_target_pairs={{0,4},{1,5},{2,6},{3,7},{4,0},{5,1},{6,2},{7,3},{8,12},{9,13},{10,... | collective-permute-start | bytes 589832 | tf_op jit(solution)/shard_map/ppermute | solution.py:33
  12.5 8.1 %copy-start = (f32[8,16,8,256]{3,0,1,2:T(8,128)}, f32[8,16,8,256]{3,0,1,2:T(8,128)S(1)}, u32[]{:S(2)}) copy-start(f32[8,16,8,256]{3,0,1,2:T(8,128)S(1)} %copy.15) | copy-start | bytes 3145732
  17.5 11.0 %collective-permute-start.5 = (f32[24,8,256]{2,1,0:T(8,128)}, f32[24,8,256]{2,1,0:T(8,128)}, u32[]{:S(2)}, u32[]{:S(2)}) collective-permute-start(f32[24,8,256]{2,1,0:T(8,128)} %broadcast_select_fusion.1), channel_id=1, source_target_pairs={{0,8},{1,9},{2,10},{3,11},{4,12},{5,13},{6,14},{7,15},{8,0},{9,1},... | collective-permute-start | bytes 589832 | tf_op jit(solution)/shard_map/ppermute | solution.py:33
  20.7 44.2 %collective-permute-start.1 = (f32[6,16,8,256]{3,2,1,0:T(8,128)S(1)}, f32[6,16,8,256]{3,2,1,0:T(8,128)S(1)}, u32[]{:S(2)}, u32[]{:S(2)}) collective-permute-start(f32[6,16,8,256]{3,2,1,0:T(8,128)S(1)} %get-tuple-element.10), channel_id=1, source_target_pairs={{16,0},{32,16},{48,32},{64,48},{80,64},{96,80},{112,96},{128,112},... | collective-permute-start | bytes 2359304 | tf_op jit(solution)/shard_map/ppermute | solution.py:14
  26.5 38.4 %collective-permute-start = (f32[6,16,8,256]{3,2,1,0:T(8,128)S(1)}, f32[6,16,8,256]{3,2,1,0:T(8,128)S(1)}, u32[]{:S(2)}, u32[]{:S(2)}) collective-permute-start(f32[6,16,8,256]{3,2,1,0:T(8,128)S(1)} %get-tuple-element.11), channel_id=1, source_target_pairs={{0,16},{16,32},{32,48},{48,64},{64,80},{80,96},{96,112},{112,128},... | collective-permute-start | bytes 2359304 | tf_op jit(solution)/shard_map/ppermute | solution.py:14
  28.4 1.1 %copy-start.6 = (s32[16]{0:T(128)S(1)}, s32[16]{0:T(128)}, u32[]{:S(2)}) copy-start(s32[16]{0:T(128)} %param.10) | copy-start | bytes 196
  29.4 2.8 %collective-permute-start.6 = (f32[24,8,256]{2,1,0:T(8,128)S(1)}, f32[24,8,256]{2,1,0:T(8,128)S(1)}, u32[]{:S(2)}, u32[]{:S(2)}) collective-permute-start(f32[24,8,256]{2,1,0:T(8,128)S(1)} %broadcast_select_fusion.2), channel_id=1, source_target_pairs={{0,1},{1,0},{2,3},{3,2},{4,5},{5,4},{6,7},{7,6},{8,9},{9,8},{10,11... | collective-permute-start | bytes 589832 | tf_op jit(solution)/shard_map/ppermute | solution.py:33
  33.1 36.9 %collective-permute-start.8 = (f32[32,6,256]{2,1,0:T(8,128)}, f32[32,6,256]{2,1,0:T(8,128)}, u32[]{:S(2)}, u32[]{:S(2)}) collective-permute-start(f32[32,6,256]{2,1,0:T(8,128)} %get-tuple-element.12), channel_id=1, source_target_pairs={{16,0},{32,16},{48,32},{64,48},{80,64},{96,80},{112,96},{128,112},... | collective-permute-start | bytes 589832 | tf_op jit(solution)/shard_map/ppermute | solution.py:14
  40.0 37.1 %collective-permute-start.7 = (f32[32,6,256]{2,1,0:T(8,128)}, f32[32,6,256]{2,1,0:T(8,128)}, u32[]{:S(2)}, u32[]{:S(2)}) collective-permute-start(f32[32,6,256]{2,1,0:T(8,128)} %get-tuple-element.13), channel_id=1, source_target_pairs={{0,16},{16,32},{32,48},{48,64},{64,80},{80,96},{96,112},{112,128},... | collective-permute-start | bytes 589832 | tf_op jit(solution)/shard_map/ppermute | solution.py:14
  64.9 12.2 %copy-start.3 = (f32[6,16,8,256]{3,2,1,0:T(8,128)}, f32[6,16,8,256]{3,2,1,0:T(8,128)S(1)}, u32[]{:S(2)}) copy-start(f32[6,16,8,256]{3,2,1,0:T(8,128)S(1)} %collective-permute-done.1.north) | copy-start | bytes 2359300
  64.9 12.2 %copy-start.4 = (f32[6,16,8,256]{3,2,1,0:T(8,128)}, f32[6,16,8,256]{3,2,1,0:T(8,128)S(1)}, u32[]{:S(2)}) copy-start(f32[6,16,8,256]{3,2,1,0:T(8,128)S(1)} %collective-permute-done.south) | copy-start | bytes 2359300

commit v6 on v5

--- a/solution.py
+++ b/solution.py
@@ -50,17 +50,14 @@
     scalars, own, south, north, courant, south_courant, north_courant, coefficient,
     emissions, out, held, pivots, ratios, lowers, planes,
 ):
-    height, _, tracer_count, width = own.shape
-    levels = held.shape[0]
+    levels, height, tracer_count, width = held.shape
     halo = south.shape[0]
     rows = height + 2 * halo
-    level = pl.program_id(0)
     lane_shape = (tracer_count, width)
 
     def spread(row_ref, row):
         return jnp.broadcast_to(row_ref[pl.ds(row, 1), :], lane_shape)
 
-    @pl.when(level == 0)
     def _prepare():
         zero_plane = jnp.zeros((height, width), jnp.float32)
         previous_ratio = zero_plane
@@ -77,49 +74,54 @@
                 ratios[lev, row] = spread(planes.at[1], row)
                 lowers[lev, row] = spread(planes.at[2], row)
 
-    def wind_row(component, row):
-        index = component * levels + level
-        if row < halo:
-            return spread(south_courant.at[index], row)
-        if row < halo + height:
-            return spread(courant.at[index], row - halo)
-        return spread(north_courant.at[index], row - halo - height)
-
-    first_row = scalars[3 * ROUNDS]
-    zonal_up, zonal_down, merid_up, merid_down = [], [], [], []
-    for row in range(rows):
-        zonal = wind_row(0, row)
-        meridional = wind_row(1, row)
-        if row == halo:
-            meridional = meridional * first_row
-        zonal_up.append(jnp.maximum(zonal, 0.0))
-        zonal_down.append(jnp.minimum(zonal, 0.0))
-        merid_up.append(jnp.maximum(meridional, 0.0))
-        merid_down.append(jnp.minimum(meridional, 0.0))
-
-    mixing = [south[row, 0] for row in range(halo)]
-    mixing += [own[row, 0] for row in range(height)]
-    mixing += [north[row, 0] for row in range(halo)]
-    for substep in range(ROUNDS):
-        low, high = substep + 1, rows - 2 - substep
-        south_flux = {}
-        for row in range(low, high + 2):
-            south_flux[row] = merid_up[row] * mixing[row - 1] + merid_down[row] * mixing[row]
-        advanced = list(mixing)
-        for row in range(low, high + 1):
-            band = 0 if row < halo else (1 if row < halo + height else 2)
-            fraction = scalars[3 * substep + band]
-            from_west = pltpu.roll(mixing[row], 1, 1)
-            west_flux = zonal_up[row] * from_west + zonal_down[row] * mixing[row]
-            east_flux = pltpu.roll(west_flux, width - 1, 1)
-            advanced[row] = mixing[row] - fraction * (
-                (east_flux - west_flux) + (south_flux[row + 1] - south_flux[row])
-            )
-        mixing = advanced
-    for row in range(height):
-        held[level, row] = mixing[halo + row]
-
-    @pl.when(level == levels - 1)
+    _prepare()
+
+    def advect(level, carry):
+        def wind_row(component, row):
+            index = component * levels + level
+            if row < halo:
+                return spread(south_courant.at[index], row)
+            if row < halo + height:
+                return spread(courant.at[index], row - halo)
+            return spread(north_courant.at[index], row - halo - height)
+
+        first_row = scalars[3 * ROUNDS]
+        zonal_up, zonal_down, merid_up, merid_down = [], [], [], []
+        for row in range(rows):
+            zonal = wind_row(0, row)
+            meridional = wind_row(1, row)
+            if row == halo:
+                meridional = meridional * first_row
+            zonal_up.append(jnp.maximum(zonal, 0.0))
+            zonal_down.append(jnp.minimum(zonal, 0.0))
+            merid_up.append(jnp.maximum(meridional, 0.0))
+            merid_down.append(jnp.minimum(meridional, 0.0))
+
+        mixing = [south[row, level] for row in range(halo)]
+        mixing += [own[row, level] for row in range(height)]
+        mixing += [north[row, level] for row in range(halo)]
+        for substep in range(ROUNDS):
+            low, high = substep + 1, rows - 2 - substep
+            south_flux = {}
+            for row in range(low, high + 2):
+                south_flux[row] = merid_up[row] * mixing[row - 1] + merid_down[row] * mixing[row]
+            advanced = list(mixing)
+            for row in range(low, high + 1):
+                band = 0 if row < halo else (1 if row < halo + height else 2)
+                fraction = scalars[3 * substep + band]
+                from_west = pltpu.roll(mixing[row], 1, 1)
+                west_flux = zonal_up[row] * from_west + zonal_down[row] * mixing[row]
+                east_flux = pltpu.roll(west_flux, width - 1, 1)
+                advanced[row] = mixing[row] - fraction * (
+                    (east_flux - west_flux) + (south_flux[row + 1] - south_flux[row])
+                )
+            mixing = advanced
+        for row in range(height):
+            held[level, row] = mixing[halo + row]
+        return carry
+
+    lax.fori_loop(0, levels, advect, 0)
+
     def _finish():
         for row in range(height):
             held[0, row] = held[0, row] + emissions[row]
@@ -135,35 +137,19 @@
                 current = held[lev, row] + ratios[lev, row] * current
                 out[row, lev] = current
 
+    _finish()
+
 
 def transport(scalars, own, south, north, courant, south_courant, north_courant,
               coefficient, emissions):
     height, levels, tracer_count, width = own.shape
-    halo = south.shape[0]
-
-    def whole(shape):
-        return pl.BlockSpec(shape, lambda i: (0,) * len(shape))
-
-    def by_level(shape):
-        return pl.BlockSpec((shape[0], 1) + shape[2:], lambda i: (0, i, 0, 0))
-
+    vmem = pl.BlockSpec(memory_space=pltpu.VMEM)
     table = pltpu.VMEM((levels, height, tracer_count, width), jnp.float32)
     return pl.pallas_call(
         transport_kernel,
-        grid=(levels,),
         out_shape=jax.ShapeDtypeStruct(own.shape, jnp.float32),
-        in_specs=[
-            pl.BlockSpec(memory_space=pltpu.SMEM),
-            by_level(own.shape),
-            by_level(south.shape),
-            by_level(north.shape),
-            whole(courant.shape),
-            whole(south_courant.shape),
-            whole(north_courant.shape),
-            whole(coefficient.shape),
-            whole(emissions.shape),
-        ],
-        out_specs=whole(own.shape),
+        in_specs=[pl.BlockSpec(memory_space=pltpu.SMEM)] + [vmem] * 8,
+        out_specs=vmem,
         scratch_shapes=[
             table,
             table,
@@ -173,7 +159,7 @@
         ],
         cost_estimate=pl.CostEstimate(
             flops=levels * tracer_count * width * 78 * 14,
-            bytes_accessed=4 * (3 * own.size + 2 * south.size + 3 * courant.size),
+            bytes_accessed=4 * (2 * own.size + 2 * south.size + 3 * courant.size),
             transcendentals=0,
         ),
     )(scalars, own, south, north, courant, south_courant, north_courant,

time: 98.2 us -> 97.8 us (level)
  the two profiles are of different devices: /device:TPU:192 before, /device:TPU:161 now
where the time goes in v6:
time: 97.8 us; the launch traced here: 95.8 us
  waiting for transfers between devices  38.7 us (40%)
  starting transfers between devices  24.5 us (25%)
  Pallas kernels  17.5 us (18%)
  local copies, waits for them, and re-layouts  7.51 us (8%)
  other arithmetic  6.9 us (7%)
    ppermute x4, waiting for transfers between devices, from_behind(): return lax.ppermute(value, axis, pairs)  29.4 us
    pallas_call x1, Pallas kernels, transport(): pl.pallas_call(transport_kernel, out_shape=jax.ShapeDtypeStruct(own.shape...  17.5 us
    ppermute x4, starting transfers between devices, from_behind(): return lax.ppermute(value, axis, pairs)  16.3 us
    ppermute x5, waiting for transfers between devices, swap(): return lax.ppermute(current, axis, pairs)  9.27 us
    ppermute x5, starting transfers between devices, swap(): return lax.ppermute(current, axis, pairs)  8.13 us
    transpose x1, local copies, waits for them, and re-layouts, shards(): return jnp.transpose(mixed, (2, 1, 0, 3))  2.8 us
    unnamed x18, local copies, waits for them, and re-layouts  2.13 us
  transfers between devices with their start and end apart: 9, of which 4 were waited for; matrix products, arithmetic and copies ran while one was open for 10% of the time, Pallas kernels for 0%

profile of v6, /device:TPU:161, one launch (start us, length us, event | category | flops | bytes accessed | tf_op | source)
XLA Modules:
  0.0 95.8 jit_solution(6927621348267698915)
XLA Ops:
  0.2 1.2 %slice_select_fusion = f32[24,8,256]{2,1,0:T(8,128)S(1)} fusion(f32[32,8,256]{2,1,0:T(8,128)} %bitcast.17, pred[]{:T(512)S(6)} %eq.49, f32[24]{0:T(128)S(1)} %slice.39, f32[15,8,256]{2,1,0:T(8,128)} %bitcast.19), kind=kLoop, calls=%fused_computation.5 | loop fusion | flops 147456 | bytes 778337 | tf_op jit(solution)/shard_map/jit(_where)/select_n | solution.py:29
  1.4 0.8 collective-permute-start.2
  3.6 0.8 collective-permute-start.3
  4.4 5.6 %collective-permute-done.3 = f32[24,8,256]{2,1,0:T(8,128)S(1)} collective-permute-done((f32[24,8,256]{2,1,0:T(8,128)S(1)}, f32[24,8,256]{2,1,0:T(8,128)S(1)}, u32[]{:S(2)}, u32[]{:S(2)}) %collective-permute-start.3) | collective-permute-done | bytes 196640 | tf_op jit(solution)/shard_map/ppermute | solution.py:33
  10.1 1.3 %collective-permute-start.4 = (f32[24,8,256]{2,1,0:T(8,128)S(1)}, f32[24,8,256]{2,1,0:T(8,128)S(1)}, u32[]{:S(2)}, u32[]{:S(2)}) collective-permute-start(f32[24,8,256]{2,1,0:T(8,128)S(1)} %broadcast_select_fusion), channel_id=1, source_target_pairs={{0,4},{1,5},{2,6},{3,7},{4,0},{5,1},{6,2},{7,3},{8,12},{9,13},{10,... | collective-permute-start | bytes 589832 | tf_op jit(solution)/shard_map/ppermute | solution.py:33
  12.0 3.6 %collective-permute-done.4 = f32[24,8,256]{2,1,0:T(8,128)S(1)} collective-permute-done((f32[24,8,256]{2,1,0:T(8,128)S(1)}, f32[24,8,256]{2,1,0:T(8,128)S(1)}, u32[]{:S(2)}, u32[]{:S(2)}) %collective-permute-start.4) | collective-permute-done | bytes 196640 | tf_op jit(solution)/shard_map/ppermute | solution.py:33
  15.6 0.7 broadcast_select_fusion.1
  16.3 2.7 %collective-permute-start.5 = (f32[24,8,256]{2,1,0:T(8,128)}, f32[24,8,256]{2,1,0:T(8,128)}, u32[]{:S(2)}, u32[]{:S(2)}) collective-permute-start(f32[24,8,256]{2,1,0:T(8,128)} %broadcast_select_fusion.1), channel_id=1, source_target_pairs={{0,8},{1,9},{2,10},{3,11},{4,12},{5,13},{6,14},{7,15},{8,0},{9,1},... | collective-permute-start | bytes 589832 | tf_op jit(solution)/shard_map/ppermute | solution.py:33
  19.2 4.6 %collective-permute-start.1 = (f32[6,16,8,256]{3,2,1,0:T(8,128)S(1)}, f32[6,16,8,256]{3,2,1,0:T(8,128)S(1)}, u32[]{:S(2)}, u32[]{:S(2)}) collective-permute-start(f32[6,16,8,256]{3,2,1,0:T(8,128)S(1)} %get-tuple-element.10), channel_id=1, source_target_pairs={{16,0},{32,16},{48,32},{64,48},{80,64},{96,80},{112,96},{128,112},... | collective-permute-start | bytes 2359304 | tf_op jit(solution)/shard_map/ppermute | solution.py:14
  23.8 1.9 %collective-permute-start = (f32[6,16,8,256]{3,2,1,0:T(8,128)S(1)}, f32[6,16,8,256]{3,2,1,0:T(8,128)S(1)}, u32[]{:S(2)}, u32[]{:S(2)}) collective-permute-start(f32[6,16,8,256]{3,2,1,0:T(8,128)S(1)} %get-tuple-element.11), channel_id=1, source_target_pairs={{0,16},{16,32},{32,48},{48,64},{64,80},{80,96},{96,112},{112,128},... | collective-permute-start | bytes 2359304 | tf_op jit(solution)/shard_map/ppermute | solution.py:14
  25.8 1.0 %broadcast_select_fusion.2 = f32[24,8,256]{2,1,0:T(8,128)S(1)} fusion(f32[24,8,256]{2,1,0:T(8,128)} %collective-permute-done.5, f32[24,8,256]{2,1,0:T(8,128)} %broadcast_select_fusion.1, pred[]{:T(512)S(6)} %eq.52), kind=kLoop, calls=%fused_computation.8 | loop fusion | flops 49152 | bytes 589825 | tf_op jit(solution)/shard_map/jit(_where)/select_n | solution.py:38
  26.8 2.5 %collective-permute-start.6 = (f32[24,8,256]{2,1,0:T(8,128)S(1)}, f32[24,8,256]{2,1,0:T(8,128)S(1)}, u32[]{:S(2)}, u32[]{:S(2)}) collective-permute-start(f32[24,8,256]{2,1,0:T(8,128)S(1)} %broadcast_select_fusion.2), channel_id=1, source_target_pairs={{0,1},{1,0},{2,3},{3,2},{4,5},{5,4},{6,7},{7,6},{8,9},{9,8},{10,11... | collective-permute-start | bytes 589832 | tf_op jit(solution)/shard_map/ppermute | solution.py:33
  29.3 0.7 fusion.2
  30.0 2.0 %convert_divide_fusion = (f32[3]{0:T(128)S(1)}, s32[3]{0:T(128)S(1)}) fusion(s32[1]{0:T(128)} %bitcast.2, s32[1]{0:T(128)} %bitcast.1, s32[1]{0:T(128)} %bitcast), kind=kLoop, calls=%fused_computation.22 | loop fusion | flops 12 | bytes 36 | tf_op jit(solution)/shard_map/div | solution.py:201
  32.0 0.8 fusion.7
  32.8 7.9 %collective-permute-start.8 = (f32[32,6,256]{2,1,0:T(8,128)}, f32[32,6,256]{2,1,0:T(8,128)}, u32[]{:S(2)}, u32[]{:S(2)}) collective-permute-start(f32[32,6,256]{2,1,0:T(8,128)} %get-tuple-element.12), channel_id=1, source_target_pairs={{16,0},{32,16},{48,32},{64,48},{80,64},{96,80},{112,96},{128,112},... | collective-permute-start | bytes 589832 | tf_op jit(solution)/shard_map/ppermute | solution.py:14
  40.7 1.9 %collective-permute-start.7 = (f32[32,6,256]{2,1,0:T(8,128)}, f32[32,6,256]{2,1,0:T(8,128)}, u32[]{:S(2)}, u32[]{:S(2)}) collective-permute-start(f32[32,6,256]{2,1,0:T(8,128)} %get-tuple-element.13), channel_id=1, source_target_pairs={{0,16},{16,32},{32,48},{48,64},{64,80},{80,96},{96,112},{112,128},... | collective-permute-start | bytes 589832 | tf_op jit(solution)/shard_map/ppermute | solution.py:14
  42.7 1.5 %copy.16 = f32[8,8,256]{2,0,1:T(8,128)} copy(f32[8,8,256]{2,1,0:T(8,128)} %param.7) | data formatting | bytes 131072 | tf_op args[1]
  44.8 0.6 slice.44.coefficient
  45.4 0.7 slice.41.courant
  46.1 23.7 %collective-permute-done.south = f32[6,16,8,256]{3,2,1,0:T(8,128)S(1)} collective-permute-done((f32[6,16,8,256]{3,2,1,0:T(8,128)S(1)}, f32[6,16,8,256]{3,2,1,0:T(8,128)S(1)}, u32[]{:S(2)}, u32[]{:S(2)}) %collective-permute-start) | collective-permute-done | bytes 786464 | tf_op jit(solution)/shard_map/ppermute | solution.py:14
  69.8 5.7 %collective-permute-done.7.south_courant = f32[32,6,256]{2,1,0:T(8,128)} collective-permute-done((f32[32,6,256]{2,1,0:T(8,128)}, f32[32,6,256]{2,1,0:T(8,128)}, u32[]{:S(2)}, u32[]{:S(2)}) %collective-permute-start.7) | collective-permute-done | bytes 196640 | tf_op jit(solution)/shard_map/ppermute | solution.py:14
  75.5 17.5 %shard_map.64 = f32[8,16,8,256]{3,2,1,0:T(8,128)} custom-call(f32[19]{0:T(128)} %pad_maximum_fusion.1.scalars, f32[8,16,8,256]{3,2,1,0:T(8,128)} %bitcast.15, f32[6,16,8,256]{3,2,1,0:T(8,128)} %copy-done.4, f32[6,16,8,256]{3,2,1,0:T(8,128)} %copy-done.3, f32[32,8,256]{2,1,0:T(8,128)} %slice.41.courant, f32[32,6,256]{2,1,0:T(8,128)} %collective-permute-done.7.south_courant, ...), custom_call_target="tpu_custom_call" | custom-call | flops 35782656 | bytes 4456448 | tf_op jit(solution)/shard_map/pallas_call | solution.py:148
  93.0 2.8 %copy.12 = f32[8,16,8,256]{3,2,1,0:T(8,128)} copy(f32[8,16,8,256]{3,0,1,2:T(8,128)} %bitcast.16) | data formatting | bytes 2097152 | tf_op jit(solution)/shard_map/transpose | solution.py:208
  (32 shorter events, 2.4 us)
Async XLA Ops:
  0.0 2.2 %copy-start.7 = (s32[16]{0:T(128)S(1)}, s32[16]{0:T(128)}, u32[]{:S(2)}) copy-start(s32[16]{0:T(128)} %param.11) | copy-start | bytes 196
  0.0 3.4 %copy-start.5 = (f32[1,15,8,256]{3,2,1,0:T(8,128)S(1)}, f32[1,15,8,256]{3,2,1,0:T(8,128)}, u32[]{:S(2)}) copy-start(f32[1,15,8,256]{3,2,1,0:T(8,128)} %param.9) | copy-start | bytes 368644
  0.2 3.3 %copy-start.1 = (f32[1,2,16,8,256]{4,3,2,1,0:T(8,128)S(1)}, f32[1,2,16,8,256]{4,3,2,1,0:T(8,128)}, u32[]{:S(2)}) copy-start(f32[1,2,16,8,256]{4,3,2,1,0:T(8,128)} %param.8) | copy-start | bytes 786436
  0.2 11.2 %copy-start.2 = (f32[8,16,8,256]{3,2,1,0:T(8,128)S(1)}, f32[8,16,8,256]{3,2,1,0:T(8,128)}, u32[]{:S(2)}) copy-start(f32[8,16,8,256]{3,2,1,0:T(8,128)} %param.6) | copy-start | bytes 3145732
  1.4 2.1 %collective-permute-start.2 = (f32[24,8,256]{2,1,0:T(8,128)S(1)}, f32[24,8,256]{2,1,0:T(8,128)S(1)}, u32[]{:S(2)}, u32[]{:S(2)}) collective-permute-start(f32[24,8,256]{2,1,0:T(8,128)S(1)} %slice_select_fusion), channel_id=1, source_target_pairs={{0,1},{1,0},{2,3},{3,2},{4,5},{5,4},{6,7},{7,6},{8,9},{9,8},{10,11... | collective-permute-start | bytes 589832 | tf_op jit(solution)/shard_map/ppermute | solution.py:33
  3.6 6.5 %collective-permute-start.3 = (f32[24,8,256]{2,1,0:T(8,128)S(1)}, f32[24,8,256]{2,1,0:T(8,128)S(1)}, u32[]{:S(2)}, u32[]{:S(2)}) collective-permute-start(f32[24,8,256]{2,1,0:T(8,128)S(1)} %select_select_fusion), channel_id=1, source_target_pairs={{0,2},{1,3},{2,0},{3,1},{4,6},{5,7},{6,4},{7,5},{8,10},{9,11},{10,... | collective-permute-start | bytes 589832 | tf_op jit(solution)/shard_map/ppermute | solution.py:33
  10.1 5.5 %collective-permute-start.4 = (f32[24,8,256]{2,1,0:T(8,128)S(1)}, f32[24,8,256]{2,1,0:T(8,128)S(1)}, u32[]{:S(2)}, u32[]{:S(2)}) collective-permute-start(f32[24,8,256]{2,1,0:T(8,128)S(1)} %broadcast_select_fusion), channel_id=1, source_target_pairs={{0,4},{1,5},{2,6},{3,7},{4,0},{5,1},{6,2},{7,3},{8,12},{9,13},{10,... | collective-permute-start | bytes 589832 | tf_op jit(solution)/shard_map/ppermute | solution.py:33
  12.0 7.2 %copy-start = (f32[8,16,8,256]{3,0,1,2:T(8,128)}, f32[8,16,8,256]{3,0,1,2:T(8,128)S(1)}, u32[]{:S(2)}) copy-start(f32[8,16,8,256]{3,0,1,2:T(8,128)S(1)} %copy.15) | copy-start | bytes 3145732
  16.3 9.5 %collective-permute-start.5 = (f32[24,8,256]{2,1,0:T(8,128)}, f32[24,8,256]{2,1,0:T(8,128)}, u32[]{:S(2)}, u32[]{:S(2)}) collective-permute-start(f32[24,8,256]{2,1,0:T(8,128)} %broadcast_select_fusion.1), channel_id=1, source_target_pairs={{0,8},{1,9},{2,10},{3,11},{4,12},{5,13},{6,14},{7,15},{8,0},{9,1},... | collective-permute-start | bytes 589832 | tf_op jit(solution)/shard_map/ppermute | solution.py:33
  19.2 26.9 %collective-permute-start.1 = (f32[6,16,8,256]{3,2,1,0:T(8,128)S(1)}, f32[6,16,8,256]{3,2,1,0:T(8,128)S(1)}, u32[]{:S(2)}, u32[]{:S(2)}) collective-permute-start(f32[6,16,8,256]{3,2,1,0:T(8,128)S(1)} %get-tuple-element.10), channel_id=1, source_target_pairs={{16,0},{32,16},{48,32},{64,48},{80,64},{96,80},{112,96},{128,112},... | collective-permute-start | bytes 2359304 | tf_op jit(solution)/shard_map/ppermute | solution.py:14
  23.8 46.0 %collective-permute-start = (f32[6,16,8,256]{3,2,1,0:T(8,128)S(1)}, f32[6,16,8,256]{3,2,1,0:T(8,128)S(1)}, u32[]{:S(2)}, u32[]{:S(2)}) collective-permute-start(f32[6,16,8,256]{3,2,1,0:T(8,128)S(1)} %get-tuple-element.11), channel_id=1, source_target_pairs={{0,16},{16,32},{32,48},{48,64},{64,80},{80,96},{96,112},{112,128},... | collective-permute-start | bytes 2359304 | tf_op jit(solution)/shard_map/ppermute | solution.py:14
  25.8 3.5 %copy-start.6 = (s32[16]{0:T(128)S(1)}, s32[16]{0:T(128)}, u32[]{:S(2)}) copy-start(s32[16]{0:T(128)} %param.10) | copy-start | bytes 196
  26.8 5.2 %collective-permute-start.6 = (f32[24,8,256]{2,1,0:T(8,128)S(1)}, f32[24,8,256]{2,1,0:T(8,128)S(1)}, u32[]{:S(2)}, u32[]{:S(2)}) collective-permute-start(f32[24,8,256]{2,1,0:T(8,128)S(1)} %broadcast_select_fusion.2), channel_id=1, source_target_pairs={{0,1},{1,0},{2,3},{3,2},{4,5},{5,4},{6,7},{7,6},{8,9},{9,8},{10,11... | collective-permute-start | bytes 589832 | tf_op jit(solution)/shard_map/ppermute | solution.py:33
  32.8 37.0 %collective-permute-start.8 = (f32[32,6,256]{2,1,0:T(8,128)}, f32[32,6,256]{2,1,0:T(8,128)}, u32[]{:S(2)}, u32[]{:S(2)}) collective-permute-start(f32[32,6,256]{2,1,0:T(8,128)} %get-tuple-element.12), channel_id=1, source_target_pairs={{16,0},{32,16},{48,32},{64,48},{80,64},{96,80},{112,96},{128,112},... | collective-permute-start | bytes 589832 | tf_op jit(solution)/shard_map/ppermute | solution.py:14
  40.7 34.8 %collective-permute-start.7 = (f32[32,6,256]{2,1,0:T(8,128)}, f32[32,6,256]{2,1,0:T(8,128)}, u32[]{:S(2)}, u32[]{:S(2)}) collective-permute-start(f32[32,6,256]{2,1,0:T(8,128)} %get-tuple-element.13), channel_id=1, source_target_pairs={{0,16},{16,32},{32,48},{48,64},{64,80},{80,96},{96,112},{112,128},... | collective-permute-start | bytes 589832 | tf_op jit(solution)/shard_map/ppermute | solution.py:14
  46.1 29.4 %copy-start.3 = (f32[6,16,8,256]{3,2,1,0:T(8,128)}, f32[6,16,8,256]{3,2,1,0:T(8,128)S(1)}, u32[]{:S(2)}) copy-start(f32[6,16,8,256]{3,2,1,0:T(8,128)S(1)} %collective-permute-done.1.north) | copy-start | bytes 2359300
  69.8 5.7 %copy-start.4 = (f32[6,16,8,256]{3,2,1,0:T(8,128)}, f32[6,16,8,256]{3,2,1,0:T(8,128)S(1)}, u32[]{:S(2)}) copy-start(f32[6,16,8,256]{3,2,1,0:T(8,128)S(1)} %collective-permute-done.south) | copy-start | bytes 2359300

commit v7 on v6

--- a/solution.py
+++ b/solution.py
@@ -43,12 +43,12 @@
         jnp.concatenate([current, other]),
         jnp.concatenate([other, current]),
     )
-    return whole[: value.shape[0]]
+    return whole
 
 
 def transport_kernel(
-    scalars, own, south, north, courant, south_courant, north_courant, coefficient,
-    emissions, out, held, pivots, ratios, lowers, planes,
+    substeps, own, south, north, chosen, south_courant, north_courant, emissions, out,
+    held, pivots, ratios, lowers, planes, fractions,
 ):
     levels, height, tracer_count, width = held.shape
     halo = south.shape[0]
@@ -58,7 +58,24 @@
     def spread(row_ref, row):
         return jnp.broadcast_to(row_ref[pl.ds(row, 1), :], lane_shape)
 
+    tiles = substeps.shape[0]
+    tile_position = lax.axis_index("tile")
+    courant = chosen
+    coefficient = chosen.at[pl.ds(2 * levels, levels - 1)]
+
     def _prepare():
+        bands = (
+            jnp.maximum(tile_position - 1, 0),
+            tile_position,
+            jnp.minimum(tile_position + 1, tiles - 1),
+        )
+        for band, position in enumerate(bands):
+            count = substeps[position]
+            spread_count = jnp.full(lane_shape, count.astype(jnp.float32))
+            for substep in range(ROUNDS):
+                fractions[3 * substep + band] = jnp.where(
+                    substep < count, 1.0 / spread_count, jnp.float32(0.0)
+                )
         zero_plane = jnp.zeros((height, width), jnp.float32)
         previous_ratio = zero_plane
         for lev in range(levels):
@@ -85,7 +102,7 @@
                 return spread(courant.at[index], row - halo)
             return spread(north_courant.at[index], row - halo - height)
 
-        first_row = scalars[3 * ROUNDS]
+        first_row = jnp.where(tile_position > 0, jnp.float32(1.0), jnp.float32(0.0))
         zonal_up, zonal_down, merid_up, merid_down = [], [], [], []
         for row in range(rows):
             zonal = wind_row(0, row)
@@ -108,7 +125,7 @@
             advanced = list(mixing)
             for row in range(low, high + 1):
                 band = 0 if row < halo else (1 if row < halo + height else 2)
-                fraction = scalars[3 * substep + band]
+                fraction = fractions[3 * substep + band]
                 from_west = pltpu.roll(mixing[row], 1, 1)
                 west_flux = zonal_up[row] * from_west + zonal_down[row] * mixing[row]
                 east_flux = pltpu.roll(west_flux, width - 1, 1)
@@ -140,15 +157,15 @@
     _finish()
 
 
-def transport(scalars, own, south, north, courant, south_courant, north_courant,
-              coefficient, emissions):
+def transport(substeps, own, south, north, chosen, south_courant, north_courant,
+              emissions):
     height, levels, tracer_count, width = own.shape
     vmem = pl.BlockSpec(memory_space=pltpu.VMEM)
     table = pltpu.VMEM((levels, height, tracer_count, width), jnp.float32)
     return pl.pallas_call(
         transport_kernel,
         out_shape=jax.ShapeDtypeStruct(own.shape, jnp.float32),
-        in_specs=[pl.BlockSpec(memory_space=pltpu.SMEM)] + [vmem] * 8,
+        in_specs=[pl.BlockSpec(memory_space=pltpu.SMEM)] + [vmem] * 7,
         out_specs=vmem,
         scratch_shapes=[
             table,
@@ -156,14 +173,14 @@
             table,
             table,
             pltpu.VMEM((3, height, width), jnp.float32),
+            pltpu.VMEM((3 * ROUNDS, tracer_count, width), jnp.float32),
         ],
         cost_estimate=pl.CostEstimate(
             flops=levels * tracer_count * width * 78 * 14,
-            bytes_accessed=4 * (2 * own.size + 2 * south.size + 3 * courant.size),
+            bytes_accessed=4 * (2 * own.size + 2 * south.size + chosen.size),
             transcendentals=0,
         ),
-    )(scalars, own, south, north, courant, south_courant, north_courant,
-      coefficient, emissions)
+    )(substeps, own, south, north, chosen, south_courant, north_courant, emissions)
 
 
 def shards(tracers, emissions, winds, diffusivity, substeps, loader):
@@ -181,29 +198,15 @@
     )
     chosen = broadcast_from(local, "group", loader_slot)
     courant = chosen[: 2 * levels]
-    coefficient = chosen[2 * levels :]
 
     by_row = jnp.transpose(tracers, (2, 1, 0, 3))
     south_rows = from_behind(by_row[height - halo :], "tile", 1)
     north_rows = from_behind(by_row[:halo], "tile", -1)
     south_courant = from_behind(courant[:, height - halo :], "tile", 1)
     north_courant = from_behind(courant[:, :halo], "tile", -1)
-
-    def count_of(position):
-        clamped = jnp.clip(position, 0, tiles - 1)
-        return jnp.sum(jnp.where(tile_numbers == clamped, substeps, 0))
-
-    counts = jnp.stack(
-        [count_of(tile_position - 1), count_of(tile_position), count_of(tile_position + 1)]
-    )
-    counts_float = counts.astype(jnp.float32)
-    steps = jnp.arange(ROUNDS)[:, None]
-    fractions = jnp.where(steps < counts[None, :], 1.0 / counts_float[None, :], jnp.float32(0.0))
-    first_row = jnp.where(tile_position > 0, jnp.float32(1.0), jnp.float32(0.0))
-    scalars = jnp.concatenate([fractions.reshape(-1), first_row[None]])
     mixed = transport(
-        scalars, by_row, south_rows, north_rows, courant, south_courant,
-        north_courant, coefficient, jnp.transpose(emissions, (1, 0, 2)),
+        substeps, by_row, south_rows, north_rows, chosen, south_courant,
+        north_courant, jnp.transpose(emissions, (1, 0, 2)),
     )
     return jnp.transpose(mixed, (2, 1, 0, 3))
 

time: 97.8 us -> 97.8 us (level)
  waiting for transfers between devices: 38.7 us -> 44.3 us
  other arithmetic: 6.9 us -> 3.68 us
  local copies, waits for them, and re-layouts: 7.51 us -> 5.12 us
    ppermute x4, waiting for transfers between devices: 29.4 us -> 34 us  [from_behind(): return lax.ppermute(value, axis, pairs)]
    div x1 -> x0, other arithmetic: 1.95 us -> none  [shards(): 1.0 / counts_float[None, :]]
    slice x2 -> x0, local copies, waits for them, and re-layouts: 1.37 us -> none  [the longest x1 0.72 us: shards(): courant = chosen[:2 * levels]]
    ppermute x5, waiting for transfers between devices: 9.27 us -> 10.3 us  [swap(): return lax.ppermute(current, axis, pairs)]
    unnamed x18 -> x22, local copies, waits for them, and re-layouts: 2.13 us -> 1.98 us
  transfers between devices with their start and end apart: 9 -> 9, of which waited for: 4 -> 5; matrix products, arithmetic and copies ran while one was open for 10% -> 3% of each run, Pallas kernels for 0% -> 0%
where the time goes in v7:
time: 97.8 us; the launch traced here: 96 us
  waiting for transfers between devices  44.3 us (45%)
  starting transfers between devices  24.4 us (25%)
  Pallas kernels  17.6 us (18%)
  local copies, waits for them, and re-layouts  5.12 us (5%)
  other arithmetic  3.68 us (4%)
    ppermute x4, waiting for transfers between devices, from_behind(): return lax.ppermute(value, axis, pairs)  34 us
    pallas_call x1, Pallas kernels, transport(): pl.pallas_call(transport_kernel, out_shape=jax.ShapeDtypeStruct(own.shape...  17.6 us
    ppermute x4, starting transfers between devices, from_behind(): return lax.ppermute(value, axis, pairs)  16.3 us
    ppermute x5, waiting for transfers between devices, swap(): return lax.ppermute(current, axis, pairs)  10.3 us
    ppermute x5, starting transfers between devices, swap(): return lax.ppermute(current, axis, pairs)  8.13 us
    transpose x1, local copies, waits for them, and re-layouts, shards(): return jnp.transpose(mixed, (2, 1, 0, 3))  2.8 us
    unnamed x22, local copies, waits for them, and re-layouts  1.98 us
  transfers between devices with their start and end apart: 9, of which 5 were waited for; matrix products, arithmetic and copies ran while one was open for 3% of the time, Pallas kernels for 0%

profile of v7, /device:TPU:161, one launch (start us, length us, event | category | flops | bytes accessed | tf_op | source)
XLA Modules:
  0.0 96.0 jit_solution(6975434211126763393)
XLA Ops:
  0.2 1.2 %slice_select_fusion = f32[24,8,256]{2,1,0:T(8,128)S(1)} fusion(f32[32,8,256]{2,1,0:T(8,128)} %bitcast.13, pred[]{:T(512)S(6)} %eq.25, f32[24]{0:T(128)S(1)} %slice.29, f32[15,8,256]{2,1,0:T(8,128)} %bitcast.15), kind=kLoop, calls=%fused_computation.5 | loop fusion | flops 147456 | bytes 778337 | tf_op jit(solution)/shard_map/jit(_where)/select_n | solution.py:29
  1.4 0.8 collective-permute-start.2
  2.2 0.6 fusion.1
  3.6 0.8 collective-permute-start.3
  4.4 5.6 %collective-permute-done.3 = f32[24,8,256]{2,1,0:T(8,128)S(1)} collective-permute-done((f32[24,8,256]{2,1,0:T(8,128)S(1)}, f32[24,8,256]{2,1,0:T(8,128)S(1)}, u32[]{:S(2)}, u32[]{:S(2)}) %collective-permute-start.3) | collective-permute-done | bytes 196640 | tf_op jit(solution)/shard_map/ppermute | solution.py:33
  10.1 1.3 %collective-permute-start.4 = (f32[24,8,256]{2,1,0:T(8,128)S(1)}, f32[24,8,256]{2,1,0:T(8,128)S(1)}, u32[]{:S(2)}, u32[]{:S(2)}) collective-permute-start(f32[24,8,256]{2,1,0:T(8,128)S(1)} %broadcast_select_fusion), channel_id=1, source_target_pairs={{0,4},{1,5},{2,6},{3,7},{4,0},{5,1},{6,2},{7,3},{8,12},{9,13},{10,... | collective-permute-start | bytes 589832 | tf_op jit(solution)/shard_map/ppermute | solution.py:33
  11.4 0.6 copy.12
  12.0 3.6 %collective-permute-done.4 = f32[24,8,256]{2,1,0:T(8,128)S(1)} collective-permute-done((f32[24,8,256]{2,1,0:T(8,128)S(1)}, f32[24,8,256]{2,1,0:T(8,128)S(1)}, u32[]{:S(2)}, u32[]{:S(2)}) %collective-permute-start.4) | collective-permute-done | bytes 196640 | tf_op jit(solution)/shard_map/ppermute | solution.py:33
  15.6 0.7 broadcast_select_fusion.1
  16.3 2.7 %collective-permute-start.5 = (f32[24,8,256]{2,1,0:T(8,128)}, f32[24,8,256]{2,1,0:T(8,128)}, u32[]{:S(2)}, u32[]{:S(2)}) collective-permute-start(f32[24,8,256]{2,1,0:T(8,128)} %broadcast_select_fusion.1), channel_id=1, source_target_pairs={{0,8},{1,9},{2,10},{3,11},{4,12},{5,13},{6,14},{7,15},{8,0},{9,1},... | collective-permute-start | bytes 589832 | tf_op jit(solution)/shard_map/ppermute | solution.py:33
  19.1 0.1 fusion.2
  19.2 4.6 %collective-permute-start.1 = (f32[6,16,8,256]{3,2,1,0:T(8,128)S(1)}, f32[6,16,8,256]{3,2,1,0:T(8,128)S(1)}, u32[]{:S(2)}, u32[]{:S(2)}) collective-permute-start(f32[6,16,8,256]{3,2,1,0:T(8,128)S(1)} %get-tuple-element.5), channel_id=1, source_target_pairs={{16,0},{32,16},{48,32},{64,48},{80,64},{96,80},{112,96},{128,112},... | collective-permute-start | bytes 2359304 | tf_op jit(solution)/shard_map/ppermute | solution.py:14
  23.9 1.9 %collective-permute-start = (f32[6,16,8,256]{3,2,1,0:T(8,128)S(1)}, f32[6,16,8,256]{3,2,1,0:T(8,128)S(1)}, u32[]{:S(2)}, u32[]{:S(2)}) collective-permute-start(f32[6,16,8,256]{3,2,1,0:T(8,128)S(1)} %get-tuple-element.6), channel_id=1, source_target_pairs={{0,16},{16,32},{32,48},{48,64},{64,80},{80,96},{96,112},{112,128},... | collective-permute-start | bytes 2359304 | tf_op jit(solution)/shard_map/ppermute | solution.py:14
  25.8 1.0 %broadcast_select_fusion.2 = f32[24,8,256]{2,1,0:T(8,128)S(1)} fusion(f32[24,8,256]{2,1,0:T(8,128)} %collective-permute-done.5, f32[24,8,256]{2,1,0:T(8,128)} %broadcast_select_fusion.1, pred[]{:T(512)S(6)} %eq.28), kind=kLoop, calls=%fused_computation.8 | loop fusion | flops 49152 | bytes 589825 | tf_op jit(solution)/shard_map/jit(_where)/select_n | solution.py:38
  26.8 2.5 %collective-permute-start.6 = (f32[24,8,256]{2,1,0:T(8,128)S(1)}, f32[24,8,256]{2,1,0:T(8,128)S(1)}, u32[]{:S(2)}, u32[]{:S(2)}) collective-permute-start(f32[24,8,256]{2,1,0:T(8,128)S(1)} %broadcast_select_fusion.2), channel_id=1, source_target_pairs={{0,1},{1,0},{2,3},{3,2},{4,5},{5,4},{6,7},{7,6},{8,9},{9,8},{10,11... | collective-permute-start | bytes 589832 | tf_op jit(solution)/shard_map/ppermute | solution.py:33
  29.3 1.1 %collective-permute-done.6 = f32[24,8,256]{2,1,0:T(8,128)S(1)} collective-permute-done((f32[24,8,256]{2,1,0:T(8,128)S(1)}, f32[24,8,256]{2,1,0:T(8,128)S(1)}, u32[]{:S(2)}, u32[]{:S(2)}) %collective-permute-start.6) | collective-permute-done | bytes 196640 | tf_op jit(solution)/shard_map/ppermute | solution.py:33
  30.5 0.7 copy-done.1
  31.2 7.8 %collective-permute-start.8 = (f32[32,6,256]{2,1,0:T(8,128)S(1)}, f32[32,6,256]{2,1,0:T(8,128)S(1)}, u32[]{:S(2)}, u32[]{:S(2)}) collective-permute-start(f32[32,6,256]{2,1,0:T(8,128)S(1)} %get-tuple-element.7), channel_id=1, source_target_pairs={{16,0},{32,16},{48,32},{64,48},{80,64},{96,80},{112,96},{128,112},... | collective-permute-start | bytes 589832 | tf_op jit(solution)/shard_map/ppermute | solution.py:14
  39.0 1.9 %collective-permute-start.7 = (f32[32,6,256]{2,1,0:T(8,128)S(1)}, f32[32,6,256]{2,1,0:T(8,128)}, u32[]{:S(2)}, u32[]{:S(2)}) collective-permute-start(f32[32,6,256]{2,1,0:T(8,128)S(1)} %get-tuple-element.8), channel_id=1, source_target_pairs={{0,16},{16,32},{32,48},{48,64},{64,80},{80,96},{96,112},{112,128},... | collective-permute-start | bytes 589832 | tf_op jit(solution)/shard_map/ppermute | solution.py:14
  40.9 0.6 copy.13
  41.6 28.2 %collective-permute-done.south = f32[6,16,8,256]{3,2,1,0:T(8,128)S(1)} collective-permute-done((f32[6,16,8,256]{3,2,1,0:T(8,128)S(1)}, f32[6,16,8,256]{3,2,1,0:T(8,128)S(1)}, u32[]{:S(2)}, u32[]{:S(2)}) %collective-permute-start) | collective-permute-done | bytes 786464 | tf_op jit(solution)/shard_map/ppermute | solution.py:14
  69.8 5.7 %collective-permute-done.7.south_courant = f32[32,6,256]{2,1,0:T(8,128)} collective-permute-done((f32[32,6,256]{2,1,0:T(8,128)S(1)}, f32[32,6,256]{2,1,0:T(8,128)}, u32[]{:S(2)}, u32[]{:S(2)}) %collective-permute-start.7) | collective-permute-done | bytes 196640 | tf_op jit(solution)/shard_map/ppermute | solution.py:14
  75.6 17.6 %shard_map.64 = f32[8,16,8,256]{3,2,1,0:T(8,128)} custom-call(s32[16]{0:T(128)} %substeps.1, f32[8,16,8,256]{3,2,1,0:T(8,128)} %bitcast.11, f32[6,16,8,256]{3,2,1,0:T(8,128)} %copy-done.5, f32[6,16,8,256]{3,2,1,0:T(8,128)} %copy-done.4, f32[48,8,256]{2,1,0:T(8,128)} %copy-done.1, f32[32,6,256]{2,1,0:T(8,128)} %collective-permute-done.7.south_courant, ...), custom_call_target="tpu_custom_call" | custom-call | flops 35782656 | bytes 4063232 | tf_op jit(solution)/shard_map/pallas_call | solution.py:165
  93.1 2.8 %copy.9 = f32[8,16,8,256]{3,2,1,0:T(8,128)} copy(f32[8,16,8,256]{3,0,1,2:T(8,128)} %bitcast.12) | data formatting | bytes 2097152 | tf_op jit(solution)/shard_map/transpose | solution.py:211
  (29 shorter events, 0.4 us)
Async XLA Ops:
  0.0 2.2 %copy-start.9 = (s32[16]{0:T(128)S(1)}, s32[16]{0:T(128)}, u32[]{:S(2)}) copy-start(s32[16]{0:T(128)} %param.11) | copy-start | bytes 196
  0.0 3.4 %copy-start.6 = (f32[1,15,8,256]{3,2,1,0:T(8,128)S(1)}, f32[1,15,8,256]{3,2,1,0:T(8,128)}, u32[]{:S(2)}) copy-start(f32[1,15,8,256]{3,2,1,0:T(8,128)} %param.9) | copy-start | bytes 368644
  0.2 3.3 %copy-start.2 = (f32[1,2,16,8,256]{4,3,2,1,0:T(8,128)S(1)}, f32[1,2,16,8,256]{4,3,2,1,0:T(8,128)}, u32[]{:S(2)}) copy-start(f32[1,2,16,8,256]{4,3,2,1,0:T(8,128)} %param.8) | copy-start | bytes 786436
  0.2 11.2 %copy-start.3 = (f32[8,16,8,256]{3,2,1,0:T(8,128)S(1)}, f32[8,16,8,256]{3,2,1,0:T(8,128)}, u32[]{:S(2)}) copy-start(f32[8,16,8,256]{3,2,1,0:T(8,128)} %param.6) | copy-start | bytes 3145732
  1.4 2.1 %collective-permute-start.2 = (f32[24,8,256]{2,1,0:T(8,128)S(1)}, f32[24,8,256]{2,1,0:T(8,128)S(1)}, u32[]{:S(2)}, u32[]{:S(2)}) collective-permute-start(f32[24,8,256]{2,1,0:T(8,128)S(1)} %slice_select_fusion), channel_id=1, source_target_pairs={{0,1},{1,0},{2,3},{3,2},{4,5},{5,4},{6,7},{7,6},{8,9},{9,8},{10,11... | collective-permute-start | bytes 589832 | tf_op jit(solution)/shard_map/ppermute | solution.py:33
  3.6 6.5 %collective-permute-start.3 = (f32[24,8,256]{2,1,0:T(8,128)S(1)}, f32[24,8,256]{2,1,0:T(8,128)S(1)}, u32[]{:S(2)}, u32[]{:S(2)}) collective-permute-start(f32[24,8,256]{2,1,0:T(8,128)S(1)} %select_select_fusion), channel_id=1, source_target_pairs={{0,2},{1,3},{2,0},{3,1},{4,6},{5,7},{6,4},{7,5},{8,10},{9,11},{10,... | collective-permute-start | bytes 589832 | tf_op jit(solution)/shard_map/ppermute | solution.py:33
  10.1 5.5 %collective-permute-start.4 = (f32[24,8,256]{2,1,0:T(8,128)S(1)}, f32[24,8,256]{2,1,0:T(8,128)S(1)}, u32[]{:S(2)}, u32[]{:S(2)}) collective-permute-start(f32[24,8,256]{2,1,0:T(8,128)S(1)} %broadcast_select_fusion), channel_id=1, source_target_pairs={{0,4},{1,5},{2,6},{3,7},{4,0},{5,1},{6,2},{7,3},{8,12},{9,13},{10,... | collective-permute-start | bytes 589832 | tf_op jit(solution)/shard_map/ppermute | solution.py:33
  12.0 7.2 %copy-start = (f32[8,16,8,256]{3,0,1,2:T(8,128)}, f32[8,16,8,256]{3,0,1,2:T(8,128)S(1)}, u32[]{:S(2)}) copy-start(f32[8,16,8,256]{3,0,1,2:T(8,128)S(1)} %copy.12) | copy-start | bytes 3145732
  16.3 9.5 %collective-permute-start.5 = (f32[24,8,256]{2,1,0:T(8,128)}, f32[24,8,256]{2,1,0:T(8,128)}, u32[]{:S(2)}, u32[]{:S(2)}) collective-permute-start(f32[24,8,256]{2,1,0:T(8,128)} %broadcast_select_fusion.1), channel_id=1, source_target_pairs={{0,8},{1,9},{2,10},{3,11},{4,12},{5,13},{6,14},{7,15},{8,0},{9,1},... | collective-permute-start | bytes 589832 | tf_op jit(solution)/shard_map/ppermute | solution.py:33
  19.2 22.4 %collective-permute-start.1 = (f32[6,16,8,256]{3,2,1,0:T(8,128)S(1)}, f32[6,16,8,256]{3,2,1,0:T(8,128)S(1)}, u32[]{:S(2)}, u32[]{:S(2)}) collective-permute-start(f32[6,16,8,256]{3,2,1,0:T(8,128)S(1)} %get-tuple-element.5), channel_id=1, source_target_pairs={{16,0},{32,16},{48,32},{64,48},{80,64},{96,80},{112,96},{128,112},... | collective-permute-start | bytes 2359304 | tf_op jit(solution)/shard_map/ppermute | solution.py:14
  23.9 46.0 %collective-permute-start = (f32[6,16,8,256]{3,2,1,0:T(8,128)S(1)}, f32[6,16,8,256]{3,2,1,0:T(8,128)S(1)}, u32[]{:S(2)}, u32[]{:S(2)}) collective-permute-start(f32[6,16,8,256]{3,2,1,0:T(8,128)S(1)} %get-tuple-element.6), channel_id=1, source_target_pairs={{0,16},{16,32},{32,48},{48,64},{64,80},{80,96},{96,112},{112,128},... | collective-permute-start | bytes 2359304 | tf_op jit(solution)/shard_map/ppermute | solution.py:14
  26.8 3.6 %collective-permute-start.6 = (f32[24,8,256]{2,1,0:T(8,128)S(1)}, f32[24,8,256]{2,1,0:T(8,128)S(1)}, u32[]{:S(2)}, u32[]{:S(2)}) collective-permute-start(f32[24,8,256]{2,1,0:T(8,128)S(1)} %broadcast_select_fusion.2), channel_id=1, source_target_pairs={{0,1},{1,0},{2,3},{3,2},{4,5},{5,4},{6,7},{7,6},{8,9},{9,8},{10,11... | collective-permute-start | bytes 589832 | tf_op jit(solution)/shard_map/ppermute | solution.py:33
  30.4 0.8 copy-start.1
  30.4 10.5 %copy-start.8 = (f32[8,8,256]{2,1,0:T(8,128)S(1)}, f32[8,8,256]{2,1,0:T(8,128)}, u32[]{:S(2)}) copy-start(f32[8,8,256]{2,1,0:T(8,128)} %param.7) | copy-start | bytes 196612
  31.2 38.7 %collective-permute-start.8 = (f32[32,6,256]{2,1,0:T(8,128)S(1)}, f32[32,6,256]{2,1,0:T(8,128)S(1)}, u32[]{:S(2)}, u32[]{:S(2)}) collective-permute-start(f32[32,6,256]{2,1,0:T(8,128)S(1)} %get-tuple-element.7), channel_id=1, source_target_pairs={{16,0},{32,16},{48,32},{64,48},{80,64},{96,80},{112,96},{128,112},... | collective-permute-start | bytes 589832 | tf_op jit(solution)/shard_map/ppermute | solution.py:14
  39.0 36.6 %collective-permute-start.7 = (f32[32,6,256]{2,1,0:T(8,128)S(1)}, f32[32,6,256]{2,1,0:T(8,128)}, u32[]{:S(2)}, u32[]{:S(2)}) collective-permute-start(f32[32,6,256]{2,1,0:T(8,128)S(1)} %get-tuple-element.8), channel_id=1, source_target_pairs={{0,16},{16,32},{32,48},{48,64},{64,80},{80,96},{96,112},{112,128},... | collective-permute-start | bytes 589832 | tf_op jit(solution)/shard_map/ppermute | solution.py:14
  41.6 34.0 %copy-start.4 = (f32[6,16,8,256]{3,2,1,0:T(8,128)}, f32[6,16,8,256]{3,2,1,0:T(8,128)S(1)}, u32[]{:S(2)}) copy-start(f32[6,16,8,256]{3,2,1,0:T(8,128)S(1)} %collective-permute-done.1.north) | copy-start | bytes 2359300
  69.8 5.7 %copy-start.5 = (f32[6,16,8,256]{3,2,1,0:T(8,128)}, f32[6,16,8,256]{3,2,1,0:T(8,128)S(1)}, u32[]{:S(2)}) copy-start(f32[6,16,8,256]{3,2,1,0:T(8,128)S(1)} %collective-permute-done.south) | copy-start | bytes 2359300
  69.8 5.7 %copy-start.7 = (f32[32,6,256]{2,1,0:T(8,128)}, f32[32,6,256]{2,1,0:T(8,128)S(1)}, u32[]{:S(2)}) copy-start(f32[32,6,256]{2,1,0:T(8,128)S(1)} %collective-permute-done.8.north_courant) | copy-start | bytes 589828

commit v8 on v7

--- a/solution.py
+++ b/solution.py
@@ -14,36 +14,129 @@
     return lax.ppermute(value, axis, pairs)
 
 
-def broadcast_from(value, axis, root):
-    count = lax.axis_size(axis)
-    assert count & (count - 1) == 0 and count >= 2
-    position = lax.axis_index(axis)
-    distance = position ^ root
-    core = position % 2
+def exchange_kernel(
+    masked, up, down, chosen, south, north, south_courant, north_courant,
+    total, received, send_sems, recv_sems,
+):
+    mesh = pl.DeviceIdType.MESH
+    tiles = lax.axis_size("tile")
+    bits = lax.axis_size("group").bit_length() - 1
+    tile = lax.axis_index("tile")
+    me = lax.axis_index("group")
+    core = me % 2
+    half = masked.shape[0] // 2
+    planes = south_courant.shape[0]
+
+    def partner(bit):
+        return me + (1 << bit) * (1 - 2 * ((me // (1 << bit)) % 2))
+
+    barrier = pltpu.get_barrier_semaphore()
+    for bit in range(bits):
+        pl.semaphore_signal(barrier, 1, device_id=(tile, partner(bit)), device_id_type=mesh)
+
+    @pl.when(tile > 0)
+    def _():
+        pl.semaphore_signal(barrier, 1, device_id=(tile - 1, me), device_id_type=mesh)
+
+    @pl.when(tile < tiles - 1)
+    def _():
+        pl.semaphore_signal(barrier, 1, device_id=(tile + 1, me), device_id_type=mesh)
+
+    has_south = (tile + tiles - 1) // tiles
+    has_north = (2 * tiles - 3 - tile) // (tiles - 1)
+    pl.semaphore_wait(barrier, bits + has_south + has_north)
+
+    def along_tile(source, target, slot, by):
+        return pltpu.make_async_remote_copy(
+            src_ref=source, dst_ref=target, send_sem=send_sems.at[slot],
+            recv_sem=recv_sems.at[slot], device_id=(tile + by, me), device_id_type=mesh,
+        )
+
+    @pl.when(tile < tiles - 1)
+    def _():
+        along_tile(up, south, 0, 1).start()
+
+    @pl.when(tile > 0)
+    def _():
+        along_tile(down, north, 1, -1).start()
+
+    @pl.when(tile == 0)
+    def _():
+        south[...] = jnp.zeros_like(south)
+        south_courant[...] = jnp.zeros_like(south_courant)
+
+    @pl.when(tile == tiles - 1)
+    def _():
+        north[...] = jnp.zeros_like(north)
+        north_courant[...] = jnp.zeros_like(north_courant)
+
+    def along_group(source, bit, slot):
+        copy = pltpu.make_async_remote_copy(
+            src_ref=source, dst_ref=received.at[slot], send_sem=send_sems.at[2 + slot],
+            recv_sem=recv_sems.at[2 + slot], device_id=(tile, partner(bit)),
+            device_id_type=mesh,
+        )
+        copy.start()
+        copy.wait()
+
+    along_group(masked.at[pl.ds((1 - core) * half, half)], 0, 0)
+    total[...] = masked[pl.ds(core * half, half)] + received[0]
+    for bit in range(1, bits):
+        along_group(total, bit, bit)
+        total[...] = total[...] + received[bit]
+    along_group(total, 0, bits)
+    chosen[pl.ds(core * half, half)] = total[...]
+    chosen[pl.ds((1 - core) * half, half)] = received[bits]
+
+    @pl.when(tile < tiles - 1)
+    def _():
+        along_tile(chosen.at[pl.ds(0, planes)], south_courant, 2 + bits + 1, 1).start()
+
+    @pl.when(tile > 0)
+    def _():
+        along_tile(chosen.at[pl.ds(0, planes)], north_courant, 2 + bits + 2, -1).start()
+
+    @pl.when(tile < tiles - 1)
+    def _():
+        along_tile(up, south, 0, 1).wait_send()
+        along_tile(chosen.at[pl.ds(0, planes)], south_courant, 2 + bits + 1, 1).wait_send()
+        along_tile(up, north, 1, 1).wait_recv()
+        along_tile(chosen.at[pl.ds(0, planes)], north_courant, 2 + bits + 2, 1).wait_recv()
+
+    @pl.when(tile > 0)
+    def _():
+        along_tile(down, north, 1, -1).wait_send()
+        along_tile(chosen.at[pl.ds(0, planes)], north_courant, 2 + bits + 2, -1).wait_send()
+        along_tile(down, south, 0, -1).wait_recv()
+        along_tile(chosen.at[pl.ds(0, planes)], south_courant, 2 + bits + 1, -1).wait_recv()
+
+
+def exchange(value, by_row, root, halo, planes):
+    groups = lax.axis_size("group")
+    assert groups & (groups - 1) == 0 and groups >= 2
+    bits = groups.bit_length() - 1
     half = -(-value.shape[0] // 2)
     padded = jnp.concatenate(
         [value, jnp.zeros((2 * half - value.shape[0],) + value.shape[1:], value.dtype)]
     )
-    low, high = padded[:half], padded[half:]
-    mine = jnp.where(core == 0, low, high)
-    theirs = jnp.where(core == 0, high, low)
-
-    def swap(current, bit):
-        pairs = [(i, i ^ (1 << bit)) for i in range(count)]
-        return lax.ppermute(current, axis, pairs)
-
-    current = jnp.where(distance == 1, swap(theirs, 0), mine)
-    bit = 1
-    while (1 << bit) < count:
-        current = jnp.where((distance >> bit) == 1, swap(current, bit), current)
-        bit += 1
-    other = swap(current, 0)
-    whole = jnp.where(
-        core == 0,
-        jnp.concatenate([current, other]),
-        jnp.concatenate([other, current]),
-    )
-    return whole
+    masked = jnp.where(lax.axis_index("group") == root, padded, jnp.zeros_like(padded))
+    height = by_row.shape[0]
+    vmem = pl.BlockSpec(memory_space=pltpu.VMEM)
+    rows = jax.ShapeDtypeStruct((halo,) + by_row.shape[1:], by_row.dtype)
+    winds = jax.ShapeDtypeStruct((planes,) + value.shape[1:], value.dtype)
+    return pl.pallas_call(
+        exchange_kernel,
+        out_shape=(jax.ShapeDtypeStruct(padded.shape, padded.dtype), rows, rows, winds, winds),
+        in_specs=[vmem] * 3,
+        out_specs=(vmem,) * 5,
+        scratch_shapes=[
+            pltpu.VMEM((half,) + value.shape[1:], value.dtype),
+            pltpu.VMEM((bits + 1, half) + value.shape[1:], value.dtype),
+            pltpu.SemaphoreType.DMA((bits + 5,)),
+            pltpu.SemaphoreType.DMA((bits + 5,)),
+        ],
+        compiler_params=pltpu.CompilerParams(collective_id=0, has_side_effects=True),
+    )(masked, by_row[height - halo :], by_row[:halo])
 
 
 def transport_kernel(
@@ -97,7 +190,7 @@
         def wind_row(component, row):
             index = component * levels + level
             if row < halo:
-                return spread(south_courant.at[index], row)
+                return spread(south_courant.at[index], row + height - halo)
             if row < halo + height:
                 return spread(courant.at[index], row - halo)
             return spread(north_courant.at[index], row - halo - height)
@@ -196,14 +289,10 @@
     local = jnp.concatenate(
         [winds[0].reshape(2 * levels, height, width), diffusivity[0]], axis=0
     )
-    chosen = broadcast_from(local, "group", loader_slot)
-    courant = chosen[: 2 * levels]
-
     by_row = jnp.transpose(tracers, (2, 1, 0, 3))
-    south_rows = from_behind(by_row[height - halo :], "tile", 1)
-    north_rows = from_behind(by_row[:halo], "tile", -1)
-    south_courant = from_behind(courant[:, height - halo :], "tile", 1)
-    north_courant = from_behind(courant[:, :halo], "tile", -1)
+    chosen, south_rows, north_rows, south_courant, north_courant = exchange(
+        local, by_row, loader_slot, halo, 2 * levels
+    )
     mixed = transport(
         substeps, by_row, south_rows, north_rows, chosen, south_courant,
         north_courant, jnp.transpose(emissions, (1, 0, 2)),

time: 97.8 us -> 106 us (1.084); the launches traced: 96 us -> 106 us
  Pallas kernels: 17.6 us -> 96.2 us
  waiting for transfers between devices: 44.3 us -> 0 us
  starting transfers between devices: 24.4 us -> 0 us
  local copies, waits for them, and re-layouts: 5.12 us -> 7.48 us
  other arithmetic: 3.68 us -> 1.57 us
    pallas_call x0 -> x1, Pallas kernels: none -> 78.6 us  [exchange(): pl.pallas_call(exchange_kernel, out_shape=(jax.ShapeDtypeStruct(padded.sh...]
    ppermute x9 -> x0, waiting for transfers between devices: 44.3 us -> none  [the longest x4 34 us: from_behind(): return lax.ppermute(value, axis, pairs)]
    ppermute x9 -> x0, starting transfers between devices: 24.4 us -> none  [the longest x4 16.3 us: from_behind(): return lax.ppermute(value, axis, pairs)]
    select_n x6 -> x1, other arithmetic: 3.05 us -> 0.86 us  [exchange(): jnp.where(lax.axis_index('group') == root, padded, jnp.zeros_like(padded))]
    unnamed x22 -> x12, local copies, waits for them, and re-layouts: 1.98 us -> 3.29 us
  transfers between devices with their start and end apart: 9 -> 0, of which waited for: 5 -> 0; matrix products, arithmetic and copies ran while one was open for 3% -> 0% of each run, Pallas kernels for 0% -> 0%
where the time goes in v8:
time: 106 us
  Pallas kernels  96.2 us (91%)
  local copies, waits for them, and re-layouts  7.48 us (7%)
  other arithmetic  1.57 us (1%)
    pallas_call x1, Pallas kernels, exchange(): pl.pallas_call(exchange_kernel, out_shape=(jax.ShapeDtypeStruct(padded.sh...  78.6 us
    pallas_call x1, Pallas kernels, transport(): pl.pallas_call(transport_kernel, out_shape=jax.ShapeDtypeStruct(own.shape...  17.6 us
    unnamed x12, local copies, waits for them, and re-layouts  3.29 us
    transpose x1, local copies, waits for them, and re-layouts, shards(): return jnp.transpose(mixed, (2, 1, 0, 3))  2.8 us

profile of v8, /device:TPU:161, one launch (start us, length us, event | category | flops | bytes accessed | tf_op | source)
XLA Modules:
  0.0 106.0 jit_solution(723651970156789442)
XLA Ops:
  0.0 1.8 %copy.12 = f32[8,16,8,256]{3,0,1,2:T(8,128)S(1)} copy(f32[8,16,8,256]{3,2,1,0:T(8,128)} %param.6) | data formatting | bytes 2097152 | tf_op args[0]
  1.8 0.0 copy-start
  1.9 0.0 copy-start.1
  1.9 0.0 copy-start.2
  1.9 1.3 %fusion.1 = (f32[6,16,8,256]{3,2,1,0:T(8,128)}, f32[6,16,8,256]{3,2,1,0:T(8,128)}) fusion(f32[8,16,8,256]{3,2,1,0:T(8,128)S(1)} %bitcast.10), kind=kLoop, calls=%fused_computation.5 | loop fusion | bytes 3145728 | tf_op jit(solution)/shard_map/slice | solution.py:139
  3.2 0.1 copy-done
  3.3 0.0 copy-start.4
  3.3 0.7 copy-done.4
  4.0 0.7 fusion
  5.4 0.1 pad.2.clone
  5.5 0.0 copy-done.1
  5.5 0.0 copy-done.2
  5.5 0.9 maximum_select_fusion.masked
  6.3 0.0 copy-start.3
  6.3 78.6 %shard_map.64 = (f32[48,8,256]{2,1,0:T(8,128)}, f32[6,16,8,256]{3,2,1,0:T(8,128)}, f32[6,16,8,256]{3,2,1,0:T(8,128)}, f32[32,8,256]{2,1,0:T(8,128)}, f32[32,8,256]{2,1,0:T(8,128)}) custom-call(f32[48,8,256]{2,1,0:T(8,128)} %maximum_select_fusion.masked, f32[6,16,8,256]{3,2,1,0:T(8,128)} %get-tuple-element.16.up, f32[6,16,8,256]{3,2,1,0:T(8,128)} %get-tuple-element.15.down), custom_call_target="tpu_custom_call" | custom-call | tf_op jit(solution)/shard_map/pallas_call | solution.py:127
  85.0 0.0 copy-done.3
  85.0 0.6 copy.13
  85.6 17.6 %shard_map.65 = f32[8,16,8,256]{3,2,1,0:T(8,128)} custom-call(s32[16]{0:T(128)} %substeps.1, f32[8,16,8,256]{3,2,1,0:T(8,128)} %bitcast.11, f32[6,16,8,256]{3,2,1,0:T(8,128)} %get-tuple-element.10.south, f32[6,16,8,256]{3,2,1,0:T(8,128)} %get-tuple-element.11.north, f32[48,8,256]{2,1,0:T(8,128)} %get-tuple-element.12.chosen, ...), custom_call_target="tpu_custom_call" | custom-call | flops 35782656 | bytes 4063232 | tf_op jit(solution)/shard_map/pallas_call | solution.py:258
  103.2 2.8 %copy.9 = f32[8,16,8,256]{3,2,1,0:T(8,128)} copy(f32[8,16,8,256]{3,0,1,2:T(8,128)} %bitcast.12) | data formatting | bytes 2097152 | tf_op jit(solution)/shard_map/transpose | solution.py:300
Async XLA Ops:
  1.8 1.5 %copy-start = (f32[8,16,8,256]{3,0,1,2:T(8,128)}, f32[8,16,8,256]{3,0,1,2:T(8,128)S(1)}, u32[]{:S(2)}) copy-start(f32[8,16,8,256]{3,0,1,2:T(8,128)S(1)} %copy.12) | copy-start | bytes 3145732
  1.9 3.6 %copy-start.1 = (f32[1,2,16,8,256]{4,3,2,1,0:T(8,128)S(1)}, f32[1,2,16,8,256]{4,3,2,1,0:T(8,128)}, u32[]{:S(2)}) copy-start(f32[1,2,16,8,256]{4,3,2,1,0:T(8,128)} %param.8) | copy-start | bytes 786436
  1.9 3.6 %copy-start.2 = (f32[1,15,8,256]{3,2,1,0:T(8,128)S(1)}, f32[1,15,8,256]{3,2,1,0:T(8,128)}, u32[]{:S(2)}) copy-start(f32[1,15,8,256]{3,2,1,0:T(8,128)} %param.9) | copy-start | bytes 368644
  3.3 0.7 copy-start.4
  6.3 78.7 %copy-start.3 = (f32[8,8,256]{2,1,0:T(8,128)S(1)}, f32[8,8,256]{2,1,0:T(8,128)}, u32[]{:S(2)}) copy-start(f32[8,8,256]{2,1,0:T(8,128)} %param.7) | copy-start | bytes 196612

commit v9 on v8

--- a/solution.py
+++ b/solution.py
@@ -52,14 +52,6 @@
             recv_sem=recv_sems.at[slot], device_id=(tile + by, me), device_id_type=mesh,
         )
 
-    @pl.when(tile < tiles - 1)
-    def _():
-        along_tile(up, south, 0, 1).start()
-
-    @pl.when(tile > 0)
-    def _():
-        along_tile(down, north, 1, -1).start()
-
     @pl.when(tile == 0)
     def _():
         south[...] = jnp.zeros_like(south)
@@ -84,6 +76,14 @@
     for bit in range(1, bits):
         along_group(total, bit, bit)
         total[...] = total[...] + received[bit]
+        if bit == 1:
+            @pl.when(tile < tiles - 1)
+            def _():
+                along_tile(up, south, 0, 1).start()
+
+            @pl.when(tile > 0)
+            def _():
+                along_tile(down, north, 1, -1).start()
     along_group(total, 0, bits)
     chosen[pl.ds(core * half, half)] = total[...]
     chosen[pl.ds((1 - core) * half, half)] = received[bits]

time: 106 us -> 91 us (0.86)
  Pallas kernels: 96.2 us -> 80.7 us
    pallas_call x1, Pallas kernels: 78.6 us -> 63.2 us  [exchange(): pl.pallas_call(exchange_kernel, out_shape=(jax.ShapeDtypeStruct(padded.sh...]
where the time goes in v9:
time: 91 us; the launch traced here: 90.5 us
  Pallas kernels  80.7 us (89%)
  local copies, waits for them, and re-layouts  7.48 us (8%)
  other arithmetic  1.57 us (2%)
    pallas_call x1, Pallas kernels, exchange(): pl.pallas_call(exchange_kernel, out_shape=(jax.ShapeDtypeStruct(padded.sh...  63.2 us
    pallas_call x1, Pallas kernels, transport(): pl.pallas_call(transport_kernel, out_shape=jax.ShapeDtypeStruct(own.shape...  17.6 us
    unnamed x12, local copies, waits for them, and re-layouts  3.29 us
    transpose x1, local copies, waits for them, and re-layouts, shards(): return jnp.transpose(mixed, (2, 1, 0, 3))  2.8 us

profile of v9, /device:TPU:161, one launch (start us, length us, event | category | flops | bytes accessed | tf_op | source)
XLA Modules:
  0.0 90.5 jit_solution(12692263696019787587)
XLA Ops:
  0.0 1.8 %copy.12 = f32[8,16,8,256]{3,0,1,2:T(8,128)S(1)} copy(f32[8,16,8,256]{3,2,1,0:T(8,128)} %param.6) | data formatting | bytes 2097152 | tf_op args[0]
  1.8 0.0 copy-start
  1.9 0.0 copy-start.1
  1.9 0.0 copy-start.2
  1.9 1.3 %fusion.1 = (f32[6,16,8,256]{3,2,1,0:T(8,128)}, f32[6,16,8,256]{3,2,1,0:T(8,128)}) fusion(f32[8,16,8,256]{3,2,1,0:T(8,128)S(1)} %bitcast.10), kind=kLoop, calls=%fused_computation.5 | loop fusion | bytes 3145728 | tf_op jit(solution)/shard_map/slice | solution.py:139
  3.2 0.1 copy-done
  3.3 0.0 copy-start.4
  3.3 0.7 copy-done.4
  4.0 0.7 fusion
  5.4 0.1 pad.2.clone
  5.5 0.0 copy-done.1
  5.5 0.0 copy-done.2
  5.5 0.9 maximum_select_fusion.masked
  6.3 0.0 copy-start.3
  6.3 63.2 %shard_map.64 = (f32[48,8,256]{2,1,0:T(8,128)}, f32[6,16,8,256]{3,2,1,0:T(8,128)}, f32[6,16,8,256]{3,2,1,0:T(8,128)}, f32[32,8,256]{2,1,0:T(8,128)}, f32[32,8,256]{2,1,0:T(8,128)}) custom-call(f32[48,8,256]{2,1,0:T(8,128)} %maximum_select_fusion.masked, f32[6,16,8,256]{3,2,1,0:T(8,128)} %get-tuple-element.16.up, f32[6,16,8,256]{3,2,1,0:T(8,128)} %get-tuple-element.15.down), custom_call_target="tpu_custom_call" | custom-call | tf_op jit(solution)/shard_map/pallas_call | solution.py:127
  69.5 0.0 copy-done.3
  69.5 0.6 copy.13
  70.2 17.6 %shard_map.65 = f32[8,16,8,256]{3,2,1,0:T(8,128)} custom-call(s32[16]{0:T(128)} %substeps.1, f32[8,16,8,256]{3,2,1,0:T(8,128)} %bitcast.11, f32[6,16,8,256]{3,2,1,0:T(8,128)} %get-tuple-element.10.south, f32[6,16,8,256]{3,2,1,0:T(8,128)} %get-tuple-element.11.north, f32[48,8,256]{2,1,0:T(8,128)} %get-tuple-element.12.chosen, ...), custom_call_target="tpu_custom_call" | custom-call | flops 35782656 | bytes 4063232 | tf_op jit(solution)/shard_map/pallas_call | solution.py:258
  87.7 2.8 %copy.9 = f32[8,16,8,256]{3,2,1,0:T(8,128)} copy(f32[8,16,8,256]{3,0,1,2:T(8,128)} %bitcast.12) | data formatting | bytes 2097152 | tf_op jit(solution)/shard_map/transpose | solution.py:300
Async XLA Ops:
  1.8 1.5 %copy-start = (f32[8,16,8,256]{3,0,1,2:T(8,128)}, f32[8,16,8,256]{3,0,1,2:T(8,128)S(1)}, u32[]{:S(2)}) copy-start(f32[8,16,8,256]{3,0,1,2:T(8,128)S(1)} %copy.12) | copy-start | bytes 3145732
  1.9 3.6 %copy-start.1 = (f32[1,2,16,8,256]{4,3,2,1,0:T(8,128)S(1)}, f32[1,2,16,8,256]{4,3,2,1,0:T(8,128)}, u32[]{:S(2)}) copy-start(f32[1,2,16,8,256]{4,3,2,1,0:T(8,128)} %param.8) | copy-start | bytes 786436
  1.9 3.6 %copy-start.2 = (f32[1,15,8,256]{3,2,1,0:T(8,128)S(1)}, f32[1,15,8,256]{3,2,1,0:T(8,128)}, u32[]{:S(2)}) copy-start(f32[1,15,8,256]{3,2,1,0:T(8,128)} %param.9) | copy-start | bytes 368644
  3.3 0.7 copy-start.4
  6.3 63.2 %copy-start.3 = (f32[8,8,256]{2,1,0:T(8,128)S(1)}, f32[8,8,256]{2,1,0:T(8,128)}, u32[]{:S(2)}) copy-start(f32[8,8,256]{2,1,0:T(8,128)} %param.7) | copy-start | bytes 196612

commit v10 on v9

--- a/solution.py
+++ b/solution.py
@@ -76,7 +76,7 @@
     for bit in range(1, bits):
         along_group(total, bit, bit)
         total[...] = total[...] + received[bit]
-        if bit == 1:
+        if bit == 2:
             @pl.when(tile < tiles - 1)
             def _():
                 along_tile(up, south, 0, 1).start()

time: 91 us -> 96.5 us (1.060)
  Pallas kernels: 80.7 us -> 85.6 us
    pallas_call x1, Pallas kernels: 63.2 us -> 68 us  [exchange(): pl.pallas_call(exchange_kernel, out_shape=(jax.ShapeDtypeStruct(padded.sh...]
where the time goes in v10:
time: 96.5 us; the launch traced here: 95.4 us
  Pallas kernels  85.6 us (89%)
  local copies, waits for them, and re-layouts  7.48 us (8%)
  other arithmetic  1.57 us (2%)
    pallas_call x1, Pallas kernels, exchange(): pl.pallas_call(exchange_kernel, out_shape=(jax.ShapeDtypeStruct(padded.sh...  68 us
    pallas_call x1, Pallas kernels, transport(): pl.pallas_call(transport_kernel, out_shape=jax.ShapeDtypeStruct(own.shape...  17.6 us
    unnamed x12, local copies, waits for them, and re-layouts  3.29 us
    transpose x1, local copies, waits for them, and re-layouts, shards(): return jnp.transpose(mixed, (2, 1, 0, 3))  2.8 us

profile of v10, /device:TPU:161, one launch (start us, length us, event | category | flops | bytes accessed | tf_op | source)
XLA Modules:
  0.0 95.4 jit_solution(5689538238115000391)
XLA Ops:
  0.0 1.8 %copy.12 = f32[8,16,8,256]{3,0,1,2:T(8,128)S(1)} copy(f32[8,16,8,256]{3,2,1,0:T(8,128)} %param.6) | data formatting | bytes 2097152 | tf_op args[0]
  1.8 0.0 copy-start
  1.9 0.0 copy-start.1
  1.9 0.0 copy-start.2
  1.9 1.3 %fusion.1 = (f32[6,16,8,256]{3,2,1,0:T(8,128)}, f32[6,16,8,256]{3,2,1,0:T(8,128)}) fusion(f32[8,16,8,256]{3,2,1,0:T(8,128)S(1)} %bitcast.10), kind=kLoop, calls=%fused_computation.5 | loop fusion | bytes 3145728 | tf_op jit(solution)/shard_map/slice | solution.py:139
  3.2 0.1 copy-done
  3.3 0.0 copy-start.4
  3.3 0.7 copy-done.4
  4.0 0.7 fusion
  5.4 0.1 pad.2.clone
  5.5 0.0 copy-done.1
  5.5 0.0 copy-done.2
  5.5 0.9 maximum_select_fusion.masked
  6.3 0.0 copy-start.3
  6.3 68.0 %shard_map.64 = (f32[48,8,256]{2,1,0:T(8,128)}, f32[6,16,8,256]{3,2,1,0:T(8,128)}, f32[6,16,8,256]{3,2,1,0:T(8,128)}, f32[32,8,256]{2,1,0:T(8,128)}, f32[32,8,256]{2,1,0:T(8,128)}) custom-call(f32[48,8,256]{2,1,0:T(8,128)} %maximum_select_fusion.masked, f32[6,16,8,256]{3,2,1,0:T(8,128)} %get-tuple-element.16.up, f32[6,16,8,256]{3,2,1,0:T(8,128)} %get-tuple-element.15.down), custom_call_target="tpu_custom_call" | custom-call | tf_op jit(solution)/shard_map/pallas_call | solution.py:127
  74.3 0.0 copy-done.3
  74.4 0.6 copy.13
  75.0 17.6 %shard_map.65 = f32[8,16,8,256]{3,2,1,0:T(8,128)} custom-call(s32[16]{0:T(128)} %substeps.1, f32[8,16,8,256]{3,2,1,0:T(8,128)} %bitcast.11, f32[6,16,8,256]{3,2,1,0:T(8,128)} %get-tuple-element.10.south, f32[6,16,8,256]{3,2,1,0:T(8,128)} %get-tuple-element.11.north, f32[48,8,256]{2,1,0:T(8,128)} %get-tuple-element.12.chosen, ...), custom_call_target="tpu_custom_call" | custom-call | flops 35782656 | bytes 4063232 | tf_op jit(solution)/shard_map/pallas_call | solution.py:258
  92.6 2.8 %copy.9 = f32[8,16,8,256]{3,2,1,0:T(8,128)} copy(f32[8,16,8,256]{3,0,1,2:T(8,128)} %bitcast.12) | data formatting | bytes 2097152 | tf_op jit(solution)/shard_map/transpose | solution.py:300
Async XLA Ops:
  1.8 1.5 %copy-start = (f32[8,16,8,256]{3,0,1,2:T(8,128)}, f32[8,16,8,256]{3,0,1,2:T(8,128)S(1)}, u32[]{:S(2)}) copy-start(f32[8,16,8,256]{3,0,1,2:T(8,128)S(1)} %copy.12) | copy-start | bytes 3145732
  1.9 3.6 %copy-start.1 = (f32[1,2,16,8,256]{4,3,2,1,0:T(8,128)S(1)}, f32[1,2,16,8,256]{4,3,2,1,0:T(8,128)}, u32[]{:S(2)}) copy-start(f32[1,2,16,8,256]{4,3,2,1,0:T(8,128)} %param.8) | copy-start | bytes 786436
  1.9 3.6 %copy-start.2 = (f32[1,15,8,256]{3,2,1,0:T(8,128)S(1)}, f32[1,15,8,256]{3,2,1,0:T(8,128)}, u32[]{:S(2)}) copy-start(f32[1,15,8,256]{3,2,1,0:T(8,128)} %param.9) | copy-start | bytes 368644
  3.3 0.7 copy-start.4
  6.3 68.0 %copy-start.3 = (f32[8,8,256]{2,1,0:T(8,128)S(1)}, f32[8,8,256]{2,1,0:T(8,128)}, u32[]{:S(2)}) copy-start(f32[8,8,256]{2,1,0:T(8,128)} %param.7) | copy-start | bytes 196612

commit v11 on v9

--- a/solution.py
+++ b/solution.py
@@ -141,7 +141,7 @@
 
 def transport_kernel(
     substeps, own, south, north, chosen, south_courant, north_courant, emissions, out,
-    held, pivots, ratios, lowers, planes, fractions,
+    held, pivots, ratios, lowers, planes, fractions, winds,
 ):
     levels, height, tracer_count, width = held.shape
     halo = south.shape[0]
@@ -186,7 +186,7 @@
 
     _prepare()
 
-    def advect(level, carry):
+    def prepare_winds(level, carry):
         def wind_row(component, row):
             index = component * levels + level
             if row < halo:
@@ -196,16 +196,22 @@
             return spread(north_courant.at[index], row - halo - height)
 
         first_row = jnp.where(tile_position > 0, jnp.float32(1.0), jnp.float32(0.0))
-        zonal_up, zonal_down, merid_up, merid_down = [], [], [], []
         for row in range(rows):
             zonal = wind_row(0, row)
             meridional = wind_row(1, row)
             if row == halo:
                 meridional = meridional * first_row
-            zonal_up.append(jnp.maximum(zonal, 0.0))
-            zonal_down.append(jnp.minimum(zonal, 0.0))
-            merid_up.append(jnp.maximum(meridional, 0.0))
-            merid_down.append(jnp.minimum(meridional, 0.0))
+            winds[level, row, 0] = jnp.maximum(zonal, 0.0)
+            winds[level, row, 1] = jnp.minimum(zonal, 0.0)
+            winds[level, row, 2] = jnp.maximum(meridional, 0.0)
+            winds[level, row, 3] = jnp.minimum(meridional, 0.0)
+        return carry
+
+    lax.fori_loop(0, levels, prepare_winds, 0)
+
+    def advect(level, carry):
+        def wind(row, part):
+            return winds[level, row, part]
 
         mixing = [south[row, level] for row in range(halo)]
         mixing += [own[row, level] for row in range(height)]
@@ -214,13 +220,13 @@
             low, high = substep + 1, rows - 2 - substep
             south_flux = {}
             for row in range(low, high + 2):
-                south_flux[row] = merid_up[row] * mixing[row - 1] + merid_down[row] * mixing[row]
+                south_flux[row] = wind(row, 2) * mixing[row - 1] + wind(row, 3) * mixing[row]
             advanced = list(mixing)
             for row in range(low, high + 1):
                 band = 0 if row < halo else (1 if row < halo + height else 2)
                 fraction = fractions[3 * substep + band]
                 from_west = pltpu.roll(mixing[row], 1, 1)
-                west_flux = zonal_up[row] * from_west + zonal_down[row] * mixing[row]
+                west_flux = wind(row, 0) * from_west + wind(row, 1) * mixing[row]
                 east_flux = pltpu.roll(west_flux, width - 1, 1)
                 advanced[row] = mixing[row] - fraction * (
                     (east_flux - west_flux) + (south_flux[row + 1] - south_flux[row])
@@ -267,6 +273,7 @@
             table,
             pltpu.VMEM((3, height, width), jnp.float32),
             pltpu.VMEM((3 * ROUNDS, tracer_count, width), jnp.float32),
+            pltpu.VMEM((levels, height + 2 * south.shape[0], 4, tracer_count, width), jnp.float32),
         ],
         cost_estimate=pl.CostEstimate(
             flops=levels * tracer_count * width * 78 * 14,

time: 91 us -> 91.8 us (level)
  no operation moved by 1% of the time
where the time goes in v11:
time: 91.8 us; the launch traced here: 91.3 us
  Pallas kernels  81.6 us (89%)
  local copies, waits for them, and re-layouts  7.48 us (8%)
  other arithmetic  1.57 us (2%)
    pallas_call x1, Pallas kernels, exchange(): pl.pallas_call(exchange_kernel, out_shape=(jax.ShapeDtypeStruct(padded.sh...  63.2 us
    pallas_call x1, Pallas kernels, transport(): pl.pallas_call(transport_kernel, out_shape=jax.ShapeDtypeStruct(own.shape...  18.4 us
    unnamed x12, local copies, waits for them, and re-layouts  3.29 us
    transpose x1, local copies, waits for them, and re-layouts, shards(): return jnp.transpose(mixed, (2, 1, 0, 3))  2.8 us

profile of v11, /device:TPU:161, one launch (start us, length us, event | category | flops | bytes accessed | tf_op | source)
XLA Modules:
  0.0 91.3 jit_solution(14846095013528013250)
XLA Ops:
  0.0 1.8 %copy.12 = f32[8,16,8,256]{3,0,1,2:T(8,128)S(1)} copy(f32[8,16,8,256]{3,2,1,0:T(8,128)} %param.6) | data formatting | bytes 2097152 | tf_op args[0]
  1.8 0.0 copy-start
  1.9 0.0 copy-start.1
  1.9 0.0 copy-start.2
  1.9 1.3 %fusion.1 = (f32[6,16,8,256]{3,2,1,0:T(8,128)}, f32[6,16,8,256]{3,2,1,0:T(8,128)}) fusion(f32[8,16,8,256]{3,2,1,0:T(8,128)S(1)} %bitcast.10), kind=kLoop, calls=%fused_computation.5 | loop fusion | bytes 3145728 | tf_op jit(solution)/shard_map/slice | solution.py:139
  3.2 0.1 copy-done
  3.3 0.0 copy-start.4
  3.3 0.7 copy-done.4
  4.0 0.7 fusion
  5.4 0.1 pad.2.clone
  5.5 0.0 copy-done.1
  5.5 0.0 copy-done.2
  5.5 0.9 maximum_select_fusion.masked
  6.3 0.0 copy-start.3
  6.3 63.2 %shard_map.64 = (f32[48,8,256]{2,1,0:T(8,128)}, f32[6,16,8,256]{3,2,1,0:T(8,128)}, f32[6,16,8,256]{3,2,1,0:T(8,128)}, f32[32,8,256]{2,1,0:T(8,128)}, f32[32,8,256]{2,1,0:T(8,128)}) custom-call(f32[48,8,256]{2,1,0:T(8,128)} %maximum_select_fusion.masked, f32[6,16,8,256]{3,2,1,0:T(8,128)} %get-tuple-element.16.up, f32[6,16,8,256]{3,2,1,0:T(8,128)} %get-tuple-element.15.down), custom_call_target="tpu_custom_call" | custom-call | tf_op jit(solution)/shard_map/pallas_call | solution.py:127
  69.5 0.0 copy-done.3
  69.5 0.6 copy.13
  70.2 18.4 %shard_map.65 = f32[8,16,8,256]{3,2,1,0:T(8,128)} custom-call(s32[16]{0:T(128)} %substeps.1, f32[8,16,8,256]{3,2,1,0:T(8,128)} %bitcast.11, f32[6,16,8,256]{3,2,1,0:T(8,128)} %get-tuple-element.10.south, f32[6,16,8,256]{3,2,1,0:T(8,128)} %get-tuple-element.11.north, f32[48,8,256]{2,1,0:T(8,128)} %get-tuple-element.12.chosen, ...), custom_call_target="tpu_custom_call" | custom-call | flops 35782656 | bytes 4063232 | tf_op jit(solution)/shard_map/pallas_call | solution.py:264
  88.5 2.8 %copy.9 = f32[8,16,8,256]{3,2,1,0:T(8,128)} copy(f32[8,16,8,256]{3,0,1,2:T(8,128)} %bitcast.12) | data formatting | bytes 2097152 | tf_op jit(solution)/shard_map/transpose | solution.py:307
Async XLA Ops:
  1.8 1.5 %copy-start = (f32[8,16,8,256]{3,0,1,2:T(8,128)}, f32[8,16,8,256]{3,0,1,2:T(8,128)S(1)}, u32[]{:S(2)}) copy-start(f32[8,16,8,256]{3,0,1,2:T(8,128)S(1)} %copy.12) | copy-start | bytes 3145732
  1.9 3.6 %copy-start.1 = (f32[1,2,16,8,256]{4,3,2,1,0:T(8,128)S(1)}, f32[1,2,16,8,256]{4,3,2,1,0:T(8,128)}, u32[]{:S(2)}) copy-start(f32[1,2,16,8,256]{4,3,2,1,0:T(8,128)} %param.8) | copy-start | bytes 786436
  1.9 3.6 %copy-start.2 = (f32[1,15,8,256]{3,2,1,0:T(8,128)S(1)}, f32[1,15,8,256]{3,2,1,0:T(8,128)}, u32[]{:S(2)}) copy-start(f32[1,15,8,256]{3,2,1,0:T(8,128)} %param.9) | copy-start | bytes 368644
  3.3 0.7 copy-start.4
  6.3 63.2 %copy-start.3 = (f32[8,8,256]{2,1,0:T(8,128)S(1)}, f32[8,8,256]{2,1,0:T(8,128)}, u32[]{:S(2)}) copy-start(f32[8,8,256]{2,1,0:T(8,128)} %param.7) | copy-start | bytes 196612

commit v12 on v9

--- a/solution.py
+++ b/solution.py
@@ -26,6 +26,8 @@
     core = me % 2
     half = masked.shape[0] // 2
     planes = south_courant.shape[0]
+    halo = south_courant.shape[1]
+    rows_from = chosen.shape[1] - halo
 
     def partner(bit):
         return me + (1 << bit) * (1 - 2 * ((me // (1 << bit)) % 2))
@@ -90,25 +92,25 @@
 
     @pl.when(tile < tiles - 1)
     def _():
-        along_tile(chosen.at[pl.ds(0, planes)], south_courant, 2 + bits + 1, 1).start()
+        along_tile(chosen.at[pl.ds(0, planes), pl.ds(rows_from, halo)], south_courant, 2 + bits + 1, 1).start()
 
     @pl.when(tile > 0)
     def _():
-        along_tile(chosen.at[pl.ds(0, planes)], north_courant, 2 + bits + 2, -1).start()
+        along_tile(chosen.at[pl.ds(0, planes), pl.ds(0, halo)], north_courant, 2 + bits + 2, -1).start()
 
     @pl.when(tile < tiles - 1)
     def _():
         along_tile(up, south, 0, 1).wait_send()
-        along_tile(chosen.at[pl.ds(0, planes)], south_courant, 2 + bits + 1, 1).wait_send()
+        along_tile(chosen.at[pl.ds(0, planes), pl.ds(rows_from, halo)], south_courant, 2 + bits + 1, 1).wait_send()
         along_tile(up, north, 1, 1).wait_recv()
-        along_tile(chosen.at[pl.ds(0, planes)], north_courant, 2 + bits + 2, 1).wait_recv()
+        along_tile(chosen.at[pl.ds(0, planes), pl.ds(0, halo)], north_courant, 2 + bits + 2, 1).wait_recv()
 
     @pl.when(tile > 0)
     def _():
         along_tile(down, north, 1, -1).wait_send()
-        along_tile(chosen.at[pl.ds(0, planes)], north_courant, 2 + bits + 2, -1).wait_send()
+        along_tile(chosen.at[pl.ds(0, planes), pl.ds(0, halo)], north_courant, 2 + bits + 2, -1).wait_send()
         along_tile(down, south, 0, -1).wait_recv()
-        along_tile(chosen.at[pl.ds(0, planes)], south_courant, 2 + bits + 1, -1).wait_recv()
+        along_tile(chosen.at[pl.ds(0, planes), pl.ds(rows_from, halo)], south_courant, 2 + bits + 1, -1).wait_recv()
 
 
 def exchange(value, by_row, root, halo, planes):
@@ -123,7 +125,7 @@
     height = by_row.shape[0]
     vmem = pl.BlockSpec(memory_space=pltpu.VMEM)
     rows = jax.ShapeDtypeStruct((halo,) + by_row.shape[1:], by_row.dtype)
-    winds = jax.ShapeDtypeStruct((planes,) + value.shape[1:], value.dtype)
+    winds = jax.ShapeDtypeStruct((planes, halo) + value.shape[2:], value.dtype)
     return pl.pallas_call(
         exchange_kernel,
         out_shape=(jax.ShapeDtypeStruct(padded.shape, padded.dtype), rows, rows, winds, winds),
@@ -190,7 +192,7 @@
         def wind_row(component, row):
             index = component * levels + level
             if row < halo:
-                return spread(south_courant.at[index], row + height - halo)
+                return spread(south_courant.at[index], row)
             if row < halo + height:
                 return spread(courant.at[index], row - halo)
             return spread(north_courant.at[index], row - halo - height)

time: 91 us -> 88.2 us (0.969)
  Pallas kernels: 80.7 us -> 77.9 us
    pallas_call x1, Pallas kernels: 63.2 us -> 60.4 us  [exchange(): pl.pallas_call(exchange_kernel, out_shape=(jax.ShapeDtypeStruct(padded.sh...]
where the time goes in v12:
time: 88.2 us; the launch traced here: 87.7 us
  Pallas kernels  77.9 us (88%)
  local copies, waits for them, and re-layouts  7.48 us (8%)
  other arithmetic  1.57 us (2%)
    pallas_call x1, Pallas kernels, exchange(): pl.pallas_call(exchange_kernel, out_shape=(jax.ShapeDtypeStruct(padded.sh...  60.4 us
    pallas_call x1, Pallas kernels, transport(): pl.pallas_call(transport_kernel, out_shape=jax.ShapeDtypeStruct(own.shape...  17.6 us
    unnamed x12, local copies, waits for them, and re-layouts  3.29 us
    transpose x1, local copies, waits for them, and re-layouts, shards(): return jnp.transpose(mixed, (2, 1, 0, 3))  2.8 us

profile of v12, /device:TPU:161, one launch (start us, length us, event | category | flops | bytes accessed | tf_op | source)
XLA Modules:
  0.0 87.7 jit_solution(8154654870893372613)
XLA Ops:
  0.0 1.8 %copy.12 = f32[8,16,8,256]{3,0,1,2:T(8,128)S(1)} copy(f32[8,16,8,256]{3,2,1,0:T(8,128)} %param.6) | data formatting | bytes 2097152 | tf_op args[0]
  1.8 0.0 copy-start
  1.9 0.0 copy-start.1
  1.9 0.0 copy-start.2
  1.9 1.3 %fusion.1 = (f32[6,16,8,256]{3,2,1,0:T(8,128)}, f32[6,16,8,256]{3,2,1,0:T(8,128)}) fusion(f32[8,16,8,256]{3,2,1,0:T(8,128)S(1)} %bitcast.10), kind=kLoop, calls=%fused_computation.5 | loop fusion | bytes 3145728 | tf_op jit(solution)/shard_map/slice | solution.py:141
  3.2 0.1 copy-done
  3.3 0.0 copy-start.4
  3.3 0.7 copy-done.4
  4.0 0.7 fusion
  5.4 0.1 pad.2.clone
  5.5 0.0 copy-done.1
  5.5 0.0 copy-done.2
  5.5 0.9 maximum_select_fusion.masked
  6.3 0.0 copy-start.3
  6.3 60.4 %shard_map.64 = (f32[48,8,256]{2,1,0:T(8,128)}, f32[6,16,8,256]{3,2,1,0:T(8,128)}, f32[6,16,8,256]{3,2,1,0:T(8,128)}, f32[32,6,256]{2,1,0:T(8,128)}, f32[32,6,256]{2,1,0:T(8,128)}) custom-call(f32[48,8,256]{2,1,0:T(8,128)} %maximum_select_fusion.masked, f32[6,16,8,256]{3,2,1,0:T(8,128)} %get-tuple-element.16.up, f32[6,16,8,256]{3,2,1,0:T(8,128)} %get-tuple-element.15.down), custom_call_target="tpu_custom_call" | custom-call | tf_op jit(solution)/shard_map/pallas_call | solution.py:129
  66.7 0.0 copy-done.3
  66.7 0.6 copy.13
  67.4 17.6 %shard_map.65 = f32[8,16,8,256]{3,2,1,0:T(8,128)} custom-call(s32[16]{0:T(128)} %substeps.1, f32[8,16,8,256]{3,2,1,0:T(8,128)} %bitcast.11, f32[6,16,8,256]{3,2,1,0:T(8,128)} %get-tuple-element.10.south, f32[6,16,8,256]{3,2,1,0:T(8,128)} %get-tuple-element.11.north, f32[48,8,256]{2,1,0:T(8,128)} %get-tuple-element.12.chosen, ...), custom_call_target="tpu_custom_call" | custom-call | flops 35782656 | bytes 4063232 | tf_op jit(solution)/shard_map/pallas_call | solution.py:260
  84.9 2.8 %copy.9 = f32[8,16,8,256]{3,2,1,0:T(8,128)} copy(f32[8,16,8,256]{3,0,1,2:T(8,128)} %bitcast.12) | data formatting | bytes 2097152 | tf_op jit(solution)/shard_map/transpose | solution.py:302
Async XLA Ops:
  1.8 1.5 %copy-start = (f32[8,16,8,256]{3,0,1,2:T(8,128)}, f32[8,16,8,256]{3,0,1,2:T(8,128)S(1)}, u32[]{:S(2)}) copy-start(f32[8,16,8,256]{3,0,1,2:T(8,128)S(1)} %copy.12) | copy-start | bytes 3145732
  1.9 3.6 %copy-start.1 = (f32[1,2,16,8,256]{4,3,2,1,0:T(8,128)S(1)}, f32[1,2,16,8,256]{4,3,2,1,0:T(8,128)}, u32[]{:S(2)}) copy-start(f32[1,2,16,8,256]{4,3,2,1,0:T(8,128)} %param.8) | copy-start | bytes 786436
  1.9 3.6 %copy-start.2 = (f32[1,15,8,256]{3,2,1,0:T(8,128)S(1)}, f32[1,15,8,256]{3,2,1,0:T(8,128)}, u32[]{:S(2)}) copy-start(f32[1,15,8,256]{3,2,1,0:T(8,128)} %param.9) | copy-start | bytes 368644
  3.3 0.7 copy-start.4
  6.3 60.4 %copy-start.3 = (f32[8,8,256]{2,1,0:T(8,128)S(1)}, f32[8,8,256]{2,1,0:T(8,128)}, u32[]{:S(2)}) copy-start(f32[8,8,256]{2,1,0:T(8,128)} %param.7) | copy-start | bytes 196612

commit v13 on v12

--- a/solution.py
+++ b/solution.py
@@ -15,7 +15,7 @@
 
 
 def exchange_kernel(
-    masked, up, down, chosen, south, north, south_courant, north_courant,
+    masked, by_row, chosen, south, north, south_courant, north_courant,
     total, received, send_sems, recv_sems,
 ):
     mesh = pl.DeviceIdType.MESH
@@ -28,6 +28,8 @@
     planes = south_courant.shape[0]
     halo = south_courant.shape[1]
     rows_from = chosen.shape[1] - halo
+    up = by_row.at[pl.ds(by_row.shape[0] - halo, halo)]
+    down = by_row.at[pl.ds(0, halo)]
 
     def partner(bit):
         return me + (1 << bit) * (1 - 2 * ((me // (1 << bit)) % 2))
@@ -129,7 +131,7 @@
     return pl.pallas_call(
         exchange_kernel,
         out_shape=(jax.ShapeDtypeStruct(padded.shape, padded.dtype), rows, rows, winds, winds),
-        in_specs=[vmem] * 3,
+        in_specs=[vmem] * 2,
         out_specs=(vmem,) * 5,
         scratch_shapes=[
             pltpu.VMEM((half,) + value.shape[1:], value.dtype),
@@ -138,7 +140,7 @@
             pltpu.SemaphoreType.DMA((bits + 5,)),
         ],
         compiler_params=pltpu.CompilerParams(collective_id=0, has_side_effects=True),
-    )(masked, by_row[height - halo :], by_row[:halo])
+    )(masked, by_row)
 
 
 def transport_kernel(

time: 88.2 us -> 89.3 us (1.012)
  other arithmetic: 1.57 us -> 3.13 us
    slice x1 -> x0, local copies, waits for them, and re-layouts: 1.31 us -> none  [exchange(): by_row[:halo]]
    unnamed x12 -> x4, local copies, waits for them, and re-layouts: 3.29 us -> 4.28 us
    select_n x1, other arithmetic: 0.86 us -> 1.81 us  [exchange(): jnp.where(lax.axis_index('group') == root, padded, jnp.zeros_like(padded))]
where the time goes in v13:
time: 89.3 us; the launch traced here: 88.8 us
  Pallas kernels  77.8 us (87%)
  local copies, waits for them, and re-layouts  7.16 us (8%)
  other arithmetic  3.13 us (4%)
    pallas_call x1, Pallas kernels, exchange(): pl.pallas_call(exchange_kernel, out_shape=(jax.ShapeDtypeStruct(padded.sh...  60.2 us
    pallas_call x1, Pallas kernels, transport(): pl.pallas_call(transport_kernel, out_shape=jax.ShapeDtypeStruct(own.shape...  17.6 us
    unnamed x4, local copies, waits for them, and re-layouts  4.28 us
    transpose x1, local copies, waits for them, and re-layouts, shards(): return jnp.transpose(mixed, (2, 1, 0, 3))  2.8 us
    select_n x1, other arithmetic, exchange(): jnp.where(lax.axis_index('group') == root, padded, jnp.zeros_like(padded))  1.81 us

profile of v13, /device:TPU:161, one launch (start us, length us, event | category | flops | bytes accessed | tf_op | source)
XLA Modules:
  0.0 88.8 jit_solution(7857208351700450213)
XLA Ops:
  0.0 0.0 copy-start
  0.0 1.3 %fusion = s32[]{:T(128)} fusion(s32[16]{0:T(128)} %param.11, s32[]{:T(128)S(6)} %axis_index.25), kind=kLoop, calls=%fused_computation.4 | loop fusion | flops 47 | bytes 72 | tf_op jit(solution)/shard_map/reduce_sum | solution.py:287
  2.0 0.1 pad.2.clone
  2.1 1.5 %copy.13 = f32[8,8,256]{2,0,1:T(8,128)} copy(f32[8,8,256]{2,1,0:T(8,128)} %param.7) | data formatting | bytes 131072 | tf_op args[1]
  3.5 0.0 copy-done
  3.5 1.8 %maximum_select_fusion.masked = f32[48,8,256]{2,1,0:T(8,128)} fusion(f32[15,8,256]{2,1,0:T(8,128)S(1)} %bitcast.15, f32[32,8,256]{2,1,0:T(8,128)} %bitcast.14, f32[48]{0:T(128)S(1)} %pad.2.clone, pred[]{:T(512)S(6)} %eq.11), kind=kLoop, calls=%fused_computation.1 | loop fusion | flops 294912 | bytes 778433 | tf_op jit(solution)/shard_map/jit(_where)/select_n | solution.py:126
  5.3 2.8 %copy.12 = f32[8,16,8,256]{3,0,1,2:T(8,128)} copy(f32[8,16,8,256]{3,2,1,0:T(8,128)} %param.6) | data formatting | bytes 2097152 | tf_op args[0]
  8.1 60.2 %shard_map.64 = (f32[48,8,256]{2,1,0:T(8,128)}, f32[6,16,8,256]{3,2,1,0:T(8,128)}, f32[6,16,8,256]{3,2,1,0:T(8,128)}, f32[32,6,256]{2,1,0:T(8,128)}, f32[32,6,256]{2,1,0:T(8,128)}) custom-call(f32[48,8,256]{2,1,0:T(8,128)} %maximum_select_fusion.masked, f32[8,16,8,256]{3,2,1,0:T(8,128)} %bitcast.10), custom_call_target="tpu_custom_call" | custom-call | tf_op jit(solution)/shard_map/pallas_call | solution.py:131
  68.4 17.6 %shard_map.65 = f32[8,16,8,256]{3,2,1,0:T(8,128)} custom-call(s32[16]{0:T(128)} %substeps.1, f32[8,16,8,256]{3,2,1,0:T(8,128)} %bitcast.11, f32[6,16,8,256]{3,2,1,0:T(8,128)} %get-tuple-element.10.south, f32[6,16,8,256]{3,2,1,0:T(8,128)} %get-tuple-element.11.north, f32[48,8,256]{2,1,0:T(8,128)} %get-tuple-element.12.chosen, ...), custom_call_target="tpu_custom_call" | custom-call | flops 35782656 | bytes 4063232 | tf_op jit(solution)/shard_map/pallas_call | solution.py:262
  86.0 2.8 %copy.9 = f32[8,16,8,256]{3,2,1,0:T(8,128)} copy(f32[8,16,8,256]{3,0,1,2:T(8,128)} %bitcast.12) | data formatting | bytes 2097152 | tf_op jit(solution)/shard_map/transpose | solution.py:304
Async XLA Ops:
  0.0 3.5 %copy-start = (f32[1,15,8,256]{3,2,1,0:T(8,128)S(1)}, f32[1,15,8,256]{3,2,1,0:T(8,128)}, u32[]{:S(2)}) copy-start(f32[1,15,8,256]{3,2,1,0:T(8,128)} %param.9) | copy-start | bytes 368644

commit v14 on v12

--- a/solution.py
+++ b/solution.py
@@ -243,13 +243,14 @@
                     held[lev, row] + lowers[lev, row] * previous_value
                 ) * pivots[lev, row]
                 held[lev, row] = previous_value
-            current = held[levels - 1, row]
-            out[row, levels - 1] = current
-            for lev in range(levels - 2, -1, -1):
-                current = held[lev, row] + ratios[lev, row] * current
-                out[row, lev] = current
 
     _finish()
+
+    current = [held[levels - 1, row] for row in range(height)]
+    out[:, levels - 1] = jnp.swapaxes(jnp.stack(current), 0, 1)
+    for lev in range(levels - 2, -1, -1):
+        current = [held[lev, row] + ratios[lev, row] * current[row] for row in range(height)]
+        out[:, lev] = jnp.swapaxes(jnp.stack(current), 0, 1)
 
 
 def transport(substeps, own, south, north, chosen, south_courant, north_courant,
@@ -259,7 +260,7 @@
     table = pltpu.VMEM((levels, height, tracer_count, width), jnp.float32)
     return pl.pallas_call(
         transport_kernel,
-        out_shape=jax.ShapeDtypeStruct(own.shape, jnp.float32),
+        out_shape=jax.ShapeDtypeStruct((tracer_count, levels, height, width), jnp.float32),
         in_specs=[pl.BlockSpec(memory_space=pltpu.SMEM)] + [vmem] * 7,
         out_specs=vmem,
         scratch_shapes=[
@@ -299,7 +300,7 @@
         substeps, by_row, south_rows, north_rows, chosen, south_courant,
         north_courant, jnp.transpose(emissions, (1, 0, 2)),
     )
-    return jnp.transpose(mixed, (2, 1, 0, 3))
+    return mixed
 
 
 def solution(mesh):

time: 88.2 us -> 85.2 us (0.966)
  local copies, waits for them, and re-layouts: 7.48 us -> 4.67 us
    transpose x1 -> x0, local copies, waits for them, and re-layouts: 2.8 us -> none  [shards(): return jnp.transpose(mixed, (2, 1, 0, 3))]
where the time goes in v14:
time: 85.2 us; the launch traced here: 84.8 us
  Pallas kernels  78.1 us (92%)
  local copies, waits for them, and re-layouts  4.67 us (5%)
  other arithmetic  1.46 us (2%)
    pallas_call x1, Pallas kernels, exchange(): pl.pallas_call(exchange_kernel, out_shape=(jax.ShapeDtypeStruct(padded.sh...  60.4 us
    pallas_call x1, Pallas kernels, transport(): pl.pallas_call(transport_kernel, out_shape=jax.ShapeDtypeStruct((tracer_c...  17.7 us
    unnamed x12, local copies, waits for them, and re-layouts  3.26 us

profile of v14, /device:TPU:161, one launch (start us, length us, event | category | flops | bytes accessed | tf_op | source)
XLA Modules:
  0.0 84.8 jit_solution(8830927516888923732)
XLA Ops:
  0.0 1.8 %copy.11 = f32[8,16,8,256]{3,0,1,2:T(8,128)S(1)} copy(f32[8,16,8,256]{3,2,1,0:T(8,128)} %param.6) | data formatting | bytes 2097152 | tf_op args[0]
  1.8 0.0 copy-start
  1.8 0.0 copy-start.1
  1.9 0.0 copy-start.2
  1.9 1.3 %fusion.1 = (f32[6,16,8,256]{3,2,1,0:T(8,128)}, f32[6,16,8,256]{3,2,1,0:T(8,128)}) fusion(f32[8,16,8,256]{3,2,1,0:T(8,128)S(1)} %bitcast.9), kind=kLoop, calls=%fused_computation.5 | loop fusion | bytes 3145728 | tf_op jit(solution)/shard_map/slice | solution.py:141
  3.2 0.1 copy-done
  3.3 0.0 copy-start.4
  3.3 0.7 copy-done.4
  4.0 0.6 fusion
  5.1 0.1 pad.2.clone
  5.2 0.0 copy-done.1
  5.2 0.0 copy-done.2
  5.2 0.9 %maximum_select_fusion.masked = f32[48,8,256]{2,1,0:T(8,128)} fusion(f32[15,8,256]{2,1,0:T(8,128)S(1)} %bitcast.13, f32[32,8,256]{2,1,0:T(8,128)S(1)} %bitcast.12, f32[48]{0:T(128)S(1)} %pad.2.clone, pred[]{:T(512)S(6)} %eq.11), kind=kLoop, calls=%fused_computation.1 | loop fusion | flops 294912 | bytes 778433 | tf_op jit(solution)/shard_map/jit(_where)/select_n | solution.py:124
  6.1 0.0 copy-start.3
  6.1 60.4 %shard_map.64 = (f32[48,8,256]{2,1,0:T(8,128)}, f32[6,16,8,256]{3,2,1,0:T(8,128)}, f32[6,16,8,256]{3,2,1,0:T(8,128)}, f32[32,6,256]{2,1,0:T(8,128)}, f32[32,6,256]{2,1,0:T(8,128)}) custom-call(f32[48,8,256]{2,1,0:T(8,128)} %maximum_select_fusion.masked, f32[6,16,8,256]{3,2,1,0:T(8,128)} %get-tuple-element.16.up, f32[6,16,8,256]{3,2,1,0:T(8,128)} %get-tuple-element.15.down), custom_call_target="tpu_custom_call" | custom-call | tf_op jit(solution)/shard_map/pallas_call | solution.py:129
  66.5 0.0 copy-done.3
  66.5 0.6 copy.12
  67.1 17.7 %shard_map.65 = f32[8,16,8,256]{3,2,1,0:T(8,128)} custom-call(s32[16]{0:T(128)} %substeps.1, f32[8,16,8,256]{3,2,1,0:T(8,128)} %bitcast.10, f32[6,16,8,256]{3,2,1,0:T(8,128)} %get-tuple-element.10.south, f32[6,16,8,256]{3,2,1,0:T(8,128)} %get-tuple-element.11.north, f32[48,8,256]{2,1,0:T(8,128)} %get-tuple-element.12.chosen, ...), custom_call_target="tpu_custom_call" | custom-call | flops 35782656 | bytes 4063232 | tf_op jit(solution)/shard_map/pallas_call | solution.py:261
Async XLA Ops:
  1.8 1.5 %copy-start = (f32[8,16,8,256]{3,0,1,2:T(8,128)}, f32[8,16,8,256]{3,0,1,2:T(8,128)S(1)}, u32[]{:S(2)}) copy-start(f32[8,16,8,256]{3,0,1,2:T(8,128)S(1)} %copy.11) | copy-start | bytes 3145732
  1.8 3.4 %copy-start.1 = (f32[1,2,16,8,256]{4,3,2,1,0:T(8,128)S(1)}, f32[1,2,16,8,256]{4,3,2,1,0:T(8,128)}, u32[]{:S(2)}) copy-start(f32[1,2,16,8,256]{4,3,2,1,0:T(8,128)} %param.8) | copy-start | bytes 786436
  1.9 3.3 %copy-start.2 = (f32[1,15,8,256]{3,2,1,0:T(8,128)S(1)}, f32[1,15,8,256]{3,2,1,0:T(8,128)}, u32[]{:S(2)}) copy-start(f32[1,15,8,256]{3,2,1,0:T(8,128)} %param.9) | copy-start | bytes 368644
  3.3 0.7 copy-start.4
  6.1 60.4 %copy-start.3 = (f32[8,8,256]{2,1,0:T(8,128)S(1)}, f32[8,8,256]{2,1,0:T(8,128)}, u32[]{:S(2)}) copy-start(f32[8,8,256]{2,1,0:T(8,128)} %param.7) | copy-start | bytes 196612

commit v15 on v14

--- a/solution.py
+++ b/solution.py
@@ -15,7 +15,7 @@
 
 
 def exchange_kernel(
-    masked, up, down, chosen, south, north, south_courant, north_courant,
+    masked, tracers, chosen, by_row, south, north, south_courant, north_courant,
     total, received, send_sems, recv_sems,
 ):
     mesh = pl.DeviceIdType.MESH
@@ -28,6 +28,8 @@
     planes = south_courant.shape[0]
     halo = south_courant.shape[1]
     rows_from = chosen.shape[1] - halo
+    up = by_row.at[pl.ds(by_row.shape[0] - halo, halo)]
+    down = by_row.at[pl.ds(0, halo)]
 
     def partner(bit):
         return me + (1 << bit) * (1 - 2 * ((me // (1 << bit)) % 2))
@@ -71,12 +73,15 @@
             device_id_type=mesh,
         )
         copy.start()
-        copy.wait()
-
-    along_group(masked.at[pl.ds((1 - core) * half, half)], 0, 0)
+        return copy
+
+    first = along_group(masked.at[pl.ds((1 - core) * half, half)], 0, 0)
+    for level in range(tracers.shape[1]):
+        by_row[:, level] = jnp.swapaxes(tracers[:, level], 0, 1)
+    first.wait()
     total[...] = masked[pl.ds(core * half, half)] + received[0]
     for bit in range(1, bits):
-        along_group(total, bit, bit)
+        along_group(total, bit, bit).wait()
         total[...] = total[...] + received[bit]
         if bit == 1:
             @pl.when(tile < tiles - 1)
@@ -86,7 +91,7 @@
             @pl.when(tile > 0)
             def _():
                 along_tile(down, north, 1, -1).start()
-    along_group(total, 0, bits)
+    along_group(total, 0, bits).wait()
     chosen[pl.ds(core * half, half)] = total[...]
     chosen[pl.ds((1 - core) * half, half)] = received[bits]
 
@@ -113,7 +118,7 @@
         along_tile(chosen.at[pl.ds(0, planes), pl.ds(rows_from, halo)], south_courant, 2 + bits + 1, -1).wait_recv()
 
 
-def exchange(value, by_row, root, halo, planes):
+def exchange(value, tracers, root, halo, planes):
     groups = lax.axis_size("group")
     assert groups & (groups - 1) == 0 and groups >= 2
     bits = groups.bit_length() - 1
@@ -122,15 +127,16 @@
         [value, jnp.zeros((2 * half - value.shape[0],) + value.shape[1:], value.dtype)]
     )
     masked = jnp.where(lax.axis_index("group") == root, padded, jnp.zeros_like(padded))
-    height = by_row.shape[0]
+    tracer_count, levels, height, width = tracers.shape
     vmem = pl.BlockSpec(memory_space=pltpu.VMEM)
-    rows = jax.ShapeDtypeStruct((halo,) + by_row.shape[1:], by_row.dtype)
+    by_row = jax.ShapeDtypeStruct((height, levels, tracer_count, width), tracers.dtype)
+    rows = jax.ShapeDtypeStruct((halo, levels, tracer_count, width), tracers.dtype)
     winds = jax.ShapeDtypeStruct((planes, halo) + value.shape[2:], value.dtype)
     return pl.pallas_call(
         exchange_kernel,
-        out_shape=(jax.ShapeDtypeStruct(padded.shape, padded.dtype), rows, rows, winds, winds),
-        in_specs=[vmem] * 3,
-        out_specs=(vmem,) * 5,
+        out_shape=(jax.ShapeDtypeStruct(padded.shape, padded.dtype), by_row, rows, rows, winds, winds),
+        in_specs=[vmem] * 2,
+        out_specs=(vmem,) * 6,
         scratch_shapes=[
             pltpu.VMEM((half,) + value.shape[1:], value.dtype),
             pltpu.VMEM((bits + 1, half) + value.shape[1:], value.dtype),
@@ -138,7 +144,7 @@
             pltpu.SemaphoreType.DMA((bits + 5,)),
         ],
         compiler_params=pltpu.CompilerParams(collective_id=0, has_side_effects=True),
-    )(masked, by_row[height - halo :], by_row[:halo])
+    )(masked, tracers)
 
 
 def transport_kernel(
@@ -235,8 +241,9 @@
     lax.fori_loop(0, levels, advect, 0)
 
     def _finish():
+        sources = jnp.swapaxes(emissions[...], 0, 1)
         for row in range(height):
-            held[0, row] = held[0, row] + emissions[row]
+            held[0, row] = held[0, row] + sources[row]
             previous_value = jnp.zeros(lane_shape, jnp.float32)
             for lev in range(levels):
                 previous_value = (
@@ -292,13 +299,12 @@
     local = jnp.concatenate(
         [winds[0].reshape(2 * levels, height, width), diffusivity[0]], axis=0
     )
-    by_row = jnp.transpose(tracers, (2, 1, 0, 3))
-    chosen, south_rows, north_rows, south_courant, north_courant = exchange(
-        local, by_row, loader_slot, halo, 2 * levels
+    chosen, by_row, south_rows, north_rows, south_courant, north_courant = exchange(
+        local, tracers, loader_slot, halo, 2 * levels
     )
     mixed = transport(
         substeps, by_row, south_rows, north_rows, chosen, south_courant,
-        north_courant, jnp.transpose(emissions, (1, 0, 2)),
+        north_courant, emissions,
     )
     return mixed
 

time: 85.2 us -> 82.5 us (0.968)
  local copies, waits for them, and re-layouts: 4.67 us -> 0.73 us
  other arithmetic: 1.46 us -> 2.51 us
    unnamed x12 -> x2, local copies, waits for them, and re-layouts: 3.26 us -> 0.65 us
    slice x1 -> x0, local copies, waits for them, and re-layouts: 1.33 us -> none  [exchange(): by_row[:halo]]
    select_n x1, other arithmetic: 0.86 us -> 1.88 us  [exchange(): jnp.where(lax.axis_index('group') == root, padded, jnp.zeros_like(padded))]
where the time goes in v15:
time: 82.5 us; the launch traced here: 82.1 us
  Pallas kernels  78.2 us (95%)
  other arithmetic  2.51 us (3%)
    pallas_call x1, Pallas kernels, exchange(): pl.pallas_call(exchange_kernel, out_shape=(jax.ShapeDtypeStruct(padded.sh...  60.5 us
    pallas_call x1, Pallas kernels, transport(): pl.pallas_call(transport_kernel, out_shape=jax.ShapeDtypeStruct((tracer_c...  17.7 us
    select_n x1, other arithmetic, exchange(): jnp.where(lax.axis_index('group') == root, padded, jnp.zeros_like(padded))  1.88 us

profile of v15, /device:TPU:161, one launch (start us, length us, event | category | flops | bytes accessed | tf_op | source)
XLA Modules:
  0.0 82.1 jit_solution(5568202396258268149)
XLA Ops:
  0.0 0.0 copy-start
  0.0 0.7 copy-done
  0.7 0.6 fusion
  1.9 0.1 pad.2.clone
  2.0 1.9 %maximum_select_fusion.masked = f32[48,8,256]{2,1,0:T(8,128)} fusion(f32[15,8,256]{2,1,0:T(8,128)} %bitcast.4, f32[32,8,256]{2,1,0:T(8,128)} %bitcast.3, f32[48]{0:T(128)S(1)} %pad.2.clone, pred[]{:T(512)S(6)} %eq.11), kind=kLoop, calls=%fused_computation | loop fusion | flops 294912 | bytes 778433 | tf_op jit(solution)/shard_map/jit(_where)/select_n | solution.py:129
  3.9 60.5 %shard_map.64 = (f32[48,8,256]{2,1,0:T(8,128)}, f32[8,16,8,256]{3,2,1,0:T(8,128)}, f32[6,16,8,256]{3,2,1,0:T(8,128)}, f32[6,16,8,256]{3,2,1,0:T(8,128)}, f32[32,6,256]{2,1,0:T(8,128)}, /*index=5*/f32[32,6,256]{2,1,0:T(8,128)}) custom-call(f32[48,8,256]{2,1,0:T(8,128)} %maximum_select_fusion.masked, f32[8,16,8,256]{3,2,1,0:T(8,128)} %tracers.1), custom_call_target="tpu_custom_call" | custom-call | tf_op jit(solution)/shard_map/pallas_call | solution.py:135
  64.4 17.7 %shard_map.65 = f32[8,16,8,256]{3,2,1,0:T(8,128)} custom-call(s32[16]{0:T(128)} %substeps.1, f32[8,16,8,256]{3,2,1,0:T(8,128)} %get-tuple-element.11.own, f32[6,16,8,256]{3,2,1,0:T(8,128)} %get-tuple-element.12.south, f32[6,16,8,256]{3,2,1,0:T(8,128)} %get-tuple-element.13.north, f32[48,8,256]{2,1,0:T(8,128)} %get-tuple-element.14.chosen, ...), custom_call_target="tpu_custom_call" | custom-call | flops 35782656 | bytes 4063232 | tf_op jit(solution)/shard_map/pallas_call | solution.py:268
Async XLA Ops:
  0.0 0.7 copy-start

commit v16 on v15

--- a/solution.py
+++ b/solution.py
@@ -15,8 +15,8 @@
 
 
 def exchange_kernel(
-    masked, tracers, chosen, by_row, south, north, south_courant, north_courant,
-    total, received, send_sems, recv_sems,
+    scale, courant_in, coefficient_in, tracers, chosen, by_row, south, north,
+    south_courant, north_courant, masked, total, received, send_sems, recv_sems,
 ):
     mesh = pl.DeviceIdType.MESH
     tiles = lax.axis_size("tile")
@@ -25,6 +25,13 @@
     me = lax.axis_index("group")
     core = me % 2
     half = masked.shape[0] // 2
+    weight = scale[0]
+    count = courant_in.shape[0]
+    masked[pl.ds(0, count)] = courant_in[...] * weight
+    masked[pl.ds(count, coefficient_in.shape[0])] = coefficient_in[...] * weight
+    masked[pl.ds(count + coefficient_in.shape[0], masked.shape[0] - count - coefficient_in.shape[0])] = jnp.zeros(
+        (masked.shape[0] - count - coefficient_in.shape[0],) + masked.shape[1:], jnp.float32
+    )
     planes = south_courant.shape[0]
     halo = south_courant.shape[1]
     rows_from = chosen.shape[1] - halo
@@ -118,33 +125,35 @@
         along_tile(chosen.at[pl.ds(0, planes), pl.ds(rows_from, halo)], south_courant, 2 + bits + 1, -1).wait_recv()
 
 
-def exchange(value, tracers, root, halo, planes):
+def exchange(courant, coefficient, tracers, root, halo):
     groups = lax.axis_size("group")
     assert groups & (groups - 1) == 0 and groups >= 2
     bits = groups.bit_length() - 1
-    half = -(-value.shape[0] // 2)
-    padded = jnp.concatenate(
-        [value, jnp.zeros((2 * half - value.shape[0],) + value.shape[1:], value.dtype)]
-    )
-    masked = jnp.where(lax.axis_index("group") == root, padded, jnp.zeros_like(padded))
+    planes = courant.shape[0]
+    half = -(-(planes + coefficient.shape[0]) // 2)
+    scale = jnp.where(lax.axis_index("group") == root, jnp.float32(1.0), jnp.float32(0.0))
     tracer_count, levels, height, width = tracers.shape
     vmem = pl.BlockSpec(memory_space=pltpu.VMEM)
     by_row = jax.ShapeDtypeStruct((height, levels, tracer_count, width), tracers.dtype)
     rows = jax.ShapeDtypeStruct((halo, levels, tracer_count, width), tracers.dtype)
-    winds = jax.ShapeDtypeStruct((planes, halo) + value.shape[2:], value.dtype)
+    winds = jax.ShapeDtypeStruct((planes, halo, width), courant.dtype)
     return pl.pallas_call(
         exchange_kernel,
-        out_shape=(jax.ShapeDtypeStruct(padded.shape, padded.dtype), by_row, rows, rows, winds, winds),
-        in_specs=[vmem] * 2,
+        out_shape=(
+            jax.ShapeDtypeStruct((2 * half,) + courant.shape[1:], courant.dtype),
+            by_row, rows, rows, winds, winds,
+        ),
+        in_specs=[pl.BlockSpec(memory_space=pltpu.SMEM)] + [vmem] * 3,
         out_specs=(vmem,) * 6,
         scratch_shapes=[
-            pltpu.VMEM((half,) + value.shape[1:], value.dtype),
-            pltpu.VMEM((bits + 1, half) + value.shape[1:], value.dtype),
+            pltpu.VMEM((2 * half,) + courant.shape[1:], courant.dtype),
+            pltpu.VMEM((half,) + courant.shape[1:], courant.dtype),
+            pltpu.VMEM((bits + 1, half) + courant.shape[1:], courant.dtype),
             pltpu.SemaphoreType.DMA((bits + 5,)),
             pltpu.SemaphoreType.DMA((bits + 5,)),
         ],
         compiler_params=pltpu.CompilerParams(collective_id=0, has_side_effects=True),
-    )(masked, tracers)
+    )(scale[None], courant, coefficient, tracers)
 
 
 def transport_kernel(
@@ -296,11 +305,8 @@
     width = tracers.shape[3]
     halo = ROUNDS
 
-    local = jnp.concatenate(
-        [winds[0].reshape(2 * levels, height, width), diffusivity[0]], axis=0
-    )
     chosen, by_row, south_rows, north_rows, south_courant, north_courant = exchange(
-        local, tracers, loader_slot, halo, 2 * levels
+        winds[0].reshape(2 * levels, height, width), diffusivity[0], tracers, loader_slot, halo
     )
     mixed = transport(
         substeps, by_row, south_rows, north_rows, chosen, south_courant,

time: 82.5 us -> 80.8 us (0.979)
  other arithmetic: 2.51 us -> 0.63 us
    select_n x1 -> x0, other arithmetic: 1.88 us -> none  [exchange(): jnp.where(lax.axis_index('group') == root, padded, jnp.zeros_like(padded))]
where the time goes in v16:
time: 80.8 us; the launch traced here: 80.4 us
  Pallas kernels  78.4 us (97%)
    pallas_call x1, Pallas kernels, exchange(): pl.pallas_call(exchange_kernel, out_shape=(jax.ShapeDtypeStruct((2 * half...  60.8 us
    pallas_call x1, Pallas kernels, transport(): pl.pallas_call(transport_kernel, out_shape=jax.ShapeDtypeStruct((tracer_c...  17.7 us

profile of v16, /device:TPU:161, one launch (start us, length us, event | category | flops | bytes accessed | tf_op | source)
XLA Modules:
  0.0 80.4 jit_solution(4598450795399970648)
XLA Ops:
  0.0 0.0 copy-start
  0.0 0.7 copy-done
  0.7 0.6 fusion
  1.9 60.8 %shard_map.64 = (f32[48,8,256]{2,1,0:T(8,128)}, f32[8,16,8,256]{3,2,1,0:T(8,128)}, f32[6,16,8,256]{3,2,1,0:T(8,128)}, f32[6,16,8,256]{3,2,1,0:T(8,128)}, f32[32,6,256]{2,1,0:T(8,128)}, /*index=5*/f32[32,6,256]{2,1,0:T(8,128)}) custom-call(f32[1]{0:T(128)} %bitcast.scale, f32[32,8,256]{2,1,0:T(8,128)} %bitcast.3, f32[15,8,256]{2,1,0:T(8,128)} %bitcast.4, ...), custom_call_target="tpu_custom_call" | custom-call | tf_op jit(solution)/shard_map/pallas_call | solution.py:140
  62.7 17.7 %shard_map.65 = f32[8,16,8,256]{3,2,1,0:T(8,128)} custom-call(s32[16]{0:T(128)} %substeps.1, f32[8,16,8,256]{3,2,1,0:T(8,128)} %get-tuple-element.11.own, f32[6,16,8,256]{3,2,1,0:T(8,128)} %get-tuple-element.12.south, f32[6,16,8,256]{3,2,1,0:T(8,128)} %get-tuple-element.13.north, f32[48,8,256]{2,1,0:T(8,128)} %get-tuple-element.14.chosen, ...), custom_call_target="tpu_custom_call" | custom-call | flops 35782656 | bytes 4063232 | tf_op jit(solution)/shard_map/pallas_call | solution.py:277
Async XLA Ops:
  0.0 0.7 copy-start

commit v17 on v16

--- a/solution.py
+++ b/solution.py
@@ -82,13 +82,22 @@
         copy.start()
         return copy
 
+    levels = tracers.shape[1]
+    split = levels // 2
+
+    def swap_levels(low, high):
+        for level in range(low, high):
+            by_row[:, level] = jnp.swapaxes(tracers[:, level], 0, 1)
+
     first = along_group(masked.at[pl.ds((1 - core) * half, half)], 0, 0)
-    for level in range(tracers.shape[1]):
-        by_row[:, level] = jnp.swapaxes(tracers[:, level], 0, 1)
+    swap_levels(0, split)
     first.wait()
     total[...] = masked[pl.ds(core * half, half)] + received[0]
     for bit in range(1, bits):
-        along_group(total, bit, bit).wait()
+        copy = along_group(total, bit, bit)
+        if bit == 1:
+            swap_levels(split, levels)
+        copy.wait()
         total[...] = total[...] + received[bit]
         if bit == 1:
             @pl.when(tile < tiles - 1)

time: 80.8 us -> 80.8 us (level)
  no operation moved by 1% of the time
where the time goes in v17:
time: 80.8 us; the launch traced here: 80.4 us
  Pallas kernels  78.4 us (97%)
    pallas_call x1, Pallas kernels, exchange(): pl.pallas_call(exchange_kernel, out_shape=(jax.ShapeDtypeStruct((2 * half...  60.8 us
    pallas_call x1, Pallas kernels, transport(): pl.pallas_call(transport_kernel, out_shape=jax.ShapeDtypeStruct((tracer_c...  17.7 us

profile of v17, /device:TPU:161, one launch (start us, length us, event | category | flops | bytes accessed | tf_op | source)
XLA Modules:
  0.0 80.4 jit_solution(13764464760625562170)
XLA Ops:
  0.0 0.0 copy-start
  0.0 0.7 copy-done
  0.7 0.6 fusion
  1.9 60.8 %shard_map.64 = (f32[48,8,256]{2,1,0:T(8,128)}, f32[8,16,8,256]{3,2,1,0:T(8,128)}, f32[6,16,8,256]{3,2,1,0:T(8,128)}, f32[6,16,8,256]{3,2,1,0:T(8,128)}, f32[32,6,256]{2,1,0:T(8,128)}, /*index=5*/f32[32,6,256]{2,1,0:T(8,128)}) custom-call(f32[1]{0:T(128)} %bitcast.scale, f32[32,8,256]{2,1,0:T(8,128)} %bitcast.3, f32[15,8,256]{2,1,0:T(8,128)} %bitcast.4, ...), custom_call_target="tpu_custom_call" | custom-call | tf_op jit(solution)/shard_map/pallas_call | solution.py:149
  62.7 17.7 %shard_map.65 = f32[8,16,8,256]{3,2,1,0:T(8,128)} custom-call(s32[16]{0:T(128)} %substeps.1, f32[8,16,8,256]{3,2,1,0:T(8,128)} %get-tuple-element.11.own, f32[6,16,8,256]{3,2,1,0:T(8,128)} %get-tuple-element.12.south, f32[6,16,8,256]{3,2,1,0:T(8,128)} %get-tuple-element.13.north, f32[48,8,256]{2,1,0:T(8,128)} %get-tuple-element.14.chosen, ...), custom_call_target="tpu_custom_call" | custom-call | flops 35782656 | bytes 4063232 | tf_op jit(solution)/shard_map/pallas_call | solution.py:286
Async XLA Ops:
  0.0 0.7 copy-start
